TPU v7x, 512 devices: a whole 4x8x8 slice. The times are simulated.
512 devices in a mesh: seq: 16 (over y_hi, z), head: 32 (over x, y_lo, core).
Axes of the slice: x: 4, y: 8 (y_hi: 2, y_lo: 4; y = y_hi * 4 + y_lo), z: 8, core: 2. Of those that a mesh axis runs over, the one named last changes fastest.
Arguments:
- tokens: bfloat16 [16384, 4096], P(('seq', 'head')), may hold values from -6 to 6
- doc_lengths: int32 [16], replicated, may hold values from 1 to 8704, as said below
- value_weight: bfloat16 [4096, 8192], P('seq', 'head'), may hold values from -0.09375 to 0.09375
- gate_weight: bfloat16 [4096, 8192], P('seq', 'head'), may hold values from -0.09375 to 0.09375
- state_weight: bfloat16 [8, 4096, 256], P(None, 'seq'), may hold values from -0.09375 to 0.09375
- step_weight: bfloat16 [4096, 128], P('seq', 'head'), may hold values from -0.09375 to 0.09375
- value_conv: float32 [4, 8192], P(None, 'head'), may hold values from -3 to 3
- state_conv: float32 [8, 4, 256], replicated, may hold values from -3 to 3
- step_bias: float32 [128], P('head'), may hold values from -5 to -3
- log_rate: float32 [128], P('head'), may hold values from -6 to 4
Outputs:
- layer_output: bfloat16 [16384, 8192], P('seq', 'head')
Inputs may be any that keep to these rules, and one draw needn't show every extreme that they name: `doc_lengths`: the 16 documents lie one after another, their lengths sum to 16384, and the last one holds 8704 positions.
All inputs are finite; a program needn't handle non-finite values.
Results may differ from a plain program's by a relative error of at most 0.015.
Values may be sent and summed in bfloat16 or wider, within the bound.
No kernel may reach another device: no remote copies, remote signals or barrier semaphores. Data moves between devices by JAX's collectives and lax.ppermute only.
A program may use at most 64 MiB of HBM per device.

v0:
```python
import jax
import jax.numpy as jnp
from jax import lax
from jax.sharding import PartitionSpec as P

HEADS = 128
GROUPS = 8
BLOCK = 256


def passed_along(value, axis, steps):
    count = lax.axis_size(axis)
    leading, last = (max(0, -steps), min(count, count - steps))
    return lax.ppermute(value, axis, [(source, source + steps) for source in range(leading, last)])


def segment_of(positions, starts):
    reached = (starts[None, :] <= positions[:, None]).astype(jnp.int32)
    return jnp.sum(reached, axis=1) - 1


def causal_conv(extended, taps_weight, seg_ext, row_count):
    tap_count = taps_weight.shape[0]
    own_segment = seg_ext[tap_count - 1 :]
    summed = jnp.zeros((row_count, extended.shape[1]), jnp.float32)
    for tap_index in range(tap_count):
        window = extended[tap_index : tap_index + row_count].astype(jnp.float32)
        keep_mask = (seg_ext[tap_index : tap_index + row_count] == own_segment).astype(jnp.float32)[
            :, None
        ]
        summed = summed + taps_weight[tap_index][None, :] * window * keep_mask
    return jax.nn.silu(summed).astype(jnp.bfloat16)


def block_terms(b_rows, c_rows, x_rows, decay_rows, step_rows, segments, seg_before):
    block_len = b_rows.shape[0]
    head_total = decay_rows.shape[0]
    x_heads = x_rows.reshape(block_len, head_total, -1)
    cumulative = jnp.cumsum(decay_rows, axis=1)
    products = jnp.dot(c_rows, b_rows.T, preferred_element_type=jnp.float32)
    local_index = jnp.arange(block_len)
    allowed = (local_index[None, :] <= local_index[:, None]) & (
        segments[None, :] == segments[:, None]
    )
    spread = cumulative[:, :, None] - cumulative[:, None, :]
    decay_mat = jnp.where(allowed[None], jnp.exp(jnp.where(allowed[None], spread, 0.0)), 0.0)
    scores = (products[None] * decay_mat * step_rows[:, None, :]).astype(jnp.bfloat16)
    y_inner = jnp.einsum("hij,jhp->ihp", scores, x_heads, preferred_element_type=jnp.float32)
    ending = cumulative[:, -1]
    trailing = (
        jnp.where((segments == segments[-1])[None, :], jnp.exp(ending[:, None] - cumulative), 0.0)
        * step_rows
    )
    weighted = (trailing.T[:, :, None] * x_heads.astype(jnp.float32)).astype(jnp.bfloat16)
    local_state = jnp.einsum("jn,jhp->hnp", b_rows, weighted, preferred_element_type=jnp.float32)
    factor = jnp.where(segments[-1] == seg_before, jnp.exp(ending), 0.0)
    entry_gain = jnp.where((segments == seg_before)[None, :], jnp.exp(cumulative), 0.0)
    return (y_inner.reshape(block_len, -1), local_state, factor, entry_gain)


def local_pass(state_cols, value_cols, decay_cols, step_cols, seg_rows, seg_before, block_len):
    block_count = state_cols.shape[0] // block_len
    state_dim = state_cols.shape[1] // 2
    head_total = decay_cols.shape[1]
    b_all = state_cols[:, :state_dim].reshape(block_count, block_len, state_dim)
    c_all = state_cols[:, state_dim:].reshape(block_count, block_len, state_dim)
    x_all = value_cols.reshape(block_count, block_len, -1)
    decay_all = decay_cols.reshape(block_count, block_len, head_total).transpose(0, 2, 1)
    step_all = step_cols.reshape(block_count, block_len, head_total).transpose(0, 2, 1)
    seg_all = seg_rows.reshape(block_count, block_len)

    def one_block(block_item):
        return block_terms(*block_item)

    outputs = lax.map(one_block, (b_all, c_all, x_all, decay_all, step_all, seg_all, seg_before))
    return (outputs, c_all)


def prefix_blocks(local_state, factor):

    def chain_step(carry_pair, block_item):
        running, running_gain = carry_pair
        local_term, factor_term = block_item
        return (
            (factor_term[:, None, None] * running + local_term, factor_term * running_gain),
            (running, running_gain),
        )

    initial = (
        jnp.zeros(local_state.shape[1:], jnp.float32),
        jnp.ones((factor.shape[1],), jnp.float32),
    )
    (shard_state, shard_gain), (inside, gain_list) = lax.scan(
        chain_step, initial, (local_state, factor)
    )
    return (shard_state, shard_gain, inside, gain_list)


def finish(y_inner, incoming, entry_gain, c_all, value_cols, gate_cols):
    block_count, block_len, _ = y_inner.shape
    head_total = incoming.shape[1]
    carried = jnp.einsum(
        "cin,chnp->cihp", c_all.astype(jnp.float32), incoming, precision=lax.Precision.HIGHEST
    )
    carried = carried * entry_gain.transpose(0, 2, 1)[:, :, :, None]
    x_heads = value_cols.reshape(block_count, block_len, head_total, -1).astype(jnp.float32)
    summed = y_inner.reshape(block_count, block_len, head_total, -1) + carried + x_heads
    gating = jax.nn.silu(gate_cols.astype(jnp.float32)).reshape(
        block_count, block_len, head_total, -1
    )
    return (summed * gating).reshape(block_count * block_len, -1).astype(jnp.bfloat16)


def local(
    tokens,
    doc_lengths,
    value_weight,
    gate_weight,
    state_weight,
    step_weight,
    value_conv,
    state_conv,
    step_bias,
    log_rate,
):
    tok_dev = tokens.shape[0] * lax.axis_size("head")
    heads_here = step_weight.shape[1]
    tap_count = value_conv.shape[0]
    group_index = lax.axis_index("head") * heads_here // (HEADS // GROUPS)
    state_own = lax.dynamic_index_in_dim(state_weight, group_index, 0, keepdims=False)
    conv_own = lax.dynamic_index_in_dim(state_conv, group_index, 0, keepdims=False)
    gathered = lax.all_gather(tokens, "head", axis=0, tiled=True)
    shard_pieces = (
        lax.all_gather(value_weight, "seq", axis=0, tiled=True),
        lax.all_gather(gate_weight, "seq", axis=0, tiled=True),
        lax.all_gather(state_own, "seq", axis=0, tiled=True),
        lax.all_gather(step_weight, "seq", axis=0, tiled=True),
    )
    projected = tuple(
        (
            jnp.dot(gathered, weight_piece, preferred_element_type=jnp.float32)
            for weight_piece in shard_pieces
        )
    )
    value_proj = projected[0].astype(jnp.bfloat16)
    gate_proj = projected[1].astype(jnp.bfloat16)
    state_proj = projected[2].astype(jnp.bfloat16)
    step_proj = projected[3].astype(jnp.bfloat16)
    value_cols = value_proj.shape[1]
    rim_source = jnp.concatenate(
        [value_proj[-(tap_count - 1) :], state_proj[-(tap_count - 1) :]], axis=1
    )
    rim_rows = passed_along(rim_source, "seq", 1)
    value_ext = jnp.concatenate([rim_rows[:, :value_cols], value_proj], axis=0)
    state_ext = jnp.concatenate([rim_rows[:, value_cols:], state_proj], axis=0)
    starts = jnp.cumsum(doc_lengths) - doc_lengths
    positions = lax.axis_index("seq") * tok_dev + jnp.arange(-(tap_count - 1), tok_dev)
    seg_ext = segment_of(positions, starts)
    value_act = causal_conv(value_ext, value_conv, seg_ext, tok_dev)
    state_act = causal_conv(state_ext, conv_own, seg_ext, tok_dev)
    step_size = jax.nn.softplus(step_proj.astype(jnp.float32) + step_bias[None, :])
    decay_rate = -jnp.exp(log_rate)[None, :] * step_size
    seg_rows = seg_ext[tap_count - 1 :]
    seg_before = seg_ext[tap_count - 2 : tap_count - 2 + tok_dev : BLOCK]
    (y_inner, local_state, factor, entry_gain), c_all = local_pass(
        state_act, value_act, decay_rate, step_size, seg_rows, seg_before, BLOCK
    )
    shard_state, shard_gain, inside, gain_list = prefix_blocks(local_state, factor)

    def relay(step_index, arriving):
        leaving = shard_gain[:, None, None] * arriving + shard_state
        return passed_along(leaving, "seq", 1)

    entering = lax.fori_loop(0, lax.axis_size("seq") - 1, relay, jnp.zeros_like(shard_state))
    incoming = inside + gain_list[:, :, None, None] * entering[None]
    return finish(y_inner, incoming, entry_gain, c_all, value_act, gate_proj)


def solution(mesh):
    return jax.shard_map(
        local,
        mesh=mesh,
        in_specs=(
            P(("seq", "head"), None),
            P(),
            P("seq", "head"),
            P("seq", "head"),
            P(None, "seq", None),
            P("seq", "head"),
            P(None, "head"),
            P(),
            P("head"),
            P("head"),
        ),
        out_specs=P("seq", "head"),
        check_vma=False,
    )
```

profile of v0, /device:TPU:48, one launch (start us, length us, event | category | flops | bytes accessed | tf_op | source)
XLA Modules:
  0.0 720.9 jit_solution(3404737921538199455)
XLA Ops:
  11.2 56.0 %all_gather.18 = bf16[4096,4]{0,1:T(4,128)(2,1)S(1)} all-gather(bf16[256,4]{0,1:T(4,128)(2,1)} %param.21), channel_id=1, replica_groups=mesh['seq'=16,'head'=32] {'seq'}, dimensions={0}, use_global_device_ids=true | all-gather | bytes 34816 | tf_op jit(solution)/shard_map/all_gather | solution.py:137
  69.7 48.0 %all-gather.8.cloned.1.call-done = bf16[4096,256]{1,0:T(8,128)(2,1)} async-done(((bf16[256,256]{1,0:T(8,128)(2,1)}), bf16[4096,256]{1,0:T(8,128)(2,1)}) %all-gather.8.cloned.1.call-update) | async-done | bytes 2097168 | tf_op jit(solution)/shard_map/all_gather | solution.py:134
  117.7 69.9 %all-gather.6.cloned.1.call-done = bf16[1024,4096]{1,0:T(8,128)(2,1)} async-done(((bf16[32,4096]{1,0:T(8,128)(2,1)}), bf16[1024,4096]{1,0:T(8,128)(2,1)}) %all-gather.6.cloned.1.call-update) | async-done | bytes 8388624 | tf_op jit(solution)/shard_map/all_gather | solution.py:132
  187.6 6.3 convolution_convert_fusion.1
  194.7 98.4 %all-gather.12.cloned.1.call-done = bf16[1,4096,256]{2,1,0:T(8,128)(2,1)} async-done(((bf16[1,256,256]{2,1,0:T(8,128)(2,1)}), bf16[1,4096,256]{2,1,0:T(8,128)(2,1)}) %all-gather.12.cloned.1.call-update) | async-done | bytes 2097168 | tf_op jit(solution)/shard_map/all_gather | solution.py:136
  303.3 92.2 %all-gather.10.cloned.1.call-done = bf16[4096,256]{1,0:T(8,128)(2,1)} async-done(((bf16[256,256]{1,0:T(8,128)(2,1)}), bf16[4096,256]{1,0:T(8,128)(2,1)}) %all-gather.10.cloned.1.call-update) | async-done | bytes 2097168 | tf_op jit(solution)/shard_map/all_gather | solution.py:135
  395.5 7.4 %convert_multiply_fusion = f32[1024,256]{1,0:T(8,128)} fusion(bf16[1024,4096]{1,0:T(8,128)(2,1)} %all-gather.6.cloned.1.call-done, bf16[4096,256]{1,0:T(8,128)(2,1)} %all-gather.10.cloned.1.call-done), kind=kOutput, calls=%fused_computation.49 | convolution fusion | flops 2149056512 | bytes 11534336 | tf_op jit(solution)/shard_map/dot_general | solution.py:141
  418.4 30.8 %while.43 = (s32[]{:T(128)}, f32[4,256,256]{1,2,0:T(8,128)}, f32[4,4,128,64]{2,3,1,0:T(8,128)S(1)}, f32[4,4]{1,0:T(4,128)S(1)}, f32[4,4,256]{2,1,0:T(4,128)S(1)}...) while((s32[]{:T(128)}, f32[4,256,256]{1,2,0:T(8,128)}, ...), condition=%wide.region_5.6_spmd, body=%wide.region_2.5_spmd.sunk | while | flops 69210640 | bytes 2915319 | solution.py:75
  454.1 247.6 %while.44 = (s32[]{:T(128)}, f32[4,128,64]{2,1,0:T(8,128)S(1)}, f32[4]{0:T(128)S(1)}, f32[4,128,64]{2,1,0:T(8,128)S(1)}, s32[]{:T(128)}) while((s32[]{:T(128)}, f32[4,128,64]{2,1,0:T(8,128)S(1)}, f32[4]{0:T(128)S(1)}, f32[4,128,64]{2,1,0:T(8,128)S(1)}, s32[]{:T(128)}) %tuple.85), condition=%wide.region_9.10_spmd, body=%wide.region_8.9_spmd.sunk | while | flops 65538 | bytes 917621 | solution.py:174
  457.2 12.6 %collective-permute-done = f32[4,128,64]{2,1,0:T(8,128)S(1)} collective-permute-done((f32[4,128,64]{2,1,0:T(8,128)S(1)}, f32[4,128,64]{2,1,0:T(8,128)S(1)}, u32[]{:S(2)}, u32[]{:S(2)}) %collective-permute-start) | collective-permute-done | bytes 131104 | tf_op jit(solution)/shard_map/while/body/eval_jaxpr/ppermute | solution.py:14
  471.8 15.3 %collective-permute-done = f32[4,128,64]{2,1,0:T(8,128)S(1)} collective-permute-done((f32[4,128,64]{2,1,0:T(8,128)S(1)}, f32[4,128,64]{2,1,0:T(8,128)S(1)}, u32[]{:S(2)}, u32[]{:S(2)}) %collective-permute-start) | collective-permute-done | bytes 131104 | tf_op jit(solution)/shard_map/while/body/eval_jaxpr/ppermute | solution.py:14
  489.1 15.1 %collective-permute-done = f32[4,128,64]{2,1,0:T(8,128)S(1)} collective-permute-done((f32[4,128,64]{2,1,0:T(8,128)S(1)}, f32[4,128,64]{2,1,0:T(8,128)S(1)}, u32[]{:S(2)}, u32[]{:S(2)}) %collective-permute-start) | collective-permute-done | bytes 131104 | tf_op jit(solution)/shard_map/while/body/eval_jaxpr/ppermute | solution.py:14
  506.2 15.1 %collective-permute-done = f32[4,128,64]{2,1,0:T(8,128)S(1)} collective-permute-done((f32[4,128,64]{2,1,0:T(8,128)S(1)}, f32[4,128,64]{2,1,0:T(8,128)S(1)}, u32[]{:S(2)}, u32[]{:S(2)}) %collective-permute-start) | collective-permute-done | bytes 131104 | tf_op jit(solution)/shard_map/while/body/eval_jaxpr/ppermute | solution.py:14
  523.3 19.9 %collective-permute-done = f32[4,128,64]{2,1,0:T(8,128)S(1)} collective-permute-done((f32[4,128,64]{2,1,0:T(8,128)S(1)}, f32[4,128,64]{2,1,0:T(8,128)S(1)}, u32[]{:S(2)}, u32[]{:S(2)}) %collective-permute-start) | collective-permute-done | bytes 131104 | tf_op jit(solution)/shard_map/while/body/eval_jaxpr/ppermute | solution.py:14
  545.2 17.7 %collective-permute-done = f32[4,128,64]{2,1,0:T(8,128)S(1)} collective-permute-done((f32[4,128,64]{2,1,0:T(8,128)S(1)}, f32[4,128,64]{2,1,0:T(8,128)S(1)}, u32[]{:S(2)}, u32[]{:S(2)}) %collective-permute-start) | collective-permute-done | bytes 131104 | tf_op jit(solution)/shard_map/while/body/eval_jaxpr/ppermute | solution.py:14
  564.9 15.2 %collective-permute-done = f32[4,128,64]{2,1,0:T(8,128)S(1)} collective-permute-done((f32[4,128,64]{2,1,0:T(8,128)S(1)}, f32[4,128,64]{2,1,0:T(8,128)S(1)}, u32[]{:S(2)}, u32[]{:S(2)}) %collective-permute-start) | collective-permute-done | bytes 131104 | tf_op jit(solution)/shard_map/while/body/eval_jaxpr/ppermute | solution.py:14
  582.1 14.3 %collective-permute-done = f32[4,128,64]{2,1,0:T(8,128)S(1)} collective-permute-done((f32[4,128,64]{2,1,0:T(8,128)S(1)}, f32[4,128,64]{2,1,0:T(8,128)S(1)}, u32[]{:S(2)}, u32[]{:S(2)}) %collective-permute-start) | collective-permute-done | bytes 131104 | tf_op jit(solution)/shard_map/while/body/eval_jaxpr/ppermute | solution.py:14
  598.4 16.3 %collective-permute-done = f32[4,128,64]{2,1,0:T(8,128)S(1)} collective-permute-done((f32[4,128,64]{2,1,0:T(8,128)S(1)}, f32[4,128,64]{2,1,0:T(8,128)S(1)}, u32[]{:S(2)}, u32[]{:S(2)}) %collective-permute-start) | collective-permute-done | bytes 131104 | tf_op jit(solution)/shard_map/while/body/eval_jaxpr/ppermute | solution.py:14
  616.8 13.1 %collective-permute-done = f32[4,128,64]{2,1,0:T(8,128)S(1)} collective-permute-done((f32[4,128,64]{2,1,0:T(8,128)S(1)}, f32[4,128,64]{2,1,0:T(8,128)S(1)}, u32[]{:S(2)}, u32[]{:S(2)}) %collective-permute-start) | collective-permute-done | bytes 131104 | tf_op jit(solution)/shard_map/while/body/eval_jaxpr/ppermute | solution.py:14
  631.9 12.4 %collective-permute-done = f32[4,128,64]{2,1,0:T(8,128)S(1)} collective-permute-done((f32[4,128,64]{2,1,0:T(8,128)S(1)}, f32[4,128,64]{2,1,0:T(8,128)S(1)}, u32[]{:S(2)}, u32[]{:S(2)}) %collective-permute-start) | collective-permute-done | bytes 131104 | tf_op jit(solution)/shard_map/while/body/eval_jaxpr/ppermute | solution.py:14
  646.3 12.4 %collective-permute-done = f32[4,128,64]{2,1,0:T(8,128)S(1)} collective-permute-done((f32[4,128,64]{2,1,0:T(8,128)S(1)}, f32[4,128,64]{2,1,0:T(8,128)S(1)}, u32[]{:S(2)}, u32[]{:S(2)}) %collective-permute-start) | collective-permute-done | bytes 131104 | tf_op jit(solution)/shard_map/while/body/eval_jaxpr/ppermute | solution.py:14
  660.6 12.4 %collective-permute-done = f32[4,128,64]{2,1,0:T(8,128)S(1)} collective-permute-done((f32[4,128,64]{2,1,0:T(8,128)S(1)}, f32[4,128,64]{2,1,0:T(8,128)S(1)}, u32[]{:S(2)}, u32[]{:S(2)}) %collective-permute-start) | collective-permute-done | bytes 131104 | tf_op jit(solution)/shard_map/while/body/eval_jaxpr/ppermute | solution.py:14
  675.0 12.4 %collective-permute-done = f32[4,128,64]{2,1,0:T(8,128)S(1)} collective-permute-done((f32[4,128,64]{2,1,0:T(8,128)S(1)}, f32[4,128,64]{2,1,0:T(8,128)S(1)}, u32[]{:S(2)}, u32[]{:S(2)}) %collective-permute-start) | collective-permute-done | bytes 131104 | tf_op jit(solution)/shard_map/while/body/eval_jaxpr/ppermute | solution.py:14
  689.4 12.4 %collective-permute-done = f32[4,128,64]{2,1,0:T(8,128)S(1)} collective-permute-done((f32[4,128,64]{2,1,0:T(8,128)S(1)}, f32[4,128,64]{2,1,0:T(8,128)S(1)}, u32[]{:S(2)}, u32[]{:S(2)}) %collective-permute-start) | collective-permute-done | bytes 131104 | tf_op jit(solution)/shard_map/while/body/eval_jaxpr/ppermute | solution.py:14
  (240 shorter events, 111.6 us)
Async XLA Ops:
  6.5 111.1 %all-gather.8.cloned.1.call-start = ((), (), s32[]{:S(2)}) async-start(), calls=%async_computation.1 | async-start | bytes 2228224 | tf_op jit(solution)/shard_map/all_gather | solution.py:134
  7.3 180.3 %all-gather.6.cloned.1.call-start = ((), (), s32[]{:S(2)}) async-start(), calls=%async_computation | async-start | bytes 8650752 | tf_op jit(solution)/shard_map/all_gather | solution.py:132
  8.0 285.1 %all-gather.12.cloned.1.call-start = ((), (), s32[]{:S(2)}) async-start(), calls=%async_computation.3 | async-start | bytes 2228224 | tf_op jit(solution)/shard_map/all_gather | solution.py:136
  8.8 386.7 %all-gather.10.cloned.1.call-start = ((), (), s32[]{:S(2)}) async-start(), calls=%async_computation.2 | async-start | bytes 2228224 | tf_op jit(solution)/shard_map/all_gather | solution.py:135
  300.2 102.6 %copy-start.9 = (f32[4]{0:T(128)S(1)}, f32[4]{0:T(128)}, u32[]{:S(2)}) copy-start(f32[4]{0:T(128)} %param.24) | copy-start | bytes 52
  300.3 112.0 %collective-permute-start.1 = (bf16[3,512]{1,0:T(4,128)(2,1)S(1)}, bf16[3,512]{1,0:T(4,128)(2,1)S(1)}, u32[]{:S(2)}, u32[]{:S(2)}) collective-permute-start(bf16[3,512]{1,0:T(4,128)(2,1)S(1)} %pad_maximum_fusion.2), channel_id=1, source_target_pairs={{0,32},{32,64},{64,96},{96,128},{128,160},{160,192},{192,224},{224... | collective-permute-start | bytes 9224 | tf_op jit(solution)/shard_map/ppermute | solution.py:14
  454.1 247.7 %copy-start.4 = (f32[4,4,128,64]{3,2,1,0:T(8,128)S(1)}, f32[4,4,128,64]{3,2,1,0:T(8,128)}, u32[]{:S(2)}) copy-start(f32[4,4,128,64]{3,2,1,0:T(8,128)} %get-tuple-element.135) | copy-start | bytes 1572868
  454.2 15.5 %collective-permute-start = (f32[4,128,64]{2,1,0:T(8,128)S(1)}, f32[4,128,64]{2,1,0:T(8,128)S(1)}, u32[]{:S(2)}, u32[]{:S(2)}) collective-permute-start(f32[4,128,64]{2,1,0:T(8,128)S(1)} %multiply_add_fusion.3), channel_id=1, source_target_pairs={{0,32},{32,64},{64,96},{96,128},{128,160},{160,192},{192,224},{224... | collective-permute-start | bytes 393224 | tf_op jit(solution)/shard_map/while/body/eval_jaxpr/ppermute | solution.py:14
  469.9 17.2 %collective-permute-start = (f32[4,128,64]{2,1,0:T(8,128)S(1)}, f32[4,128,64]{2,1,0:T(8,128)S(1)}, u32[]{:S(2)}, u32[]{:S(2)}) collective-permute-start(f32[4,128,64]{2,1,0:T(8,128)S(1)} %multiply_add_fusion.3), channel_id=1, source_target_pairs={{0,32},{32,64},{64,96},{96,128},{128,160},{160,192},{192,224},{224... | collective-permute-start | bytes 393224 | tf_op jit(solution)/shard_map/while/body/eval_jaxpr/ppermute | solution.py:14
  487.2 17.0 %collective-permute-start = (f32[4,128,64]{2,1,0:T(8,128)S(1)}, f32[4,128,64]{2,1,0:T(8,128)S(1)}, u32[]{:S(2)}, u32[]{:S(2)}) collective-permute-start(f32[4,128,64]{2,1,0:T(8,128)S(1)} %multiply_add_fusion.3), channel_id=1, source_target_pairs={{0,32},{32,64},{64,96},{96,128},{128,160},{160,192},{192,224},{224... | collective-permute-start | bytes 393224 | tf_op jit(solution)/shard_map/while/body/eval_jaxpr/ppermute | solution.py:14
  504.3 17.0 %collective-permute-start = (f32[4,128,64]{2,1,0:T(8,128)S(1)}, f32[4,128,64]{2,1,0:T(8,128)S(1)}, u32[]{:S(2)}, u32[]{:S(2)}) collective-permute-start(f32[4,128,64]{2,1,0:T(8,128)S(1)} %multiply_add_fusion.3), channel_id=1, source_target_pairs={{0,32},{32,64},{64,96},{96,128},{128,160},{160,192},{192,224},{224... | collective-permute-start | bytes 393224 | tf_op jit(solution)/shard_map/while/body/eval_jaxpr/ppermute | solution.py:14
  521.4 21.8 %collective-permute-start = (f32[4,128,64]{2,1,0:T(8,128)S(1)}, f32[4,128,64]{2,1,0:T(8,128)S(1)}, u32[]{:S(2)}, u32[]{:S(2)}) collective-permute-start(f32[4,128,64]{2,1,0:T(8,128)S(1)} %multiply_add_fusion.3), channel_id=1, source_target_pairs={{0,32},{32,64},{64,96},{96,128},{128,160},{160,192},{192,224},{224... | collective-permute-start | bytes 393224 | tf_op jit(solution)/shard_map/while/body/eval_jaxpr/ppermute | solution.py:14
  543.3 19.6 %collective-permute-start = (f32[4,128,64]{2,1,0:T(8,128)S(1)}, f32[4,128,64]{2,1,0:T(8,128)S(1)}, u32[]{:S(2)}, u32[]{:S(2)}) collective-permute-start(f32[4,128,64]{2,1,0:T(8,128)S(1)} %multiply_add_fusion.3), channel_id=1, source_target_pairs={{0,32},{32,64},{64,96},{96,128},{128,160},{160,192},{192,224},{224... | collective-permute-start | bytes 393224 | tf_op jit(solution)/shard_map/while/body/eval_jaxpr/ppermute | solution.py:14
  563.0 17.1 %collective-permute-start = (f32[4,128,64]{2,1,0:T(8,128)S(1)}, f32[4,128,64]{2,1,0:T(8,128)S(1)}, u32[]{:S(2)}, u32[]{:S(2)}) collective-permute-start(f32[4,128,64]{2,1,0:T(8,128)S(1)} %multiply_add_fusion.3), channel_id=1, source_target_pairs={{0,32},{32,64},{64,96},{96,128},{128,160},{160,192},{192,224},{224... | collective-permute-start | bytes 393224 | tf_op jit(solution)/shard_map/while/body/eval_jaxpr/ppermute | solution.py:14
  580.2 16.2 %collective-permute-start = (f32[4,128,64]{2,1,0:T(8,128)S(1)}, f32[4,128,64]{2,1,0:T(8,128)S(1)}, u32[]{:S(2)}, u32[]{:S(2)}) collective-permute-start(f32[4,128,64]{2,1,0:T(8,128)S(1)} %multiply_add_fusion.3), channel_id=1, source_target_pairs={{0,32},{32,64},{64,96},{96,128},{128,160},{160,192},{192,224},{224... | collective-permute-start | bytes 393224 | tf_op jit(solution)/shard_map/while/body/eval_jaxpr/ppermute | solution.py:14
  596.5 18.2 %collective-permute-start = (f32[4,128,64]{2,1,0:T(8,128)S(1)}, f32[4,128,64]{2,1,0:T(8,128)S(1)}, u32[]{:S(2)}, u32[]{:S(2)}) collective-permute-start(f32[4,128,64]{2,1,0:T(8,128)S(1)} %multiply_add_fusion.3), channel_id=1, source_target_pairs={{0,32},{32,64},{64,96},{96,128},{128,160},{160,192},{192,224},{224... | collective-permute-start | bytes 393224 | tf_op jit(solution)/shard_map/while/body/eval_jaxpr/ppermute | solution.py:14
  614.8 15.0 %collective-permute-start = (f32[4,128,64]{2,1,0:T(8,128)S(1)}, f32[4,128,64]{2,1,0:T(8,128)S(1)}, u32[]{:S(2)}, u32[]{:S(2)}) collective-permute-start(f32[4,128,64]{2,1,0:T(8,128)S(1)} %multiply_add_fusion.3), channel_id=1, source_target_pairs={{0,32},{32,64},{64,96},{96,128},{128,160},{160,192},{192,224},{224... | collective-permute-start | bytes 393224 | tf_op jit(solution)/shard_map/while/body/eval_jaxpr/ppermute | solution.py:14
  629.9 14.3 %collective-permute-start = (f32[4,128,64]{2,1,0:T(8,128)S(1)}, f32[4,128,64]{2,1,0:T(8,128)S(1)}, u32[]{:S(2)}, u32[]{:S(2)}) collective-permute-start(f32[4,128,64]{2,1,0:T(8,128)S(1)} %multiply_add_fusion.3), channel_id=1, source_target_pairs={{0,32},{32,64},{64,96},{96,128},{128,160},{160,192},{192,224},{224... | collective-permute-start | bytes 393224 | tf_op jit(solution)/shard_map/while/body/eval_jaxpr/ppermute | solution.py:14
  644.3 14.3 %collective-permute-start = (f32[4,128,64]{2,1,0:T(8,128)S(1)}, f32[4,128,64]{2,1,0:T(8,128)S(1)}, u32[]{:S(2)}, u32[]{:S(2)}) collective-permute-start(f32[4,128,64]{2,1,0:T(8,128)S(1)} %multiply_add_fusion.3), channel_id=1, source_target_pairs={{0,32},{32,64},{64,96},{96,128},{128,160},{160,192},{192,224},{224... | collective-permute-start | bytes 393224 | tf_op jit(solution)/shard_map/while/body/eval_jaxpr/ppermute | solution.py:14
  658.7 14.3 %collective-permute-start = (f32[4,128,64]{2,1,0:T(8,128)S(1)}, f32[4,128,64]{2,1,0:T(8,128)S(1)}, u32[]{:S(2)}, u32[]{:S(2)}) collective-permute-start(f32[4,128,64]{2,1,0:T(8,128)S(1)} %multiply_add_fusion.3), channel_id=1, source_target_pairs={{0,32},{32,64},{64,96},{96,128},{128,160},{160,192},{192,224},{224... | collective-permute-start | bytes 393224 | tf_op jit(solution)/shard_map/while/body/eval_jaxpr/ppermute | solution.py:14
  673.1 14.3 %collective-permute-start = (f32[4,128,64]{2,1,0:T(8,128)S(1)}, f32[4,128,64]{2,1,0:T(8,128)S(1)}, u32[]{:S(2)}, u32[]{:S(2)}) collective-permute-start(f32[4,128,64]{2,1,0:T(8,128)S(1)} %multiply_add_fusion.3), channel_id=1, source_target_pairs={{0,32},{32,64},{64,96},{96,128},{128,160},{160,192},{192,224},{224... | collective-permute-start | bytes 393224 | tf_op jit(solution)/shard_map/while/body/eval_jaxpr/ppermute | solution.py:14
  687.5 14.3 %collective-permute-start = (f32[4,128,64]{2,1,0:T(8,128)S(1)}, f32[4,128,64]{2,1,0:T(8,128)S(1)}, u32[]{:S(2)}, u32[]{:S(2)}) collective-permute-start(f32[4,128,64]{2,1,0:T(8,128)S(1)} %multiply_add_fusion.3), channel_id=1, source_target_pairs={{0,32},{32,64},{64,96},{96,128},{128,160},{160,192},{192,224},{224... | collective-permute-start | bytes 393224 | tf_op jit(solution)/shard_map/while/body/eval_jaxpr/ppermute | solution.py:14
  701.8 3.7 copy-start.3
  702.9 5.1 copy-start.1
  (6 other events, 10.0 us)
Sparse Core Ops, SparseCore 0:
  10.5 107.0 all-gather.7
  119.8 67.7 all-gather.5
  190.7 102.3 all-gather.11
  296.1 99.3 all-gather.9
where the time goes:
time: 722 us; the launch traced here: 721 us
  waiting for transfers between devices  527 us (73%)
  blocking collectives  56 us (8%)
  starting transfers between devices  33 us (5%)
  matrix products  31.8 us (4%)
  local copies, waits for them, and re-layouts  28.9 us (4%)
  other arithmetic  25.4 us (4%)
  between operations  13.3 us (2%)
    ppermute x16, waiting for transfers between devices, passed_along(): lax.ppermute(value, axis, [(source, source + steps) for source in range(l...  216 us
    all_gather x1, waiting for transfers between devices, local(): lax.all_gather(state_own, 'seq', axis=0, tiled=True)  98.4 us
    all_gather x1, waiting for transfers between devices, local(): lax.all_gather(gate_weight, 'seq', axis=0, tiled=True)  92.2 us
    all_gather x1, waiting for transfers between devices, local(): gathered = lax.all_gather(tokens, 'head', axis=0, tiled=True)  69.9 us
    all_gather x1, blocking collectives, local(): lax.all_gather(step_weight, 'seq', axis=0, tiled=True)  56 us
    all_gather x1, waiting for transfers between devices, local(): lax.all_gather(value_weight, 'seq', axis=0, tiled=True)  48 us
    ppermute x16, starting transfers between devices, passed_along(): lax.ppermute(value, axis, [(source, source + steps) for source in range(l...  32.9 us
    dot_general x4, matrix products, local(): jnp.dot(gathered, weight_piece, preferred_element_type=jnp.float32)  25.7 us
  transfers between devices with their start and end apart: 20, of which 19 were waited for; matrix products, arithmetic and copies ran while one was open for 5% of the time, Pallas kernels for 0%

commit v1 on v0

v1 whole, which is shorter than its diff:
```python
import jax
import jax.numpy as jnp
from jax import lax
from jax.sharding import Mesh
from jax.sharding import PartitionSpec as P

HEADS = 128
GROUPS = 8
BLOCK = 256
STATE = 128
YH, Z, X, Y, C = 2, 8, 4, 4, 2
SEQ = ("yh", "z")
HEAD = ("x", "y", "c")
F32 = jnp.float32
BF16 = jnp.bfloat16


def ring(count, step):
    return [(i, (i + step) % count) for i in range(count)]


def along_seq(value, step):
    return lax.ppermute(value, SEQ, [(i, i + step) for i in range(YH * Z - step)])


def ring_gather(block):
    half = block.shape[1] // 2
    right = left = block
    z = lax.axis_index("z")
    held = jnp.zeros((Z,) + block.shape, block.dtype)

    def put(held, piece, offset, row):
        return lax.dynamic_update_slice(held, piece[None], ((z + offset) % Z, 0, row, 0))

    held = put(held, block, 0, 0)
    for step in range(1, 4):
        right = lax.ppermute(right, "z", ring(Z, 1))
        left = lax.ppermute(left, "z", ring(Z, -1))
        held = put(held, right, -step + Z, 0)
        held = put(held, left, step, 0)
    right = lax.ppermute(right[:, :half], "z", ring(Z, 1))
    left = lax.ppermute(left[:, half:], "z", ring(Z, -1))
    held = put(held, right, 4, 0)
    held = put(held, left, 4, half)
    return held


def segment_of(positions, starts):
    reached = (starts[None, :] <= positions[:, None]).astype(jnp.int32)
    return jnp.sum(reached, axis=1) - 1


def causal_conv(extended, taps_weight, seg_ext, row_count):
    tap_count = taps_weight.shape[0]
    own_segment = seg_ext[tap_count - 1 :]
    summed = jnp.zeros((row_count, extended.shape[1]), F32)
    for tap_index in range(tap_count):
        window = extended[tap_index : tap_index + row_count].astype(F32)
        keep_mask = (seg_ext[tap_index : tap_index + row_count] == own_segment).astype(F32)
        summed = summed + taps_weight[tap_index][None, :] * window * keep_mask[:, None]
    return jax.nn.silu(summed).astype(BF16)


def block_terms(b_rows, c_rows, x_rows, decay_rows, step_rows, segments, seg_before):
    block_len = b_rows.shape[0]
    head_total = decay_rows.shape[0]
    x_heads = x_rows.reshape(block_len, head_total, -1)
    cumulative = jnp.cumsum(decay_rows, axis=1)
    products = jnp.dot(c_rows, b_rows.T, preferred_element_type=F32)
    local_index = jnp.arange(block_len)
    allowed = (local_index[None, :] <= local_index[:, None]) & (
        segments[None, :] == segments[:, None]
    )
    spread = cumulative[:, :, None] - cumulative[:, None, :]
    decay_mat = jnp.where(allowed[None], jnp.exp(jnp.where(allowed[None], spread, 0.0)), 0.0)
    scores = (products[None] * decay_mat * step_rows[:, None, :]).astype(BF16)
    y_inner = jnp.einsum("hij,jhp->ihp", scores, x_heads, preferred_element_type=F32)
    ending = cumulative[:, -1]
    trailing = (
        jnp.where((segments == segments[-1])[None, :], jnp.exp(ending[:, None] - cumulative), 0.0)
        * step_rows
    )
    weighted = (trailing.T[:, :, None] * x_heads.astype(F32)).astype(BF16)
    local_state = jnp.dot(
        b_rows.T, weighted.reshape(block_len, -1), preferred_element_type=F32
    )
    factor = jnp.where(segments[-1] == seg_before, jnp.exp(ending), 0.0)
    entry_gain = jnp.where((segments == seg_before)[None, :], jnp.exp(cumulative), 0.0)
    return (y_inner.reshape(block_len, -1), local_state, factor, entry_gain)


def spread_heads(values, width):
    return jnp.repeat(values, width, axis=-1)


def scan_shards(state, gain):
    rows = jnp.broadcast_to(gain[None, :], (8, gain.shape[0]))
    packed = jnp.concatenate([state, rows], axis=0)
    near = [along_seq(packed, step) for step in (1, 2, 3)]
    total, gains = packed[:STATE], packed[STATE : STATE + 1]
    for piece in near:
        total = total + gains * piece[:STATE]
        gains = gains * piece[STATE : STATE + 1]
    packed = jnp.concatenate([total, jnp.broadcast_to(gains, (8, gains.shape[1]))], axis=0)
    first, second = along_seq(packed, 1), along_seq(packed, 5)
    return first[:STATE] + first[STATE : STATE + 1] * second[:STATE]


def local(
    tokens,
    doc_lengths,
    value_weight,
    gate_weight,
    state_weight,
    step_weight,
    value_conv,
    state_conv,
    step_bias,
    log_rate,
):
    tok_dev = tokens.shape[0] * X * Y * C
    heads_here = step_weight.shape[1]
    tap_count = value_conv.shape[0]
    blocks = tok_dev // BLOCK
    cols = value_weight.shape[1]
    core = lax.axis_index("c")
    group = lax.axis_index("x") * 2 + lax.axis_index("y") // 2
    gathered = lax.all_gather(tokens, HEAD, axis=0, tiled=True)

    state_own = lax.dynamic_index_in_dim(state_weight, group, 0, keepdims=False)
    conv_own = lax.dynamic_index_in_dim(state_conv, group, 0, keepdims=False)
    state_half = jnp.where(core == 0, state_own[:, :STATE], state_own[:, STATE:])
    state_half = jnp.concatenate([state_half[:STATE], state_half[STATE:]], axis=1)
    step_rows = jnp.pad(step_weight.T, ((0, 8 - heads_here), (0, 0)))
    pack = jnp.concatenate([value_weight, state_half, step_rows, gate_weight], axis=0)
    both = lax.all_gather(pack, "yh", axis=0, tiled=False)
    first_rows = 256 + STATE + 8
    gate_all = lax.all_gather(both[:, first_rows:], "z", axis=0, tiled=False)
    held = ring_gather(both[:, :first_rows]).transpose(1, 0, 2, 3)

    depth = tokens.shape[1]
    value_all = held[:, :, :256].reshape(depth, cols)
    state_all = held[:, :, 256 : 256 + STATE]
    state_all = jnp.stack([state_all[..., :STATE], state_all[..., STATE:]], axis=2)
    state_all = state_all.reshape(depth, STATE)
    step_all = held[:, :, 256 + STATE :].transpose(0, 1, 3, 2).reshape(depth, 8)[:, :heads_here]

    half_proj = jnp.dot(gathered, state_all, preferred_element_type=F32).astype(BF16)
    other_proj = lax.ppermute(half_proj, "c", [(0, 1), (1, 0)])
    value_proj = jnp.dot(gathered, value_all, preferred_element_type=F32).astype(BF16)
    step_proj = jnp.dot(gathered, step_all, preferred_element_type=F32).astype(BF16)
    b_proj = jnp.where(core == 0, half_proj, other_proj)
    c_proj = jnp.where(core == 0, other_proj, half_proj)
    state_proj = jnp.concatenate([b_proj, c_proj], axis=1)

    rim_source = jnp.concatenate(
        [value_proj[-(tap_count - 1) :], state_proj[-(tap_count - 1) :]], axis=1
    )
    rim_rows = along_seq(rim_source, 1)
    value_ext = jnp.concatenate([rim_rows[:, :cols], value_proj], axis=0)
    state_ext = jnp.concatenate([rim_rows[:, cols:], state_proj], axis=0)
    starts = jnp.cumsum(doc_lengths) - doc_lengths
    positions = lax.axis_index(SEQ) * tok_dev + jnp.arange(-(tap_count - 1), tok_dev)
    seg_ext = segment_of(positions, starts)
    value_act = causal_conv(value_ext, value_conv, seg_ext, tok_dev)
    state_act = causal_conv(state_ext, conv_own, seg_ext, tok_dev)
    step_size = jax.nn.softplus(step_proj.astype(F32) + step_bias[None, :])
    decay_rate = -jnp.exp(log_rate)[None, :] * step_size
    seg_rows = seg_ext[tap_count - 1 :].reshape(blocks, BLOCK)
    seg_before = seg_ext[tap_count - 2 : tap_count - 2 + tok_dev : BLOCK]

    b_all = state_act[:, :STATE].reshape(blocks, BLOCK, STATE)
    c_all = state_act[:, STATE:].reshape(blocks, BLOCK, STATE)
    x_all = value_act.reshape(blocks, BLOCK, cols)
    decay_all = decay_rate.reshape(blocks, BLOCK, heads_here).transpose(0, 2, 1)
    step_all = step_size.reshape(blocks, BLOCK, heads_here).transpose(0, 2, 1)
    y_inner, local_state, factor, entry_gain = lax.map(
        lambda item: block_terms(*item),
        (b_all, c_all, x_all, decay_all, step_all, seg_rows, seg_before),
    )
    width = cols // heads_here
    factor = spread_heads(factor, width)
    running = jnp.zeros((STATE, cols), F32)
    gain = jnp.ones((cols,), F32)
    inside, gains = [], []
    for index in range(blocks):
        inside.append(running)
        gains.append(gain)
        running = factor[index][None, :] * running + local_state[index]
        gain = gain * factor[index]
    entering = scan_shards(running, gain)
    gate_full = gate_all.transpose(1, 0, 2, 3).reshape(depth, cols)
    gate_proj = jnp.dot(gathered, gate_full, preferred_element_type=F32).astype(BF16)
    outs = []
    for index in range(blocks):
        incoming = inside[index] + gains[index][None, :] * entering
        carried = jnp.dot(c_all[index].astype(F32), incoming, precision=lax.Precision.HIGHEST)
        carried = carried * spread_heads(entry_gain[index].T, width)
        total = y_inner[index] + carried + x_all[index].astype(F32)
        gating = jax.nn.silu(gate_proj[index * BLOCK : (index + 1) * BLOCK].astype(F32))
        outs.append((total * gating).astype(BF16))
    return jnp.concatenate(outs, axis=0)


def solution(mesh):
    grid = Mesh(mesh.devices.reshape(YH, Z, X, Y, C), SEQ + HEAD)
    return jax.shard_map(
        local,
        mesh=grid,
        in_specs=(
            P(SEQ + HEAD, None),
            P(),
            P(SEQ, HEAD),
            P(SEQ, HEAD),
            P(None, SEQ, None),
            P(SEQ, HEAD),
            P(None, HEAD),
            P(),
            P(HEAD),
            P(HEAD),
        ),
        out_specs=P(SEQ, HEAD),
        check_vma=False,
    )
```

time: 722 us -> 298 us (0.41)
  the two profiles are of different devices: /device:TPU:48 before, /device:TPU:112 now
where the time goes in v1:
time: 298 us; the launch traced here: 297 us
  waiting for transfers between devices  120 us (40%)
  starting transfers between devices  58.9 us (20%)
  local copies, waits for them, and re-layouts  35.8 us (12%)
  matrix products  24.7 us (8%)
  blocking collectives  21 us (7%)
  other arithmetic  17.4 us (6%)
  between operations  14.1 us (5%)
  loops' own time  5.8 us (2%)
    all_gather x1, waiting for transfers between devices, local(): gathered = lax.all_gather(tokens, HEAD, axis=0, tiled=True)  49.4 us
    ppermute x6, waiting for transfers between devices, along_seq(): lax.ppermute(value, SEQ, [(i, i + step) for i in range(YH * Z - step)])  46.3 us
    ppermute x6, starting transfers between devices, along_seq(): lax.ppermute(value, SEQ, [(i, i + step) for i in range(YH * Z - step)])  23.6 us
    all_gather x1, blocking collectives, local(): both = lax.all_gather(pack, 'yh', axis=0, tiled=False)  21 us
    ppermute x3, waiting for transfers between devices, ring_gather(): right = lax.ppermute(right, 'z', ring(Z, 1))  20.9 us
    ppermute x3, starting transfers between devices, ring_gather(): left = lax.ppermute(left, 'z', ring(Z, -1))  15.9 us
    ppermute x3, starting transfers between devices, ring_gather(): right = lax.ppermute(right, 'z', ring(Z, 1))  11.3 us
    dynamic_update_slice x9, local copies, waits for them, and re-layouts, put(): lax.dynamic_update_slice(held, piece[None], ((z + offset) % Z, 0, row, 0))  9.48 us
  transfers between devices with their start and end apart: 17, of which 13 were waited for; matrix products, arithmetic and copies ran while one was open for 11% of the time, Pallas kernels for 0%

profile of v1, /device:TPU:112, one launch (start us, length us, event | category | flops | bytes accessed | tf_op | source)
XLA Modules:
  0.0 297.2 jit_solution(12818761446502483740)
XLA Ops:
  8.8 21.0 %all-gather = bf16[1296,256]{1,0:T(8,128)(2,1)S(1)} all-gather(bf16[648,256]{1,0:T(8,128)(2,1)S(1)} %fusion.47), channel_id=2, replica_groups=mesh['yh'=2,'z'=8,'x'=4,'y'=4,'c'=2] {'yh'}, dimensions={0}, use_global_device_ids=true | all-gather | bytes 995328 | tf_op jit(solution)/shard_map/all_gather | solution.py:136
  31.4 4.3 %collective-permute-start = (bf16[2,392,256]{2,1,0:T(8,128)(2,1)S(1)}, bf16[2,392,256]{2,1,0:T(8,128)(2,1)S(1)}, u32[]{:S(2)}, u32[]{:S(2)}) collective-permute-start(bf16[2,392,256]{2,1,0:T(8,128)(2,1)S(1)} %slice.371), channel_id=1, source_target_pairs={{0,32},{32,64},{64,96},{96,128},{128,160},{160,192},{192,224},{224... | collective-permute-start | bytes 1204232 | tf_op jit(solution)/shard_map/ppermute | solution.py:37
  43.4 4.3 %collective-permute-start.2 = (bf16[2,392,256]{2,1,0:T(8,128)(2,1)S(1)}, bf16[2,392,256]{2,1,0:T(8,128)(2,1)S(1)}, u32[]{:S(2)}, u32[]{:S(2)}) collective-permute-start(bf16[2,392,256]{2,1,0:T(8,128)(2,1)S(1)} %collective-permute-done), channel_id=1, source_target_pairs={{0,32},{32,64},{64,96},{96,128},{128,160},{160,192},{192,224},{224... | collective-permute-start | bytes 1204232 | tf_op jit(solution)/shard_map/ppermute | solution.py:37
  48.1 8.5 %collective-permute-start.3 = (bf16[2,392,256]{2,1,0:T(8,128)(2,1)S(1)}, bf16[2,392,256]{2,1,0:T(8,128)(2,1)S(1)}, u32[]{:S(2)}, u32[]{:S(2)}) collective-permute-start(bf16[2,392,256]{2,1,0:T(8,128)(2,1)S(1)} %collective-permute-done.1), channel_id=1, source_target_pairs={{0,224},{32,0},{64,32},{96,64},{128,96},{160,128},{192,160},{224,1... | collective-permute-start | bytes 1204232 | tf_op jit(solution)/shard_map/ppermute | solution.py:38
  58.1 9.0 %collective-permute-done.2 = bf16[2,392,256]{2,1,0:T(8,128)(2,1)S(1)} collective-permute-done((bf16[2,392,256]{2,1,0:T(8,128)(2,1)S(1)}, bf16[2,392,256]{2,1,0:T(8,128)(2,1)S(1)}, u32[]{:S(2)}, u32[]{:S(2)}) %collective-permute-start.2) | collective-permute-done | bytes 401440 | tf_op jit(solution)/shard_map/ppermute | solution.py:37
  67.2 2.8 collective-permute-start.4
  71.3 5.5 %collective-permute-start.5 = (bf16[2,392,256]{2,1,0:T(8,128)(2,1)S(1)}, bf16[2,392,256]{2,1,0:T(8,128)(2,1)S(1)}, u32[]{:S(2)}, u32[]{:S(2)}) collective-permute-start(bf16[2,392,256]{2,1,0:T(8,128)(2,1)S(1)} %collective-permute-done.3), channel_id=1, source_target_pairs={{0,224},{32,0},{64,32},{96,64},{128,96},{160,128},{192,160},{224,1... | collective-permute-start | bytes 1204232 | tf_op jit(solution)/shard_map/ppermute | solution.py:38
  78.4 10.5 %collective-permute-done.4 = bf16[2,392,256]{2,1,0:T(8,128)(2,1)S(1)} collective-permute-done((bf16[2,392,256]{2,1,0:T(8,128)(2,1)S(1)}, bf16[2,392,256]{2,1,0:T(8,128)(2,1)S(1)}, u32[]{:S(2)}, u32[]{:S(2)}) %collective-permute-start.4) | collective-permute-done | bytes 401440 | tf_op jit(solution)/shard_map/ppermute | solution.py:37
  90.8 3.9 %collective-permute-start.7 = (bf16[2,196,256]{2,1,0:T(8,128)(2,1)S(1)}, bf16[2,196,256]{2,1,0:T(8,128)(2,1)S(1)}, u32[]{:S(2)}, u32[]{:S(2)}) collective-permute-start(bf16[2,196,256]{2,1,0:T(8,128)(2,1)S(1)} %slice.373), channel_id=1, source_target_pairs={{0,224},{32,0},{64,32},{96,64},{128,96},{160,128},{192,160},{224,1... | collective-permute-start | bytes 602120 | tf_op jit(solution)/shard_map/ppermute | solution.py:42
  100.8 3.1 %slice.374 = bf16[2,8,256,256]{3,2,1,0:T(8,128)(2,1)} slice(bf16[2,8,392,256]{3,2,1,0:T(8,128)(2,1)} %bitcast.36), slice={[0:2], [0:8], [0:256], [0:256]} | slice | bytes 4194304 | tf_op jit(solution)/shard_map/slice | solution.py:142
  106.2 3.2 %copy.121 = bf16[2,8,256,256]{3,2,1,0:T(8,128)(2,1)} copy(bf16[2,8,256,256]{3,2,0,1:T(8,128)(2,1)} %bitcast.241) | data formatting | bytes 4194304 | tf_op jit(solution)/shard_map/transpose | solution.py:192
  109.5 49.4 %all-gather.5.cloned.1.call-done = bf16[1024,4096]{1,0:T(8,128)(2,1)} async-done(((bf16[32,4096]{1,0:T(8,128)(2,1)}), bf16[1024,4096]{1,0:T(8,128)(2,1)}) %all-gather.5.cloned.1.call-update) | async-done | bytes 8388624 | tf_op jit(solution)/shard_map/all_gather | solution.py:128
  158.9 6.4 %fusion.34 = bf16[1024,128]{0,1:T(8,128)(2,1)S(1)} fusion(bf16[4096,128]{1,0:T(8,128)(2,1)S(1)} %bitcast.238, bf16[1024,4096]{1,0:T(8,128)(2,1)} %all-gather.5.cloned.1.call-done), kind=kOutput, calls=%fused_computation.58 | convolution fusion | flops 1073872896 | bytes 9699328 | tf_op jit(solution)/shard_map/dot_general | solution.py:148
  167.5 4.1 %fusion.20 = bf16[1024,256]{0,1:T(8,128)(2,1)S(1)} fusion(bf16[4096,256]{1,0:T(8,128)(2,1)} %bitcast.242, bf16[1024,4096]{1,0:T(8,128)(2,1)S(1)} %copy-done.1), kind=kOutput, calls=%fused_computation.39 | convolution fusion | flops 2147745792 | bytes 11010048 | tf_op jit(solution)/shard_map/dot_general | solution.py:150
  171.6 3.2 %fusion.21 = bf16[1024,256]{0,1:T(8,128)(2,1)} fusion(bf16[4096,256]{1,0:T(8,128)(2,1)S(1)} %bitcast.243, bf16[1024,4096]{1,0:T(8,128)(2,1)S(1)} %copy-done.1), kind=kOutput, calls=%fused_computation.40 | convolution fusion | flops 2147745792 | bytes 11010048 | tf_op jit(solution)/shard_map/dot_general | solution.py:193
  175.1 3.9 %collective-permute-start.9 = (bf16[3,512]{0,1:T(8,128)(2,1)S(1)}, bf16[3,512]{0,1:T(8,128)(2,1)S(1)}, u32[]{:S(2)}, u32[]{:S(2)}) collective-permute-start(bf16[3,512]{0,1:T(8,128)(2,1)S(1)} %pad_maximum_fusion.6), channel_id=1, source_target_pairs={{0,32},{32,64},{64,96},{96,128},{128,160},{160,192},{192,224},{224... | collective-permute-start | bytes 9224 | tf_op jit(solution)/shard_map/ppermute | solution.py:23
  185.7 34.4 %while.16 = (s32[]{:T(128)}, f32[4,256,256]{1,2,0:T(8,128)}, f32[4,128,256]{2,1,0:T(8,128)}, f32[4,4]{1,0:T(4,128)S(1)}, f32[4,4,256]{2,1,0:T(4,128)S(1)}, /*ind...) while((s32[]{:T(128)}, f32[4,256,256]{1,2,0:T(8,128)}, ...), condition=%wide.region_5.6_spmd, body=%wide.region_2.5_spmd.sunk | while | flops 69210640 | bytes 2653675 | solution.py:177
  221.9 3.7 %collective-permute-start.10 = (f32[136,256]{1,0:T(8,128)S(1)}, f32[136,256]{1,0:T(8,128)S(1)}, u32[]{:S(2)}, u32[]{:S(2)}) collective-permute-start(f32[136,256]{1,0:T(8,128)S(1)} %pad_maximum_fusion.4), channel_id=1, source_target_pairs={{0,32},{32,64},{64,96},{96,128},{128,160},{160,192},{192,224},{224... | collective-permute-start | bytes 417800 | tf_op jit(solution)/shard_map/ppermute | solution.py:23
  225.6 6.9 %collective-permute-start.11 = (f32[136,256]{1,0:T(8,128)S(1)}, f32[136,256]{1,0:T(8,128)S(1)}, u32[]{:S(2)}, u32[]{:S(2)}) collective-permute-start(f32[136,256]{1,0:T(8,128)S(1)} %pad_maximum_fusion.4), channel_id=1, source_target_pairs={{0,64},{32,96},{64,128},{96,160},{128,192},{160,224},{192,256},{22... | collective-permute-start | bytes 417800 | tf_op jit(solution)/shard_map/ppermute | solution.py:23
  234.7 2.9 collective-permute-done.10
  237.5 24.1 %collective-permute-done.11 = f32[136,256]{1,0:T(8,128)S(1)} collective-permute-done((f32[136,256]{1,0:T(8,128)S(1)}, f32[136,256]{1,0:T(8,128)S(1)}, u32[]{:S(2)}, u32[]{:S(2)}) %collective-permute-start.11) | collective-permute-done | bytes 139296 | tf_op jit(solution)/shard_map/ppermute | solution.py:23
  261.7 2.4 collective-permute-done.12
  264.2 5.1 %collective-permute-start.13 = (f32[136,256]{1,0:T(8,128)S(1)}, f32[136,256]{1,0:T(8,128)S(1)}, u32[]{:S(2)}, u32[]{:S(2)}) collective-permute-start(f32[136,256]{1,0:T(8,128)S(1)} %pad_maximum_fusion.5), channel_id=1, source_target_pairs={{0,32},{32,64},{64,96},{96,128},{128,160},{160,192},{192,224},{224... | collective-permute-start | bytes 417800 | tf_op jit(solution)/shard_map/ppermute | solution.py:23
  272.1 14.6 %collective-permute-done.14 = f32[136,256]{1,0:T(8,128)S(1)} collective-permute-done((f32[136,256]{1,0:T(8,128)S(1)}, f32[136,256]{1,0:T(8,128)S(1)}, u32[]{:S(2)}, u32[]{:S(2)}) %collective-permute-start.14) | collective-permute-done | bytes 139296 | tf_op jit(solution)/shard_map/ppermute | solution.py:23
  (233 shorter events, 74.4 us)
Async XLA Ops:
  6.5 31.0 %copy-start.6 = (s32[16]{0:T(128)S(1)}, s32[16]{0:T(128)}, u32[]{:S(2)}) copy-start(s32[16]{0:T(128)} %param.13) | copy-start | bytes 196
  6.5 31.4 %copy-start.4 = (f32[4,256]{1,0:T(4,128)S(1)}, f32[4,256]{1,0:T(4,128)}, u32[]{:S(2)}) copy-start(f32[4,256]{1,0:T(4,128)} %param.18) | copy-start | bytes 12292
  6.5 31.5 %copy-start.8 = (f32[4]{0:T(128)S(1)}, f32[4]{0:T(128)}, u32[]{:S(2)}) copy-start(f32[4]{0:T(128)} %param.21) | copy-start | bytes 52
  6.5 99.7 %all-gather.7.cloned.1.call-start = ((), (), s32[]{:S(2)}) async-start(), calls=%async_computation.1 | async-start | bytes 2359296 | tf_op jit(solution)/shard_map/all_gather | solution.py:138
  30.6 128.3 %all-gather.5.cloned.1.call-start = ((), (), s32[]{:S(2)}) async-start(), calls=%async_computation | async-start | bytes 8650752 | tf_op jit(solution)/shard_map/all_gather | solution.py:128
  31.4 12.1 %collective-permute-start = (bf16[2,392,256]{2,1,0:T(8,128)(2,1)S(1)}, bf16[2,392,256]{2,1,0:T(8,128)(2,1)S(1)}, u32[]{:S(2)}, u32[]{:S(2)}) collective-permute-start(bf16[2,392,256]{2,1,0:T(8,128)(2,1)S(1)} %slice.371), channel_id=1, source_target_pairs={{0,32},{32,64},{64,96},{96,128},{128,160},{160,192},{192,224},{224... | collective-permute-start | bytes 1204232 | tf_op jit(solution)/shard_map/ppermute | solution.py:37
  35.6 12.4 %collective-permute-start.1 = (bf16[2,392,256]{2,1,0:T(8,128)(2,1)S(1)}, bf16[2,392,256]{2,1,0:T(8,128)(2,1)S(1)}, u32[]{:S(2)}, u32[]{:S(2)}) collective-permute-start(bf16[2,392,256]{2,1,0:T(8,128)(2,1)S(1)} %slice.371), channel_id=1, source_target_pairs={{0,224},{32,0},{64,32},{96,64},{128,96},{160,128},{192,160},{224,1... | collective-permute-start | bytes 1204232 | tf_op jit(solution)/shard_map/ppermute | solution.py:38
  43.4 23.8 %collective-permute-start.2 = (bf16[2,392,256]{2,1,0:T(8,128)(2,1)S(1)}, bf16[2,392,256]{2,1,0:T(8,128)(2,1)S(1)}, u32[]{:S(2)}, u32[]{:S(2)}) collective-permute-start(bf16[2,392,256]{2,1,0:T(8,128)(2,1)S(1)} %collective-permute-done), channel_id=1, source_target_pairs={{0,32},{32,64},{64,96},{96,128},{128,160},{160,192},{192,224},{224... | collective-permute-start | bytes 1204232 | tf_op jit(solution)/shard_map/ppermute | solution.py:37
  48.1 23.2 %collective-permute-start.3 = (bf16[2,392,256]{2,1,0:T(8,128)(2,1)S(1)}, bf16[2,392,256]{2,1,0:T(8,128)(2,1)S(1)}, u32[]{:S(2)}, u32[]{:S(2)}) collective-permute-start(bf16[2,392,256]{2,1,0:T(8,128)(2,1)S(1)} %collective-permute-done.1), channel_id=1, source_target_pairs={{0,224},{32,0},{64,32},{96,64},{128,96},{160,128},{192,160},{224,1... | collective-permute-start | bytes 1204232 | tf_op jit(solution)/shard_map/ppermute | solution.py:38
  67.2 21.6 %collective-permute-start.4 = (bf16[2,392,256]{2,1,0:T(8,128)(2,1)S(1)}, bf16[2,392,256]{2,1,0:T(8,128)(2,1)S(1)}, u32[]{:S(2)}, u32[]{:S(2)}) collective-permute-start(bf16[2,392,256]{2,1,0:T(8,128)(2,1)S(1)} %collective-permute-done.2), channel_id=1, source_target_pairs={{0,32},{32,64},{64,96},{96,128},{128,160},{160,192},{192,224},{224... | collective-permute-start | bytes 1204232 | tf_op jit(solution)/shard_map/ppermute | solution.py:37
  71.3 19.5 %collective-permute-start.5 = (bf16[2,392,256]{2,1,0:T(8,128)(2,1)S(1)}, bf16[2,392,256]{2,1,0:T(8,128)(2,1)S(1)}, u32[]{:S(2)}, u32[]{:S(2)}) collective-permute-start(bf16[2,392,256]{2,1,0:T(8,128)(2,1)S(1)} %collective-permute-done.3), channel_id=1, source_target_pairs={{0,224},{32,0},{64,32},{96,64},{128,96},{160,128},{192,160},{224,1... | collective-permute-start | bytes 1204232 | tf_op jit(solution)/shard_map/ppermute | solution.py:38
  88.8 8.0 %collective-permute-start.6 = (bf16[2,196,256]{2,1,0:T(8,128)(2,1)S(1)}, bf16[2,196,256]{2,1,0:T(8,128)(2,1)S(1)}, u32[]{:S(2)}, u32[]{:S(2)}) collective-permute-start(bf16[2,196,256]{2,1,0:T(8,128)(2,1)S(1)} %slice.372), channel_id=1, source_target_pairs={{0,32},{32,64},{64,96},{96,128},{128,160},{160,192},{192,224},{224... | collective-permute-start | bytes 602120 | tf_op jit(solution)/shard_map/ppermute | solution.py:41
  90.8 8.1 %collective-permute-start.7 = (bf16[2,196,256]{2,1,0:T(8,128)(2,1)S(1)}, bf16[2,196,256]{2,1,0:T(8,128)(2,1)S(1)}, u32[]{:S(2)}, u32[]{:S(2)}) collective-permute-start(bf16[2,196,256]{2,1,0:T(8,128)(2,1)S(1)} %slice.373), channel_id=1, source_target_pairs={{0,224},{32,0},{64,32},{96,64},{128,96},{160,128},{192,160},{224,1... | collective-permute-start | bytes 602120 | tf_op jit(solution)/shard_map/ppermute | solution.py:42
  158.9 8.6 %copy-start.1 = (bf16[1024,4096]{1,0:T(8,128)(2,1)S(1)}, bf16[1024,4096]{1,0:T(8,128)(2,1)}, u32[]{:S(2)}) copy-start(bf16[1024,4096]{1,0:T(8,128)(2,1)} %all-gather.5.cloned.1.call-done) | copy-start | bytes 25165828
  165.3 9.6 %collective-permute-start.8 = (bf16[1024,128]{0,1:T(8,128)(2,1)S(1)}, bf16[1024,128]{0,1:T(8,128)(2,1)S(1)}, u32[]{:S(2)}, u32[]{:S(2)}) collective-permute-start(bf16[1024,128]{0,1:T(8,128)(2,1)S(1)} %fusion.34), channel_id=1, source_target_pairs={{0,1},{1,0},{2,3},{3,2},{4,5},{5,4},{6,7},{7,6},{8,9},{9,8},{10,11... | collective-permute-start | bytes 786440 | tf_op jit(solution)/shard_map/ppermute | solution.py:149
  175.1 7.6 %collective-permute-start.9 = (bf16[3,512]{0,1:T(8,128)(2,1)S(1)}, bf16[3,512]{0,1:T(8,128)(2,1)S(1)}, u32[]{:S(2)}, u32[]{:S(2)}) collective-permute-start(bf16[3,512]{0,1:T(8,128)(2,1)S(1)} %pad_maximum_fusion.6), channel_id=1, source_target_pairs={{0,32},{32,64},{64,96},{96,128},{128,160},{160,192},{192,224},{224... | collective-permute-start | bytes 9224 | tf_op jit(solution)/shard_map/ppermute | solution.py:23
  220.1 68.1 %copy-start.3 = (f32[4,128,256]{2,1,0:T(8,128)S(1)}, f32[4,128,256]{2,1,0:T(8,128)}, u32[]{:S(2)}) copy-start(f32[4,128,256]{2,1,0:T(8,128)} %get-tuple-element.72) | copy-start | bytes 1572868
  221.9 15.7 %collective-permute-start.10 = (f32[136,256]{1,0:T(8,128)S(1)}, f32[136,256]{1,0:T(8,128)S(1)}, u32[]{:S(2)}, u32[]{:S(2)}) collective-permute-start(f32[136,256]{1,0:T(8,128)S(1)} %pad_maximum_fusion.4), channel_id=1, source_target_pairs={{0,32},{32,64},{64,96},{96,128},{128,160},{160,192},{192,224},{224... | collective-permute-start | bytes 417800 | tf_op jit(solution)/shard_map/ppermute | solution.py:23
  225.6 36.1 %collective-permute-start.11 = (f32[136,256]{1,0:T(8,128)S(1)}, f32[136,256]{1,0:T(8,128)S(1)}, u32[]{:S(2)}, u32[]{:S(2)}) collective-permute-start(f32[136,256]{1,0:T(8,128)S(1)} %pad_maximum_fusion.4), channel_id=1, source_target_pairs={{0,64},{32,96},{64,128},{96,160},{128,192},{160,224},{192,256},{22... | collective-permute-start | bytes 417800 | tf_op jit(solution)/shard_map/ppermute | solution.py:23
  232.5 31.6 %collective-permute-start.12 = (f32[136,256]{1,0:T(8,128)S(1)}, f32[136,256]{1,0:T(8,128)S(1)}, u32[]{:S(2)}, u32[]{:S(2)}) collective-permute-start(f32[136,256]{1,0:T(8,128)S(1)} %pad_maximum_fusion.4), channel_id=1, source_target_pairs={{0,96},{32,128},{64,160},{96,192},{128,224},{160,256},{192,288},{2... | collective-permute-start | bytes 417800 | tf_op jit(solution)/shard_map/ppermute | solution.py:23
  234.7 53.5 %copy-start.7 = (f32[4,256,256]{1,2,0:T(8,128)S(1)}, f32[4,256,256]{1,2,0:T(8,128)}, u32[]{:S(2)}) copy-start(f32[4,256,256]{1,2,0:T(8,128)} %get-tuple-element.70) | copy-start | bytes 3145732
  234.7 53.5 %copy-start.9 = (bf16[1024,256]{0,1:T(8,128)(2,1)S(1)}, bf16[1024,256]{0,1:T(8,128)(2,1)}, u32[]{:S(2)}) copy-start(bf16[1024,256]{0,1:T(8,128)(2,1)} %fusion.21) | copy-start | bytes 1572868
  264.2 7.9 %collective-permute-start.13 = (f32[136,256]{1,0:T(8,128)S(1)}, f32[136,256]{1,0:T(8,128)S(1)}, u32[]{:S(2)}, u32[]{:S(2)}) collective-permute-start(f32[136,256]{1,0:T(8,128)S(1)} %pad_maximum_fusion.5), channel_id=1, source_target_pairs={{0,32},{32,64},{64,96},{96,128},{128,160},{160,192},{192,224},{224... | collective-permute-start | bytes 417800 | tf_op jit(solution)/shard_map/ppermute | solution.py:23
  269.3 17.4 %collective-permute-start.14 = (f32[136,256]{1,0:T(8,128)S(1)}, f32[136,256]{1,0:T(8,128)S(1)}, u32[]{:S(2)}, u32[]{:S(2)}) collective-permute-start(f32[136,256]{1,0:T(8,128)S(1)} %pad_maximum_fusion.5), channel_id=1, source_target_pairs={{0,160},{32,192},{64,224},{96,256},{128,288},{160,320},{192,352},{... | collective-permute-start | bytes 417800 | tf_op jit(solution)/shard_map/ppermute | solution.py:23
  (3 other events, 12.8 us)
Sparse Core Ops, SparseCore 0:
  30.7 56.6 all-gather.6
  89.6 69.2 all-gather.4

commit v2 on v1

v2 whole, which is shorter than its diff:
```python
import functools

import jax
import jax.numpy as jnp
from jax import lax
from jax.experimental import pallas as pl
from jax.experimental.pallas import tpu as pltpu
from jax.sharding import Mesh
from jax.sharding import PartitionSpec as P

HEADS = 128
GROUPS = 8
BLOCK = 256
STATE = 128
WIDTH = 64
YH, Z, X, Y, C = 2, 8, 4, 4, 2
SEQ = ("yh", "z")
HEAD = ("x", "y", "c")
F32 = jnp.float32
BF16 = jnp.bfloat16
MIB = 1024 * 1024
FAR = -1e30


def ring(count, step):
    return [(i, (i + step) % count) for i in range(count)]


def along_seq(value, step):
    return lax.ppermute(value, SEQ, [(i, i + step) for i in range(YH * Z - step)])


def ring_gather(block):
    pieces = [(0, 0, block)]
    right = left = block
    for step in range(1, 4):
        right = lax.ppermute(right, "z", ring(Z, 1))
        left = lax.ppermute(left, "z", ring(Z, -1))
        pieces += [(Z - step, 0, right), (step, 0, left)]
    right = lax.ppermute(right[:1], "z", ring(Z, 1))
    left = lax.ppermute(left[1:], "z", ring(Z, -1))
    return pieces + [(4, 0, right), (4, 1, left)]


def call(
    kernel, grid, in_specs, out_specs, out_shape, scratch=(), prefetch=0, cost=None, room=12
):
    return pl.pallas_call(
        kernel,
        grid_spec=pltpu.PrefetchScalarGridSpec(
            num_scalar_prefetch=prefetch,
            grid=grid,
            in_specs=in_specs,
            out_specs=out_specs,
            scratch_shapes=scratch,
        ),
        out_shape=out_shape,
        compiler_params=pltpu.CompilerParams(
            vmem_limit_bytes=room * MIB, dimension_semantics=("arbitrary",) * len(grid)
        ),
        cost_estimate=cost,
    )


def whole(shape):
    return pl.BlockSpec(shape, lambda *_: (0,) * len(shape))


def rows_of(shape):
    return pl.BlockSpec(shape, lambda i, *_: (i,) + (0,) * (len(shape) - 1))


def assemble_kernel(layout, scalars, *refs):
    count = len(layout)
    pieces, swapped, out = refs[:count], refs[count : 2 * count], refs[2 * count]
    z, core = scalars[0], scalars[1]
    for (offset, first, yh_count), piece, other in zip(layout, pieces, swapped):
        source = lax.rem(z + offset, Z)
        for local_yh in range(yh_count):
            start = pl.multiple_of(((first + local_yh) * Z + source) * 256, 256)
            out[pl.ds(start, 256), 0:256] = piece[local_yh, 0:256, :]
            own = pl.multiple_of(start + core * 128, 128)
            its = pl.multiple_of(start + (1 - core) * 128, 128)
            out[pl.ds(own, 128), 256:512] = piece[local_yh, 256:384, :]
            out[pl.ds(its, 128), 256:512] = other[local_yh, :, :]
            steps = piece[local_yh, 384:392, :].astype(F32).T
            steps = jnp.concatenate([steps, jnp.zeros((256, 120), F32)], axis=1)
            out[pl.ds(start, 256), 512:640] = steps.astype(BF16)


def project_kernel(tok_ref, w_ref, out_ref):
    out_ref[...] = jnp.dot(
        tok_ref[...], w_ref[...], preferred_element_type=F32
    ).astype(BF16)


def gate_kernel(tok_ref, w_ref, out_ref):
    weights = jnp.concatenate([w_ref[z, yh] for yh in range(YH) for z in range(Z)], axis=0)
    proj = jnp.dot(tok_ref[...], weights, preferred_element_type=F32).astype(BF16)
    out_ref[...] = jax.nn.silu(proj.astype(F32))


def spread(columns):
    rows = columns.shape[0]
    lane = lax.broadcasted_iota(jnp.int32, (rows, 128), 1)
    wide = [jnp.broadcast_to(columns[:, h : h + 1], (rows, 128)) for h in range(4)]
    return jnp.concatenate(
        [jnp.where(lane < WIDTH, wide[0], wide[1]), jnp.where(lane < WIDTH, wide[2], wide[3])],
        axis=1,
    )


def doc_start(starts, positions):
    found = jnp.zeros(positions.shape, jnp.int32)
    for j in range(16):
        found = jnp.where(starts[j] <= positions, starts[j], found)
    return found


def state_kernel(
    starts, base, proj_ref, rim_ref, taps_ref, small_ref,
    act_ref, cum_ref, step_ref, inside_ref, gain_ref, packed_ref,
    ext, running, gains,
):
    block = pl.program_id(0)
    first = base[0] + block * BLOCK

    @pl.when(block == 0)
    def _():
        ext[0:8, :] = rim_ref[...].astype(F32)
        running[...] = jnp.zeros_like(running)
        gains[...] = jnp.ones_like(gains)

    proj = proj_ref[...]
    tile = proj[:, 0:512].astype(F32)
    ext[8 : 8 + BLOCK, :] = tile
    positions = first + lax.broadcasted_iota(jnp.int32, (BLOCK, 128), 0)
    start = doc_start(starts, positions)
    depth = (positions - start)[:, 0:1]
    summed = taps_ref[3:4, :] * tile
    for lag in (1, 2, 3):
        window = ext[8 - lag : 8 - lag + BLOCK, :]
        summed = summed + jnp.where(depth >= lag, taps_ref[3 - lag : 4 - lag, :] * window, 0.0)
    act = jax.nn.silu(summed).astype(BF16)
    act_ref[...] = act
    ext[0:8, :] = tile[BLOCK - 8 :, :]

    step = jax.nn.softplus(proj[:, 512:640].astype(F32) + small_ref[0:1, :])
    decay = -jnp.exp(small_ref[1:2, :]) * step
    tri = (
        lax.broadcasted_iota(jnp.int32, (BLOCK, BLOCK), 1)
        <= lax.broadcasted_iota(jnp.int32, (BLOCK, BLOCK), 0)
    ).astype(F32)
    cumulative = jnp.dot(
        tri, decay, preferred_element_type=F32, precision=lax.Precision.HIGHEST
    )
    cum_ref[...] = cumulative
    step_ref[...] = step
    ending = cumulative[BLOCK - 1 : BLOCK, :]
    last_start = start[BLOCK - 1 : BLOCK, :]
    trailing = jnp.where(positions >= last_start, jnp.exp(ending - cumulative) * step, 0.0)
    weighted = (spread(trailing) * act[:, 0:256].astype(F32)).astype(BF16)
    local_state = lax.dot_general(
        act[:, 256:384], weighted, (((0,), (0,)), ((), ())), preferred_element_type=F32
    )
    factor = jnp.where(last_start < first, jnp.exp(ending), 0.0)
    factor = spread(jnp.broadcast_to(factor, (8, 128)))
    inside_ref[0] = running[...]
    gain_ref[0] = gains[...]
    running[...] = factor[0:1, :] * running[...] + local_state
    gains[...] = gains[...] * factor

    @pl.when(block == pl.num_programs(0) - 1)
    def _():
        packed_ref[0:STATE, :] = running[...].astype(BF16)
        high = gains[...].astype(BF16)
        low = (gains[...] - high.astype(F32)).astype(BF16)
        packed_ref[STATE : STATE + 16, :] = jnp.concatenate([high, low], axis=0)


def block_kernel(
    starts, base, act_ref, cum_ref, step_ref, inside_ref, gain_ref, y_ref, reach_ref
):
    first = base[0] + pl.program_id(0) * BLOCK
    act = act_ref[...]
    x_act, b_act, c_act = act[:, 0:256], act[:, 256:384], act[:, 384:512]
    cumulative = cum_ref[...]
    cum_rows, step_rows = cumulative.T, step_ref[...].T
    products = lax.dot_general(
        c_act, b_act, (((1,), (1,)), ((), ())), preferred_element_type=F32
    )
    start = doc_start(starts, first + lax.broadcasted_iota(jnp.int32, (BLOCK, 128), 0))
    row = lax.broadcasted_iota(jnp.int32, (BLOCK, BLOCK), 0)
    column = lax.broadcasted_iota(jnp.int32, (BLOCK, BLOCK), 1)
    allowed = (column <= row) & (first + column >= start[:, 0:1])
    parts = []
    for h in range(4):
        gap = cumulative[:, h : h + 1] - cum_rows[h : h + 1, :]
        decay = jnp.exp(jnp.where(allowed, gap, FAR))
        scores = (products * decay * step_rows[h : h + 1, :]).astype(BF16)
        parts.append(
            jnp.dot(scores, x_act[:, h * WIDTH : (h + 1) * WIDTH], preferred_element_type=F32)
        )
    y_inner = jnp.concatenate(parts, axis=1)
    reach = spread(jnp.where(start < first, jnp.exp(cumulative), 0.0))
    inside = inside_ref[0]
    high = inside.astype(BF16)
    low = (inside - high.astype(F32)).astype(BF16)
    carried = jnp.dot(c_act, high, preferred_element_type=F32) + jnp.dot(
        c_act, low, preferred_element_type=F32
    )
    y_ref[...] = y_inner + reach * carried + x_act.astype(F32)
    reach_ref[...] = reach * gain_ref[0, 0:1, :]


def gain_of(packed):
    return packed[STATE : STATE + 8].astype(F32) + packed[STATE + 8 : STATE + 16].astype(F32)


def near_kernel(own_ref, one_ref, two_ref, three_ref, out_ref):
    own = own_ref[...]
    total, gain = own[0:STATE].astype(F32), gain_of(own)
    for ref in (one_ref, two_ref, three_ref):
        piece = ref[...]
        total = total + gain[0:1] * piece[0:STATE].astype(F32)
        gain = gain * gain_of(piece)
    high = gain.astype(BF16)
    low = (gain - high.astype(F32)).astype(BF16)
    out_ref[0:STATE, :] = total.astype(BF16)
    out_ref[STATE : STATE + 16, :] = jnp.concatenate([high, low], axis=0)


def finish_kernel(first_ref, second_ref, act_ref, y_ref, reach_ref, gate_ref, out_ref):
    first, second = first_ref[...], second_ref[...]
    gain = gain_of(first)[0:1]
    entering = first[0:STATE].astype(F32) + gain * second[0:STATE].astype(F32)
    carried = jnp.dot(act_ref[...], entering.astype(BF16), preferred_element_type=F32)
    out_ref[...] = ((y_ref[...] + reach_ref[...] * carried) * gate_ref[...]).astype(BF16)


def shape(dims, dtype):
    return jax.ShapeDtypeStruct(dims, dtype)


def work(flops, moved, exps=0):
    return pl.CostEstimate(flops=flops, bytes_accessed=moved, transcendentals=exps)


def run_assemble(pieces, swapped, scalars):
    layout = tuple((offset, first, piece.shape[0]) for offset, first, piece in pieces)
    arrays = [piece for _, _, piece in pieces]
    return call(
        functools.partial(assemble_kernel, layout),
        (1,),
        [whole(a.shape) for a in arrays] + [whole(a.shape) for a in swapped],
        whole((4096, 640)),
        shape((4096, 640), BF16),
        prefetch=1,
        cost=work(0, 12 << 20),
        room=24,
    )(scalars, *arrays, *swapped)


def run_project(gathered, weights):
    rows, depth = gathered.shape
    cols = weights.shape[1]
    return call(
        project_kernel,
        (rows // 256,),
        [rows_of((256, depth)), whole((depth, cols))],
        rows_of((256, cols)),
        shape((rows, cols), BF16),
        cost=work(2 * rows * depth * cols, 14 << 20),
        room=48,
    )(gathered, weights)


def run_gate(gathered, gate_all):
    rows, depth = gathered.shape
    return call(
        gate_kernel,
        (rows // 256,),
        [rows_of((256, depth)), whole(gate_all.shape)],
        rows_of((256, 256)),
        shape((rows, 256), F32),
        cost=work(2 * rows * depth * 256, 11 << 20),
        room=48,
    )(gathered, gate_all)


def run_state(starts, base, proj, rim, taps, small):
    rows = proj.shape[0]
    blocks = rows // BLOCK
    return call(
        state_kernel,
        (blocks,),
        [rows_of((BLOCK, 640)), whole((8, 512)), whole((4, 512)), whole((8, 128))],
        [
            rows_of((BLOCK, 512)),
            rows_of((BLOCK, 128)),
            rows_of((BLOCK, 128)),
            rows_of((1, STATE, 256)),
            rows_of((1, 8, 256)),
            whole((STATE + 16, 256)),
        ],
        [
            shape((rows, 512), BF16),
            shape((rows, 128), F32),
            shape((rows, 128), F32),
            shape((blocks, STATE, 256), F32),
            shape((blocks, 8, 256), F32),
            shape((STATE + 16, 256), BF16),
        ],
        scratch=[
            pltpu.VMEM((8 + BLOCK, 512), F32),
            pltpu.VMEM((STATE, 256), F32),
            pltpu.VMEM((8, 256), F32),
        ],
        prefetch=2,
        cost=work(2 * rows * 128 * 256, 4 << 20, rows * 1024),
    )(starts, base, proj, rim, taps, small)


def run_blocks(starts, base, act, cum, step, inside, gains):
    rows = act.shape[0]
    blocks = rows // BLOCK
    return call(
        block_kernel,
        (blocks,),
        [
            rows_of((BLOCK, 512)),
            rows_of((BLOCK, 128)),
            rows_of((BLOCK, 128)),
            rows_of((1, STATE, 256)),
            rows_of((1, 8, 256)),
        ],
        [rows_of((BLOCK, 256)), rows_of((BLOCK, 256))],
        [shape((rows, 256), F32), shape((rows, 256), F32)],
        prefetch=2,
        cost=work(2 * rows * 256 * 1024, 5 << 20, rows * 1280),
    )(starts, base, act, cum, step, inside, gains)


def run_near(pieces):
    return call(
        near_kernel,
        (1,),
        [whole(p.shape) for p in pieces],
        whole(pieces[0].shape),
        shape(pieces[0].shape, BF16),
        cost=work(1 << 18, 1 << 19),
    )(*pieces)


def run_finish(first, second, act, y, reach, gate):
    rows = y.shape[0]
    return call(
        finish_kernel,
        (rows // BLOCK,),
        [
            whole(first.shape),
            whole(second.shape),
            pl.BlockSpec((BLOCK, 128), lambda i: (i, 3)),
            rows_of((BLOCK, 256)),
            rows_of((BLOCK, 256)),
            rows_of((BLOCK, 256)),
        ],
        rows_of((BLOCK, 256)),
        shape((rows, 256), BF16),
        cost=work(2 * rows * 128 * 256, 4 << 20),
    )(first, second, act, y, reach, gate)


def local(
    tokens,
    doc_lengths,
    value_weight,
    gate_weight,
    state_weight,
    step_weight,
    value_conv,
    state_conv,
    step_bias,
    log_rate,
):
    tok_dev = tokens.shape[0] * X * Y * C
    heads_here = step_weight.shape[1]
    core = lax.axis_index("c")
    z = lax.axis_index("z")
    group = lax.axis_index("x") * 2 + lax.axis_index("y") // 2
    gathered = lax.all_gather(tokens, HEAD, axis=0, tiled=True)

    state_half = lax.dynamic_slice(state_weight, (group, core * 128, 0), (1, 128, 256))[0]
    conv_own = lax.dynamic_index_in_dim(state_conv, group, 0, keepdims=False)
    step_rows = jnp.pad(step_weight.T, ((0, 8 - heads_here), (0, 0)))
    pack = jnp.concatenate([value_weight, state_half, step_rows, gate_weight], axis=0)
    both = lax.all_gather(pack, "yh", axis=0, tiled=False)
    pieces = ring_gather(both[:, :392])
    halves = jnp.concatenate([piece[:, 256:384] for _, _, piece in pieces], axis=0)
    halves = lax.ppermute(halves, "c", [(0, 1), (1, 0)])
    swapped, at = [], 0
    for _, _, piece in pieces:
        swapped.append(halves[at : at + piece.shape[0]])
        at += piece.shape[0]
    scalars = jnp.stack([z, core]).astype(jnp.int32)
    weights = run_assemble(pieces, swapped, scalars)
    gate_part, gathered, weights = lax.optimization_barrier((both[:, 392:], gathered, weights))
    gate_all = lax.all_gather(gate_part, "z", axis=0, tiled=False)
    proj = run_project(gathered, weights)
    rim = along_seq(proj[-8:, :512], 1)

    starts = (jnp.cumsum(doc_lengths) - doc_lengths).astype(jnp.int32)
    base = (lax.axis_index(SEQ) * tok_dev).astype(jnp.int32).reshape(1)
    taps = jnp.concatenate([value_conv, conv_own], axis=1)
    small = jnp.pad(jnp.stack([step_bias, log_rate]), ((0, 6), (0, 128 - heads_here)))
    act, cum, step, inside, gains, packed = run_state(starts, base, proj, rim, taps, small)
    near = run_near([packed] + [along_seq(packed, hop) for hop in (1, 2, 3)])
    y, reach = run_blocks(starts, base, act, cum, step, inside, gains)
    first, second = along_seq(near, 1), along_seq(near, 5)
    gate = run_gate(gathered, gate_all)
    return run_finish(first, second, act, y, reach, gate)


def solution(mesh):
    grid = Mesh(mesh.devices.reshape(YH, Z, X, Y, C), SEQ + HEAD)
    return jax.shard_map(
        local,
        mesh=grid,
        in_specs=(
            P(SEQ + HEAD, None),
            P(),
            P(SEQ, HEAD),
            P(SEQ, HEAD),
            P(None, SEQ, None),
            P(SEQ, HEAD),
            P(None, HEAD),
            P(),
            P(HEAD),
            P(HEAD),
        ),
        out_specs=P(SEQ, HEAD),
        check_vma=False,
    )
```

time: 298 us -> 180 us (0.60)
  waiting for transfers between devices: 120 us -> 34.4 us
  Pallas kernels: 0 us -> 28.6 us
  matrix products: 24.7 us -> 0 us
  other arithmetic: 17.4 us -> 1.26 us
  local copies, waits for them, and re-layouts: 35.8 us -> 21.7 us
  loops' own time: 5.8 us -> 0 us
    all_gather x1, waiting for transfers between devices: 49.4 us -> 0.01 us  [local(): gathered = lax.all_gather(tokens, HEAD, axis=0, tiled=True)]
    pallas_call x0 -> x7, Pallas kernels: none -> 28.6 us  [the longest x1 10.4 us: run_project(): call(project_kernel, (rows // 256,), [rows_of((256, depth)), whole((depth...]
    ppermute x6, waiting for transfers between devices: 46.3 us -> 19.1 us  [along_seq(): lax.ppermute(value, SEQ, [(i, i + step) for i in range(YH * Z - step)])]
    dot_general x20 -> x0, matrix products: 24.7 us -> none  [the longest x1 6.43 us: local(): jnp.dot(gathered, state_all, preferred_element_type=F32).astype(BF16)]
    unnamed x20 -> x42, local copies, waits for them, and re-layouts: 1.19 us -> 17.3 us
    dynamic_update_slice x17 -> x0, local copies, waits for them, and re-layouts: 12.6 us -> none  [the longest x9 9.48 us: put(): lax.dynamic_update_slice(held, piece[None], ((z + offset) % Z, 0, row, 0))]
    ppermute x3, waiting for transfers between devices: 20.9 us -> 11.4 us  [ring_gather(): right = lax.ppermute(right, 'z', ring(Z, 1))]
    slice x32 -> x7, local copies, waits for them, and re-layouts: 9.6 us -> 2.95 us  [the longest x2 2.19 us: local(): swapped.append(halves[at:at + piece.shape[0]])]
  transfers between devices with their start and end apart: 17 -> 17, of which waited for: 13 -> 11; matrix products, arithmetic and copies ran while one was open for 11% -> 6% of each run, Pallas kernels for 0% -> 15%
where the time goes in v2:
time: 180 us
  starting transfers between devices  58.7 us (33%)
  waiting for transfers between devices  34.4 us (19%)
  Pallas kernels  28.6 us (16%)
  local copies, waits for them, and re-layouts  21.7 us (12%)
  blocking collectives  21.1 us (12%)
  between operations  13.8 us (8%)
    ppermute x6, starting transfers between devices, along_seq(): lax.ppermute(value, SEQ, [(i, i + step) for i in range(YH * Z - step)])  23.5 us
    all_gather x1, blocking collectives, local(): both = lax.all_gather(pack, 'yh', axis=0, tiled=False)  21.1 us
    ppermute x6, waiting for transfers between devices, along_seq(): lax.ppermute(value, SEQ, [(i, i + step) for i in range(YH * Z - step)])  19.1 us
    unnamed x42, local copies, waits for them, and re-layouts  17.3 us
    ppermute x3, starting transfers between devices, ring_gather(): left = lax.ppermute(left, 'z', ring(Z, -1))  15.5 us
    ppermute x3, waiting for transfers between devices, ring_gather(): right = lax.ppermute(right, 'z', ring(Z, 1))  11.4 us
    ppermute x3, starting transfers between devices, ring_gather(): right = lax.ppermute(right, 'z', ring(Z, 1))  11 us
    pallas_call x1, Pallas kernels, run_project(): call(project_kernel, (rows // 256,), [rows_of((256, depth)), whole((depth...  10.4 us
  transfers between devices with their start and end apart: 17, of which 11 were waited for; matrix products, arithmetic and copies ran while one was open for 6% of the time, Pallas kernels for 15%

profile of v2, /device:TPU:112, one launch (start us, length us, event | category | flops | bytes accessed | tf_op | source)
XLA Modules:
  0.0 179.5 jit_solution(7583679362547587882)
XLA Ops:
  8.8 21.1 %all-gather = bf16[1296,256]{1,0:T(8,128)(2,1)S(1)} all-gather(bf16[648,256]{1,0:T(8,128)(2,1)S(1)} %fusion.3), channel_id=2, replica_groups=mesh['yh'=2,'z'=8,'x'=4,'y'=4,'c'=2] {'yh'}, dimensions={0}, use_global_device_ids=true | all-gather | bytes 995328 | tf_op jit(solution)/shard_map/all_gather | solution.py:397
  29.9 4.8 %collective-permute-start = (bf16[2,392,256]{2,1,0:T(8,128)(2,1)S(1)}, bf16[2,392,256]{2,1,0:T(8,128)(2,1)S(1)}, u32[]{:S(2)}, u32[]{:S(2)}) collective-permute-start(bf16[2,392,256]{2,1,0:T(8,128)(2,1)S(1)} %slice.94.refs_0_), channel_id=1, source_target_pairs={{0,32},{32,64},{64,96},{96,128},{128,160},{160,192},{192,224},{224... | collective-permute-start | bytes 1204232 | tf_op jit(solution)/shard_map/ppermute | solution.py:37
  37.3 4.6 %collective-permute-done.refs_1_ = bf16[2,392,256]{2,1,0:T(8,128)(2,1)S(1)} collective-permute-done((bf16[2,392,256]{2,1,0:T(8,128)(2,1)S(1)}, bf16[2,392,256]{2,1,0:T(8,128)(2,1)S(1)}, u32[]{:S(2)}, u32[]{:S(2)}) %collective-permute-start) | collective-permute-done | bytes 401440 | tf_op jit(solution)/shard_map/ppermute | solution.py:37
  41.9 4.3 %collective-permute-start.2 = (bf16[2,392,256]{2,1,0:T(8,128)(2,1)S(1)}, bf16[2,392,256]{2,1,0:T(8,128)(2,1)S(1)}, u32[]{:S(2)}, u32[]{:S(2)}) collective-permute-start(bf16[2,392,256]{2,1,0:T(8,128)(2,1)S(1)} %collective-permute-done.refs_1_), channel_id=1, source_target_pairs={{0,32},{32,64},{64,96},{96,128},{128,160},{160,192},{192,224},{224... | collective-permute-start | bytes 1204232 | tf_op jit(solution)/shard_map/ppermute | solution.py:37
  46.5 8.7 %collective-permute-start.3 = (bf16[2,392,256]{2,1,0:T(8,128)(2,1)S(1)}, bf16[2,392,256]{2,1,0:T(8,128)(2,1)S(1)}, u32[]{:S(2)}, u32[]{:S(2)}) collective-permute-start(bf16[2,392,256]{2,1,0:T(8,128)(2,1)S(1)} %collective-permute-done.1.refs_2_), channel_id=1, source_target_pairs={{0,224},{32,0},{64,32},{96,64},{128,96},{160,128},{192,160},{224,1... | collective-permute-start | bytes 1204232 | tf_op jit(solution)/shard_map/ppermute | solution.py:38
  56.5 3.9 %collective-permute-done.2.refs_3_ = bf16[2,392,256]{2,1,0:T(8,128)(2,1)S(1)} collective-permute-done((bf16[2,392,256]{2,1,0:T(8,128)(2,1)S(1)}, bf16[2,392,256]{2,1,0:T(8,128)(2,1)S(1)}, u32[]{:S(2)}, u32[]{:S(2)}) %collective-permute-start.2) | collective-permute-done | bytes 401440 | tf_op jit(solution)/shard_map/ppermute | solution.py:37
  62.4 4.9 %collective-permute-start.5 = (bf16[2,392,256]{2,1,0:T(8,128)(2,1)S(1)}, bf16[2,392,256]{2,1,0:T(8,128)(2,1)S(1)}, u32[]{:S(2)}, u32[]{:S(2)}) collective-permute-start(bf16[2,392,256]{2,1,0:T(8,128)(2,1)S(1)} %collective-permute-done.3.refs_4_), channel_id=1, source_target_pairs={{0,224},{32,0},{64,32},{96,64},{128,96},{160,128},{192,160},{224,1... | collective-permute-start | bytes 1204232 | tf_op jit(solution)/shard_map/ppermute | solution.py:38
  68.6 3.0 %collective-permute-done.4.refs_5_ = bf16[2,392,256]{2,1,0:T(8,128)(2,1)S(1)} collective-permute-done((bf16[2,392,256]{2,1,0:T(8,128)(2,1)S(1)}, bf16[2,392,256]{2,1,0:T(8,128)(2,1)S(1)}, u32[]{:S(2)}, u32[]{:S(2)}) %collective-permute-start.4) | collective-permute-done | bytes 401440 | tf_op jit(solution)/shard_map/ppermute | solution.py:37
  73.5 4.9 %collective-permute-start.7 = (bf16[1,392,256]{2,1,0:T(8,128)(2,1)S(1)}, bf16[1,392,256]{2,1,0:T(8,128)(2,1)S(1)}, u32[]{:S(2)}, u32[]{:S(2)}) collective-permute-start(bf16[1,392,256]{2,1,0:T(8,128)(2,1)S(1)} %slice.96), channel_id=1, source_target_pairs={{0,224},{32,0},{64,32},{96,64},{128,96},{160,128},{192,160},{224,1... | collective-permute-start | bytes 602120 | tf_op jit(solution)/shard_map/ppermute | solution.py:41
  85.6 2.2 %collective-permute-done.8 = bf16[16,128,256]{2,1,0:T(8,128)(2,1)} collective-permute-done((bf16[16,128,256]{2,1,0:T(8,128)(2,1)}, bf16[16,128,256]{2,1,0:T(8,128)(2,1)}, u32[]{:S(2)}, u32[]{:S(2)}) %collective-permute-start.8) | collective-permute-done | bytes 1048608 | tf_op jit(solution)/shard_map/ppermute | solution.py:400
  94.1 2.4 %copy-done.1 = bf16[4096,640]{1,0:T(8,128)(2,1)} copy-done((bf16[4096,640]{1,0:T(8,128)(2,1)}, bf16[4096,640]{1,0:T(8,128)(2,1)S(1)}, u32[]{:S(2)}) %copy-start.1) | copy-done | bytes 5242904
  97.3 10.4 %shard_map.101.proj_ref = bf16[1024,640]{1,0:T(8,128)(2,1)S(1)} custom-call(bf16[1024,4096]{1,0:T(8,128)(2,1)} %all-gather.5.cloned.1.call-done.tok_ref, bf16[4096,640]{1,0:T(8,128)(2,1)} %copy-done.1), custom_call_target="tpu_custom_call" | custom-call | flops 5368709120 | bytes 14680064 | tf_op jit(solution)/shard_map/pallas_call | solution.py:267
  108.8 3.6 %collective-permute-start.9 = (bf16[8,512]{1,0:T(8,128)(2,1)S(1)}, bf16[8,512]{1,0:T(8,128)(2,1)S(1)}, u32[]{:S(2)}, u32[]{:S(2)}) collective-permute-start(bf16[8,512]{1,0:T(8,128)(2,1)S(1)} %slice.115), channel_id=1, source_target_pairs={{0,32},{32,64},{64,96},{96,128},{128,160},{160,192},{192,224},{224... | collective-permute-start | bytes 24584 | tf_op jit(solution)/shard_map/ppermute | solution.py:30
  112.7 2.9 %collective-permute-done.9.rim_ref = bf16[8,512]{1,0:T(8,128)(2,1)S(1)} collective-permute-done((bf16[8,512]{1,0:T(8,128)(2,1)S(1)}, bf16[8,512]{1,0:T(8,128)(2,1)S(1)}, u32[]{:S(2)}, u32[]{:S(2)}) %collective-permute-start.9) | collective-permute-done | bytes 8224 | tf_op jit(solution)/shard_map/ppermute | solution.py:30
  116.9 5.6 %shard_map.102 = (bf16[1024,512]{1,0:T(8,128)(2,1)S(1)}, f32[1024,128]{1,0:T(8,128)S(1)}, f32[1024,128]{1,0:T(8,128)S(1)}, f32[4,128,256]{2,1,0:T(8,128)S(1)}, f...) custom-call(s32[16]{0:T(128)S(1)} %sub.7.starts, s32[1]{0:T(128)} %bitcast.1.base, ...), custom_call_target="tpu_custom_call" | custom-call | flops 67108864 | bytes 4194304 | tf_op jit(solution)/shard_map/pallas_call | solution.py:294
  122.5 3.3 %collective-permute-start.10 = (bf16[144,256]{1,0:T(8,128)(2,1)S(1)}, bf16[144,256]{1,0:T(8,128)(2,1)S(1)}, u32[]{:S(2)}, u32[]{:S(2)}) collective-permute-start(bf16[144,256]{1,0:T(8,128)(2,1)S(1)} %get-tuple-element.18.own_ref), channel_id=1, source_target_pairs={{0,32},{32,64},{64,96},{96,128},{128,160},{160,192},{192,224},{224... | collective-permute-start | bytes 221192 | tf_op jit(solution)/shard_map/ppermute | solution.py:30
  125.8 4.9 %collective-permute-start.11 = (bf16[144,256]{1,0:T(8,128)(2,1)S(1)}, bf16[144,256]{1,0:T(8,128)(2,1)S(1)}, u32[]{:S(2)}, u32[]{:S(2)}) collective-permute-start(bf16[144,256]{1,0:T(8,128)(2,1)S(1)} %get-tuple-element.18.own_ref), channel_id=1, source_target_pairs={{0,64},{32,96},{64,128},{96,160},{128,192},{160,224},{192,256},{22... | collective-permute-start | bytes 221192 | tf_op jit(solution)/shard_map/ppermute | solution.py:30
  130.6 5.6 %collective-permute-start.12 = (bf16[144,256]{1,0:T(8,128)(2,1)S(1)}, bf16[144,256]{1,0:T(8,128)(2,1)S(1)}, u32[]{:S(2)}, u32[]{:S(2)}) collective-permute-start(bf16[144,256]{1,0:T(8,128)(2,1)S(1)} %get-tuple-element.18.own_ref), channel_id=1, source_target_pairs={{0,96},{32,128},{64,160},{96,192},{128,224},{160,256},{192,288},{2... | collective-permute-start | bytes 221192 | tf_op jit(solution)/shard_map/ppermute | solution.py:30
  136.2 3.8 %shard_map.104 = (f32[1024,256]{1,0:T(8,128)S(1)}, f32[1024,256]{1,0:T(8,128)S(1)}) custom-call(s32[16]{0:T(128)S(1)} %sub.7.starts, s32[1]{0:T(128)} %bitcast.1.base, bf16[1024,512]{1,0:T(8,128)(2,1)S(1)} %get-tuple-element.19.act_ref, f32[1024,128]{1,0:T(8,128)S(1)} %get-tuple-element.20.cum_ref, f32[1024,128]{1,0:T(8,128)S(1)} %get-tuple-element.21.step_ref, ...), custom_call_target="tpu_custom_call" | custom-call | flops 536870912 | bytes 5242880 | tf_op jit(solution)/shard_map/pallas_call | solution.py:327
  141.0 9.2 %collective-permute-done.11.two_ref = bf16[144,256]{1,0:T(8,128)(2,1)S(1)} collective-permute-done((bf16[144,256]{1,0:T(8,128)(2,1)S(1)}, bf16[144,256]{1,0:T(8,128)(2,1)S(1)}, u32[]{:S(2)}, u32[]{:S(2)}) %collective-permute-start.11) | collective-permute-done | bytes 73760 | tf_op jit(solution)/shard_map/ppermute | solution.py:30
  151.6 4.2 %collective-permute-start.13 = (bf16[144,256]{1,0:T(8,128)(2,1)S(1)}, bf16[144,256]{1,0:T(8,128)(2,1)S(1)}, u32[]{:S(2)}, u32[]{:S(2)}) collective-permute-start(bf16[144,256]{1,0:T(8,128)(2,1)S(1)} %shard_map.103), channel_id=1, source_target_pairs={{0,32},{32,64},{64,96},{96,128},{128,160},{160,192},{192,224},{224... | collective-permute-start | bytes 221192 | tf_op jit(solution)/shard_map/ppermute | solution.py:30
  159.4 5.6 %shard_map.105.gate_ref = f32[1024,256]{1,0:T(8,128)S(1)} custom-call(bf16[1024,4096]{1,0:T(8,128)(2,1)} %all-gather.5.cloned.1.call-done.tok_ref, bf16[8,2,256,256]{3,2,1,0:T(8,128)(2,1)S(1)} %bitcast.13), custom_call_target="tpu_custom_call" | custom-call | flops 2147483648 | bytes 11534336 | tf_op jit(solution)/shard_map/pallas_call | solution.py:280
  165.0 5.7 %collective-permute-done.14.second_ref = bf16[144,256]{1,0:T(8,128)(2,1)S(1)} collective-permute-done((bf16[144,256]{1,0:T(8,128)(2,1)S(1)}, bf16[144,256]{1,0:T(8,128)(2,1)S(1)}, u32[]{:S(2)}, u32[]{:S(2)}) %collective-permute-start.14) | collective-permute-done | bytes 73760 | tf_op jit(solution)/shard_map/ppermute | solution.py:30
  170.7 1.9 %shard_map.106 = bf16[1024,256]{1,0:T(8,128)(2,1)} custom-call(bf16[144,256]{1,0:T(8,128)(2,1)S(1)} %collective-permute-done.13.first_ref, bf16[144,256]{1,0:T(8,128)(2,1)S(1)} %collective-permute-done.14.second_ref, bf16[1024,512]{1,0:T(8,128)(2,1)S(1)} %get-tuple-element.19.act_ref, f32[1024,256]{1,0:T(8,128)S(1)} %get-tuple-element.24.y_ref, ...), custom_call_target="tpu_custom_call" | custom-call | flops 67108864 | bytes 4194304 | tf_op jit(solution)/shard_map/pallas_call | solution.py:357
  (80 shorter events, 34.5 us)
Async XLA Ops:
  6.5 90.0 %all-gather.5.cloned.1.call-start = ((), (), s32[]{:S(2)}) async-start(), calls=%async_computation | async-start | bytes 8650752 | tf_op jit(solution)/shard_map/all_gather | solution.py:391
  7.3 150.5 %all-gather.7.cloned.1.call-start = ((), (), s32[]{:S(2)}) async-start(), calls=%async_computation.1 | async-start | bytes 2359296 | tf_op jit(solution)/shard_map/all_gather | solution.py:408
  29.9 12.0 %collective-permute-start = (bf16[2,392,256]{2,1,0:T(8,128)(2,1)S(1)}, bf16[2,392,256]{2,1,0:T(8,128)(2,1)S(1)}, u32[]{:S(2)}, u32[]{:S(2)}) collective-permute-start(bf16[2,392,256]{2,1,0:T(8,128)(2,1)S(1)} %slice.94.refs_0_), channel_id=1, source_target_pairs={{0,32},{32,64},{64,96},{96,128},{128,160},{160,192},{192,224},{224... | collective-permute-start | bytes 1204232 | tf_op jit(solution)/shard_map/ppermute | solution.py:37
  34.7 11.8 %collective-permute-start.1 = (bf16[2,392,256]{2,1,0:T(8,128)(2,1)S(1)}, bf16[2,392,256]{2,1,0:T(8,128)(2,1)S(1)}, u32[]{:S(2)}, u32[]{:S(2)}) collective-permute-start(bf16[2,392,256]{2,1,0:T(8,128)(2,1)S(1)} %slice.94.refs_0_), channel_id=1, source_target_pairs={{0,224},{32,0},{64,32},{96,64},{128,96},{160,128},{192,160},{224,1... | collective-permute-start | bytes 1204232 | tf_op jit(solution)/shard_map/ppermute | solution.py:38
  41.9 18.6 %collective-permute-start.2 = (bf16[2,392,256]{2,1,0:T(8,128)(2,1)S(1)}, bf16[2,392,256]{2,1,0:T(8,128)(2,1)S(1)}, u32[]{:S(2)}, u32[]{:S(2)}) collective-permute-start(bf16[2,392,256]{2,1,0:T(8,128)(2,1)S(1)} %collective-permute-done.refs_1_), channel_id=1, source_target_pairs={{0,32},{32,64},{64,96},{96,128},{128,160},{160,192},{192,224},{224... | collective-permute-start | bytes 1204232 | tf_op jit(solution)/shard_map/ppermute | solution.py:37
  46.5 15.8 %collective-permute-start.3 = (bf16[2,392,256]{2,1,0:T(8,128)(2,1)S(1)}, bf16[2,392,256]{2,1,0:T(8,128)(2,1)S(1)}, u32[]{:S(2)}, u32[]{:S(2)}) collective-permute-start(bf16[2,392,256]{2,1,0:T(8,128)(2,1)S(1)} %collective-permute-done.1.refs_2_), channel_id=1, source_target_pairs={{0,224},{32,0},{64,32},{96,64},{128,96},{160,128},{192,160},{224,1... | collective-permute-start | bytes 1204232 | tf_op jit(solution)/shard_map/ppermute | solution.py:38
  60.4 11.1 %collective-permute-start.4 = (bf16[2,392,256]{2,1,0:T(8,128)(2,1)S(1)}, bf16[2,392,256]{2,1,0:T(8,128)(2,1)S(1)}, u32[]{:S(2)}, u32[]{:S(2)}) collective-permute-start(bf16[2,392,256]{2,1,0:T(8,128)(2,1)S(1)} %collective-permute-done.2.refs_3_), channel_id=1, source_target_pairs={{0,32},{32,64},{64,96},{96,128},{128,160},{160,192},{192,224},{224... | collective-permute-start | bytes 1204232 | tf_op jit(solution)/shard_map/ppermute | solution.py:37
  62.4 11.1 %copy-start.5 = (bf16[2,392,256]{2,1,0:T(8,128)(2,1)}, bf16[2,392,256]{2,1,0:T(8,128)(2,1)S(1)}, u32[]{:S(2)}) copy-start(bf16[2,392,256]{2,1,0:T(8,128)(2,1)S(1)} %collective-permute-done.3.refs_4_) | copy-start | bytes 1204228
  62.4 11.1 %collective-permute-start.5 = (bf16[2,392,256]{2,1,0:T(8,128)(2,1)S(1)}, bf16[2,392,256]{2,1,0:T(8,128)(2,1)S(1)}, u32[]{:S(2)}, u32[]{:S(2)}) collective-permute-start(bf16[2,392,256]{2,1,0:T(8,128)(2,1)S(1)} %collective-permute-done.3.refs_4_), channel_id=1, source_target_pairs={{0,224},{32,0},{64,32},{96,64},{128,96},{160,128},{192,160},{224,1... | collective-permute-start | bytes 1204232 | tf_op jit(solution)/shard_map/ppermute | solution.py:38
  71.6 8.5 %collective-permute-start.6 = (bf16[1,392,256]{2,1,0:T(8,128)(2,1)S(1)}, bf16[1,392,256]{2,1,0:T(8,128)(2,1)S(1)}, u32[]{:S(2)}, u32[]{:S(2)}) collective-permute-start(bf16[1,392,256]{2,1,0:T(8,128)(2,1)S(1)} %slice.95), channel_id=1, source_target_pairs={{0,32},{32,64},{64,96},{96,128},{128,160},{160,192},{192,224},{224... | collective-permute-start | bytes 602120 | tf_op jit(solution)/shard_map/ppermute | solution.py:40
  73.5 8.1 %collective-permute-start.7 = (bf16[1,392,256]{2,1,0:T(8,128)(2,1)S(1)}, bf16[1,392,256]{2,1,0:T(8,128)(2,1)S(1)}, u32[]{:S(2)}, u32[]{:S(2)}) collective-permute-start(bf16[1,392,256]{2,1,0:T(8,128)(2,1)S(1)} %slice.96), channel_id=1, source_target_pairs={{0,224},{32,0},{64,32},{96,64},{128,96},{160,128},{192,160},{224,1... | collective-permute-start | bytes 602120 | tf_op jit(solution)/shard_map/ppermute | solution.py:41
  82.9 4.9 %collective-permute-start.8 = (bf16[16,128,256]{2,1,0:T(8,128)(2,1)}, bf16[16,128,256]{2,1,0:T(8,128)(2,1)}, u32[]{:S(2)}, u32[]{:S(2)}) collective-permute-start(bf16[16,128,256]{2,1,0:T(8,128)(2,1)} %slice_dynamic-update-slice_fusion.7), channel_id=1, source_target_pairs={{0,1},{1,0},{2,3},{3,2},{4,5},{5,4},{6,7},{7,6},{8,9},{9,8},{10,11... | collective-permute-start | bytes 3145736 | tf_op jit(solution)/shard_map/ppermute | solution.py:400
  90.0 7.2 %copy-start.13 = (f32[4,256]{1,0:T(4,128)S(1)}, f32[4,256]{1,0:T(4,128)}, u32[]{:S(2)}) copy-start(f32[4,256]{1,0:T(4,128)} %param.16) | copy-start | bytes 12292
  94.1 2.4 %copy-start.1 = (bf16[4096,640]{1,0:T(8,128)(2,1)}, bf16[4096,640]{1,0:T(8,128)(2,1)S(1)}, u32[]{:S(2)}) copy-start(bf16[4096,640]{1,0:T(8,128)(2,1)S(1)} %shard_map.100.w_ref) | copy-start | bytes 15728644
  97.2 15.1 %copy-start.14 = (f32[4]{0:T(128)S(1)}, f32[4]{0:T(128)}, u32[]{:S(2)}) copy-start(f32[4]{0:T(128)} %param.19) | copy-start | bytes 52
  97.3 15.1 %copy-start.15 = (f32[4]{0:T(128)S(1)}, f32[4]{0:T(128)}, u32[]{:S(2)}) copy-start(f32[4]{0:T(128)} %param.18) | copy-start | bytes 52
  97.3 15.2 %copy-start.16 = (s32[16]{0:T(128)S(1)}, s32[16]{0:T(128)}, u32[]{:S(2)}) copy-start(s32[16]{0:T(128)} %param.11) | copy-start | bytes 196
  108.8 6.8 %collective-permute-start.9 = (bf16[8,512]{1,0:T(8,128)(2,1)S(1)}, bf16[8,512]{1,0:T(8,128)(2,1)S(1)}, u32[]{:S(2)}, u32[]{:S(2)}) collective-permute-start(bf16[8,512]{1,0:T(8,128)(2,1)S(1)} %slice.115), channel_id=1, source_target_pairs={{0,32},{32,64},{64,96},{96,128},{128,160},{160,192},{192,224},{224... | collective-permute-start | bytes 24584 | tf_op jit(solution)/shard_map/ppermute | solution.py:30
  122.5 18.5 %collective-permute-start.10 = (bf16[144,256]{1,0:T(8,128)(2,1)S(1)}, bf16[144,256]{1,0:T(8,128)(2,1)S(1)}, u32[]{:S(2)}, u32[]{:S(2)}) collective-permute-start(bf16[144,256]{1,0:T(8,128)(2,1)S(1)} %get-tuple-element.18.own_ref), channel_id=1, source_target_pairs={{0,32},{32,64},{64,96},{96,128},{128,160},{160,192},{192,224},{224... | collective-permute-start | bytes 221192 | tf_op jit(solution)/shard_map/ppermute | solution.py:30
  125.8 24.5 %collective-permute-start.11 = (bf16[144,256]{1,0:T(8,128)(2,1)S(1)}, bf16[144,256]{1,0:T(8,128)(2,1)S(1)}, u32[]{:S(2)}, u32[]{:S(2)}) collective-permute-start(bf16[144,256]{1,0:T(8,128)(2,1)S(1)} %get-tuple-element.18.own_ref), channel_id=1, source_target_pairs={{0,64},{32,96},{64,128},{96,160},{128,192},{160,224},{192,256},{22... | collective-permute-start | bytes 221192 | tf_op jit(solution)/shard_map/ppermute | solution.py:30
  130.6 20.9 %collective-permute-start.12 = (bf16[144,256]{1,0:T(8,128)(2,1)S(1)}, bf16[144,256]{1,0:T(8,128)(2,1)S(1)}, u32[]{:S(2)}, u32[]{:S(2)}) collective-permute-start(bf16[144,256]{1,0:T(8,128)(2,1)S(1)} %get-tuple-element.18.own_ref), channel_id=1, source_target_pairs={{0,96},{32,128},{64,160},{96,192},{128,224},{160,256},{192,288},{2... | collective-permute-start | bytes 221192 | tf_op jit(solution)/shard_map/ppermute | solution.py:30
  151.6 13.4 %collective-permute-start.13 = (bf16[144,256]{1,0:T(8,128)(2,1)S(1)}, bf16[144,256]{1,0:T(8,128)(2,1)S(1)}, u32[]{:S(2)}, u32[]{:S(2)}) collective-permute-start(bf16[144,256]{1,0:T(8,128)(2,1)S(1)} %shard_map.103), channel_id=1, source_target_pairs={{0,32},{32,64},{64,96},{96,128},{128,160},{160,192},{192,224},{224... | collective-permute-start | bytes 221192 | tf_op jit(solution)/shard_map/ppermute | solution.py:30
  155.9 14.9 %collective-permute-start.14 = (bf16[144,256]{1,0:T(8,128)(2,1)S(1)}, bf16[144,256]{1,0:T(8,128)(2,1)S(1)}, u32[]{:S(2)}, u32[]{:S(2)}) collective-permute-start(bf16[144,256]{1,0:T(8,128)(2,1)S(1)} %shard_map.103), channel_id=1, source_target_pairs={{0,160},{32,192},{64,224},{96,256},{128,288},{160,320},{192,352},{... | collective-permute-start | bytes 221192 | tf_op jit(solution)/shard_map/ppermute | solution.py:30
  159.4 11.3 %copy-start.4 = (f32[1024,256]{1,0:T(8,128)S(1)}, f32[1024,256]{1,0:T(8,128)}, u32[]{:S(2)}) copy-start(f32[1024,256]{1,0:T(8,128)} %copy-done.3) | copy-start | bytes 3145732
  (10 other events, 10.5 us)
Sparse Core Ops, SparseCore 0:
  9.5 74.5 all-gather.4
  96.7 51.9 all-gather.6

commit v3 on v2

--- a/solution.py
+++ b/solution.py
@@ -43,7 +43,8 @@
 
 
 def call(
-    kernel, grid, in_specs, out_specs, out_shape, scratch=(), prefetch=0, cost=None, room=12
+    kernel, grid, in_specs, out_specs, out_shape, scratch=(), prefetch=0, cost=None, room=12,
+    aliases=None,
 ):
     return pl.pallas_call(
         kernel,
@@ -55,6 +56,7 @@
             scratch_shapes=scratch,
         ),
         out_shape=out_shape,
+        input_output_aliases=aliases or {},
         compiler_params=pltpu.CompilerParams(
             vmem_limit_bytes=room * MIB, dimension_semantics=("arbitrary",) * len(grid)
         ),
@@ -66,15 +68,23 @@
     return pl.BlockSpec(shape, lambda *_: (0,) * len(shape))
 
 
+def in_hbm(value):
+    return pltpu.with_memory_space_constraint(value, pltpu.HBM)
+
+
+def held(_):
+    return pl.BlockSpec(memory_space=pltpu.VMEM)
+
+
 def rows_of(shape):
     return pl.BlockSpec(shape, lambda i, *_: (i,) + (0,) * (len(shape) - 1))
 
 
-def assemble_kernel(layout, scalars, *refs):
-    count = len(layout)
-    pieces, swapped, out = refs[:count], refs[count : 2 * count], refs[2 * count]
+def first_kernel(layout, scalars, tok_ref, *refs):
+    pieces, other, proj_ref, out = refs[:-3], refs[-3], refs[-2], refs[-1]
     z, core = scalars[0], scalars[1]
-    for (offset, first, yh_count), piece, other in zip(layout, pieces, swapped):
+    count = 0
+    for (offset, first, yh_count), piece in zip(layout, pieces):
         source = lax.rem(z + offset, Z)
         for local_yh in range(yh_count):
             start = pl.multiple_of(((first + local_yh) * Z + source) * 256, 256)
@@ -82,22 +92,22 @@
             own = pl.multiple_of(start + core * 128, 128)
             its = pl.multiple_of(start + (1 - core) * 128, 128)
             out[pl.ds(own, 128), 256:512] = piece[local_yh, 256:384, :]
-            out[pl.ds(its, 128), 256:512] = other[local_yh, :, :]
+            out[pl.ds(its, 128), 256:512] = other[count, :, :]
+            count += 1
             steps = piece[local_yh, 384:392, :].astype(F32).T
             steps = jnp.concatenate([steps, jnp.zeros((256, 120), F32)], axis=1)
             out[pl.ds(start, 256), 512:640] = steps.astype(BF16)
-
-
-def project_kernel(tok_ref, w_ref, out_ref):
+    project(tok_ref, out, proj_ref)
+
+
+def project(tok_ref, w_ref, out_ref):
     out_ref[...] = jnp.dot(
         tok_ref[...], w_ref[...], preferred_element_type=F32
     ).astype(BF16)
 
 
-def gate_kernel(tok_ref, w_ref, out_ref):
-    weights = jnp.concatenate([w_ref[z, yh] for yh in range(YH) for z in range(Z)], axis=0)
-    proj = jnp.dot(tok_ref[...], weights, preferred_element_type=F32).astype(BF16)
-    out_ref[...] = jax.nn.silu(proj.astype(F32))
+def rest_kernel(tok_ref, w_ref, _, out_ref):
+    project(tok_ref, w_ref, out_ref)
 
 
 def spread(columns):
@@ -217,25 +227,34 @@
     return packed[STATE : STATE + 8].astype(F32) + packed[STATE + 8 : STATE + 16].astype(F32)
 
 
-def near_kernel(own_ref, one_ref, two_ref, three_ref, out_ref):
-    own = own_ref[...]
-    total, gain = own[0:STATE].astype(F32), gain_of(own)
-    for ref in (one_ref, two_ref, three_ref):
-        piece = ref[...]
-        total = total + gain[0:1] * piece[0:STATE].astype(F32)
-        gain = gain * gain_of(piece)
-    high = gain.astype(BF16)
-    low = (gain - high.astype(F32)).astype(BF16)
+def carry_kernel(own_ref, before_ref, out_ref):
+    own, before = own_ref[...], before_ref[...]
+    total = own[0:STATE].astype(F32) + gain_of(own)[0:1] * before[0:STATE].astype(F32)
     out_ref[0:STATE, :] = total.astype(BF16)
-    out_ref[STATE : STATE + 16, :] = jnp.concatenate([high, low], axis=0)
-
-
-def finish_kernel(first_ref, second_ref, act_ref, y_ref, reach_ref, gate_ref, out_ref):
-    first, second = first_ref[...], second_ref[...]
-    gain = gain_of(first)[0:1]
-    entering = first[0:STATE].astype(F32) + gain * second[0:STATE].astype(F32)
-    carried = jnp.dot(act_ref[...], entering.astype(BF16), preferred_element_type=F32)
-    out_ref[...] = ((y_ref[...] + reach_ref[...] * carried) * gate_ref[...]).astype(BF16)
+    out_ref[STATE : STATE + 16, :] = own[STATE : STATE + 16]
+
+
+def finish_kernel(
+    scalars, before_ref, shards_ref, act_ref, y_ref, reach_ref, tok_ref, w_ref, out_ref,
+    entering, weights,
+):
+    @pl.when(pl.program_id(0) == 0)
+    def _():
+        z = scalars[0]
+        state = jnp.zeros((STATE, 256), F32)
+        for k in range(Z - 1):
+            piece = shards_ref[k]
+            later = gain_of(piece)[0:1] * state + piece[0:STATE].astype(F32)
+            state = jnp.where(k < z, later, state)
+        entering[...] = (state + before_ref[0:STATE, :].astype(F32)).astype(BF16)
+        for k in range(Z):
+            for yh in range(YH):
+                weights[pl.ds((yh * Z + k) * 256, 256), :] = w_ref[k, yh]
+
+    gate = jnp.dot(tok_ref[...], weights[...], preferred_element_type=F32).astype(BF16)
+    carried = jnp.dot(act_ref[...], entering[...], preferred_element_type=F32)
+    total = y_ref[...] + reach_ref[...] * carried
+    out_ref[...] = (total * jax.nn.silu(gate.astype(F32))).astype(BF16)
 
 
 def shape(dims, dtype):
@@ -246,46 +265,36 @@
     return pl.CostEstimate(flops=flops, bytes_accessed=moved, transcendentals=exps)
 
 
-def run_assemble(pieces, swapped, scalars):
+def run_first(gathered, pieces, swapped, scalars):
+    rows, depth = gathered.shape
     layout = tuple((offset, first, piece.shape[0]) for offset, first, piece in pieces)
-    arrays = [piece for _, _, piece in pieces]
-    return call(
-        functools.partial(assemble_kernel, layout),
+    arrays = [in_hbm(piece) for _, _, piece in pieces] + [in_hbm(swapped)]
+    last = rows // BLOCK - 1
+    return call(
+        functools.partial(first_kernel, layout),
         (1,),
-        [whole(a.shape) for a in arrays] + [whole(a.shape) for a in swapped],
-        whole((4096, 640)),
-        shape((4096, 640), BF16),
+        [pl.BlockSpec((BLOCK, depth), lambda *_: (last, 0))] + [whole(a.shape) for a in arrays],
+        [pl.BlockSpec((BLOCK, 640), lambda *_: (last, 0)), held(None)],
+        [shape((rows, 640), BF16), shape((depth, 640), BF16)],
         prefetch=1,
-        cost=work(0, 12 << 20),
+        cost=work(2 * BLOCK * depth * 640, 12 << 20),
         room=24,
-    )(scalars, *arrays, *swapped)
-
-
-def run_project(gathered, weights):
+    )(scalars, gathered, *arrays)
+
+
+def run_rest(gathered, weights, proj):
     rows, depth = gathered.shape
-    cols = weights.shape[1]
-    return call(
-        project_kernel,
-        (rows // 256,),
-        [rows_of((256, depth)), whole((depth, cols))],
-        rows_of((256, cols)),
-        shape((rows, cols), BF16),
-        cost=work(2 * rows * depth * cols, 14 << 20),
-        room=48,
-    )(gathered, weights)
-
-
-def run_gate(gathered, gate_all):
-    rows, depth = gathered.shape
-    return call(
-        gate_kernel,
-        (rows // 256,),
-        [rows_of((256, depth)), whole(gate_all.shape)],
-        rows_of((256, 256)),
-        shape((rows, 256), F32),
-        cost=work(2 * rows * depth * 256, 11 << 20),
-        room=48,
-    )(gathered, gate_all)
+    count = rows // BLOCK - 1
+    return call(
+        rest_kernel,
+        (count,),
+        [rows_of((BLOCK, depth)), held(weights), pl.BlockSpec(memory_space=pl.ANY)],
+        rows_of((BLOCK, 640)),
+        shape((rows, 640), BF16),
+        cost=work(2 * count * BLOCK * depth * 640, 8 << 20),
+        room=16,
+        aliases={2: 0},
+    )(gathered, weights, proj)
 
 
 def run_state(starts, base, proj, rim, taps, small):
@@ -335,40 +344,45 @@
             rows_of((1, 8, 256)),
         ],
         [rows_of((BLOCK, 256)), rows_of((BLOCK, 256))],
-        [shape((rows, 256), F32), shape((rows, 256), F32)],
+        [pltpu.HBM((rows, 256), F32), pltpu.HBM((rows, 256), F32)],
         prefetch=2,
         cost=work(2 * rows * 256 * 1024, 5 << 20, rows * 1280),
     )(starts, base, act, cum, step, inside, gains)
 
 
-def run_near(pieces):
-    return call(
-        near_kernel,
+def run_carry(own, before):
+    return call(
+        carry_kernel,
         (1,),
-        [whole(p.shape) for p in pieces],
-        whole(pieces[0].shape),
-        shape(pieces[0].shape, BF16),
-        cost=work(1 << 18, 1 << 19),
-    )(*pieces)
-
-
-def run_finish(first, second, act, y, reach, gate):
-    rows = y.shape[0]
+        [held(own), held(before)],
+        held(own),
+        shape(own.shape, BF16),
+        cost=work(1 << 17, 1 << 18),
+        room=4,
+    )(own, before)
+
+
+def run_finish(scalars, before, shards, act, y, reach, gathered, gate_all):
+    rows, depth = gathered.shape
     return call(
         finish_kernel,
         (rows // BLOCK,),
         [
-            whole(first.shape),
-            whole(second.shape),
-            pl.BlockSpec((BLOCK, 128), lambda i: (i, 3)),
+            held(before),
+            held(shards),
+            pl.BlockSpec((BLOCK, 128), lambda i, *_: (i, 3)),
             rows_of((BLOCK, 256)),
             rows_of((BLOCK, 256)),
-            rows_of((BLOCK, 256)),
+            rows_of((BLOCK, depth)),
+            whole(gate_all.shape),
         ],
         rows_of((BLOCK, 256)),
         shape((rows, 256), BF16),
-        cost=work(2 * rows * 128 * 256, 4 << 20),
-    )(first, second, act, y, reach, gate)
+        scratch=[pltpu.VMEM((STATE, 256), BF16), pltpu.VMEM((depth, 256), BF16)],
+        prefetch=1,
+        cost=work(2 * rows * (128 + depth) * 256, 13 << 20),
+        room=20,
+    )(scalars, before, shards, act, y, reach, gathered, gate_all)
 
 
 def local(
@@ -398,27 +412,26 @@
     pieces = ring_gather(both[:, :392])
     halves = jnp.concatenate([piece[:, 256:384] for _, _, piece in pieces], axis=0)
     halves = lax.ppermute(halves, "c", [(0, 1), (1, 0)])
-    swapped, at = [], 0
-    for _, _, piece in pieces:
-        swapped.append(halves[at : at + piece.shape[0]])
-        at += piece.shape[0]
     scalars = jnp.stack([z, core]).astype(jnp.int32)
-    weights = run_assemble(pieces, swapped, scalars)
-    gate_part, gathered, weights = lax.optimization_barrier((both[:, 392:], gathered, weights))
+    gate_part, gathered, halves = lax.optimization_barrier((both[:, 392:], gathered, halves))
     gate_all = lax.all_gather(gate_part, "z", axis=0, tiled=False)
-    proj = run_project(gathered, weights)
+    gathered = in_hbm(gathered)
+    proj, weights = run_first(gathered, pieces, halves, scalars)
     rim = along_seq(proj[-8:, :512], 1)
+    proj = run_rest(gathered, weights, proj)
 
     starts = (jnp.cumsum(doc_lengths) - doc_lengths).astype(jnp.int32)
     base = (lax.axis_index(SEQ) * tok_dev).astype(jnp.int32).reshape(1)
     taps = jnp.concatenate([value_conv, conv_own], axis=1)
     small = jnp.pad(jnp.stack([step_bias, log_rate]), ((0, 6), (0, 128 - heads_here)))
     act, cum, step, inside, gains, packed = run_state(starts, base, proj, rim, taps, small)
-    near = run_near([packed] + [along_seq(packed, hop) for hop in (1, 2, 3)])
+    before = lax.ppermute(packed, SEQ, [(Z - 1, Z)])
     y, reach = run_blocks(starts, base, act, cum, step, inside, gains)
-    first, second = along_seq(near, 1), along_seq(near, 5)
-    gate = run_gate(gathered, gate_all)
-    return run_finish(first, second, act, y, reach, gate)
+    carried = run_carry(packed, before)
+    shards = lax.all_gather(carried, "z", axis=0, tiled=False)
+    return run_finish(
+        scalars, before, shards, act, in_hbm(y), in_hbm(reach), gathered, in_hbm(gate_all)
+    )
 
 
 def solution(mesh):

time: 180 us -> 170 us (0.944)
  the two profiles are of different devices: /device:TPU:112 before, /device:TPU:6 now
where the time goes in v3:
time: 170 us; the launch traced here: 168 us
  blocking collectives  58.4 us (34%)
  starting transfers between devices  40.1 us (24%)
  Pallas kernels  31.5 us (19%)
  waiting for transfers between devices  15.2 us (9%)
  between operations  13.7 us (8%)
  local copies, waits for them, and re-layouts  8.03 us (5%)
    all_gather x1, blocking collectives, local(): shards = lax.all_gather(carried, 'z', axis=0, tiled=False)  37.7 us
    all_gather x1, blocking collectives, local(): both = lax.all_gather(pack, 'yh', axis=0, tiled=False)  20.7 us
    ppermute x3, starting transfers between devices, ring_gather(): left = lax.ppermute(left, 'z', ring(Z, -1))  18.7 us
    ppermute x3, waiting for transfers between devices, ring_gather(): right = lax.ppermute(right, 'z', ring(Z, 1))  11 us
    pallas_call x1, Pallas kernels, run_finish(): call(finish_kernel, (rows // BLOCK,), [held(before), held(shards), pl.Blo...  8.23 us
    ppermute x3, starting transfers between devices, ring_gather(): right = lax.ppermute(right, 'z', ring(Z, 1))  8.1 us
    pallas_call x1, Pallas kernels, run_rest(): call(rest_kernel, (count,), [rows_of((BLOCK, depth)), held(weights), pl.B...  7.22 us
    pallas_call x1, Pallas kernels, run_first(): call(functools.partial(first_kernel, layout), (1,), [pl.BlockSpec((BLOCK,...  5.89 us
  transfers between devices with their start and end apart: 13, of which 5 were waited for; matrix products, arithmetic and copies ran while one was open for 5% of the time, Pallas kernels for 14%

profile of v3, /device:TPU:6, one launch (start us, length us, event | category | flops | bytes accessed | tf_op | source)
XLA Modules:
  0.0 168.2 jit_solution(16401571004046670053)
XLA Ops:
  7.8 1.0 fusion.3
  8.8 20.7 %all-gather = bf16[1296,256]{1,0:T(8,128)(2,1)S(1)} all-gather(bf16[648,256]{1,0:T(8,128)(2,1)S(1)} %fusion.3), channel_id=2, replica_groups=mesh['yh'=2,'z'=8,'x'=4,'y'=4,'c'=2] {'yh'}, dimensions={0}, use_global_device_ids=true | all-gather | bytes 995328 | tf_op jit(solution)/shard_map/all_gather | solution.py:411
  29.5 4.3 %collective-permute-start = (bf16[2,392,256]{2,1,0:T(8,128)(2,1)S(1)}, bf16[2,392,256]{2,1,0:T(8,128)(2,1)S(1)}, u32[]{:S(2)}, u32[]{:S(2)}) collective-permute-start(bf16[2,392,256]{2,1,0:T(8,128)(2,1)S(1)} %slice.59.refs_0_), channel_id=1, source_target_pairs={{0,32},{32,64},{64,96},{96,128},{128,160},{160,192},{192,224},{224... | collective-permute-start | bytes 1204232 | tf_op jit(solution)/shard_map/ppermute | solution.py:37
  33.8 7.9 %collective-permute-start.1 = (bf16[2,392,256]{2,1,0:T(8,128)(2,1)S(1)}, bf16[2,392,256]{2,1,0:T(8,128)(2,1)S(1)}, u32[]{:S(2)}, u32[]{:S(2)}) collective-permute-start(bf16[2,392,256]{2,1,0:T(8,128)(2,1)S(1)} %slice.59.refs_0_), channel_id=1, source_target_pairs={{0,224},{32,0},{64,32},{96,64},{128,96},{160,128},{192,160},{224,1... | collective-permute-start | bytes 1204232 | tf_op jit(solution)/shard_map/ppermute | solution.py:38
  42.4 3.2 %collective-permute-done.refs_1_ = bf16[2,392,256]{2,1,0:T(8,128)(2,1)S(1)} collective-permute-done((bf16[2,392,256]{2,1,0:T(8,128)(2,1)S(1)}, bf16[2,392,256]{2,1,0:T(8,128)(2,1)S(1)}, u32[]{:S(2)}, u32[]{:S(2)}) %collective-permute-start) | collective-permute-done | bytes 401440 | tf_op jit(solution)/shard_map/ppermute | solution.py:37
  45.6 1.9 %collective-permute-start.2 = (bf16[2,392,256]{2,1,0:T(8,128)(2,1)S(1)}, bf16[2,392,256]{2,1,0:T(8,128)(2,1)S(1)}, u32[]{:S(2)}, u32[]{:S(2)}) collective-permute-start(bf16[2,392,256]{2,1,0:T(8,128)(2,1)S(1)} %collective-permute-done.refs_1_), channel_id=1, source_target_pairs={{0,32},{32,64},{64,96},{96,128},{128,160},{160,192},{192,224},{224... | collective-permute-start | bytes 1204232 | tf_op jit(solution)/shard_map/ppermute | solution.py:37
  47.5 5.3 %collective-permute-start.3 = (bf16[2,392,256]{2,1,0:T(8,128)(2,1)S(1)}, bf16[2,392,256]{2,1,0:T(8,128)(2,1)S(1)}, u32[]{:S(2)}, u32[]{:S(2)}) collective-permute-start(bf16[2,392,256]{2,1,0:T(8,128)(2,1)S(1)} %collective-permute-done.1.refs_2_), channel_id=1, source_target_pairs={{0,224},{32,0},{64,32},{96,64},{128,96},{160,128},{192,160},{224,1... | collective-permute-start | bytes 1204232 | tf_op jit(solution)/shard_map/ppermute | solution.py:38
  54.2 3.4 %collective-permute-done.2.refs_3_ = bf16[2,392,256]{2,1,0:T(8,128)(2,1)S(1)} collective-permute-done((bf16[2,392,256]{2,1,0:T(8,128)(2,1)S(1)}, bf16[2,392,256]{2,1,0:T(8,128)(2,1)S(1)}, u32[]{:S(2)}, u32[]{:S(2)}) %collective-permute-start.2) | collective-permute-done | bytes 401440 | tf_op jit(solution)/shard_map/ppermute | solution.py:37
  57.6 1.9 %collective-permute-start.4 = (bf16[2,392,256]{2,1,0:T(8,128)(2,1)S(1)}, bf16[2,392,256]{2,1,0:T(8,128)(2,1)S(1)}, u32[]{:S(2)}, u32[]{:S(2)}) collective-permute-start(bf16[2,392,256]{2,1,0:T(8,128)(2,1)S(1)} %collective-permute-done.2.refs_3_), channel_id=1, source_target_pairs={{0,32},{32,64},{64,96},{96,128},{128,160},{160,192},{192,224},{224... | collective-permute-start | bytes 1204232 | tf_op jit(solution)/shard_map/ppermute | solution.py:37
  59.6 5.5 %collective-permute-start.5 = (bf16[2,392,256]{2,1,0:T(8,128)(2,1)S(1)}, bf16[2,392,256]{2,1,0:T(8,128)(2,1)S(1)}, u32[]{:S(2)}, u32[]{:S(2)}) collective-permute-start(bf16[2,392,256]{2,1,0:T(8,128)(2,1)S(1)} %collective-permute-done.3.refs_4_), channel_id=1, source_target_pairs={{0,224},{32,0},{64,32},{96,64},{128,96},{160,128},{192,160},{224,1... | collective-permute-start | bytes 1204232 | tf_op jit(solution)/shard_map/ppermute | solution.py:38
  66.4 4.3 %collective-permute-done.4.refs_5_ = bf16[2,392,256]{2,1,0:T(8,128)(2,1)S(1)} collective-permute-done((bf16[2,392,256]{2,1,0:T(8,128)(2,1)S(1)}, bf16[2,392,256]{2,1,0:T(8,128)(2,1)S(1)}, u32[]{:S(2)}, u32[]{:S(2)}) %collective-permute-start.4) | collective-permute-done | bytes 401440 | tf_op jit(solution)/shard_map/ppermute | solution.py:37
  70.8 1.9 %collective-permute-start.6 = (bf16[1,392,256]{2,1,0:T(8,128)(2,1)S(1)}, bf16[1,392,256]{2,1,0:T(8,128)(2,1)S(1)}, u32[]{:S(2)}, u32[]{:S(2)}) collective-permute-start(bf16[1,392,256]{2,1,0:T(8,128)(2,1)S(1)} %slice.66), channel_id=1, source_target_pairs={{0,32},{32,64},{64,96},{96,128},{128,160},{160,192},{192,224},{224... | collective-permute-start | bytes 602120 | tf_op jit(solution)/shard_map/ppermute | solution.py:40
  72.7 5.5 %collective-permute-start.7 = (bf16[1,392,256]{2,1,0:T(8,128)(2,1)S(1)}, bf16[1,392,256]{2,1,0:T(8,128)(2,1)S(1)}, u32[]{:S(2)}, u32[]{:S(2)}) collective-permute-start(bf16[1,392,256]{2,1,0:T(8,128)(2,1)S(1)} %slice.68), channel_id=1, source_target_pairs={{0,224},{32,0},{64,32},{96,64},{128,96},{160,128},{192,160},{224,1... | collective-permute-start | bytes 602120 | tf_op jit(solution)/shard_map/ppermute | solution.py:41
  80.3 1.2 collective-permute-done.7.refs_8_
  82.1 1.9 %collective-permute-start.8 = (bf16[16,128,256]{2,1,0:T(8,128)(2,1)}, bf16[16,128,256]{2,1,0:T(8,128)(2,1)}, u32[]{:S(2)}, u32[]{:S(2)}) collective-permute-start(bf16[16,128,256]{2,1,0:T(8,128)(2,1)} %slice_dynamic-update-slice_fusion.7), channel_id=1, source_target_pairs={{0,1},{1,0},{2,3},{3,2},{4,5},{5,4},{6,7},{7,6},{8,9},{9,8},{10,11... | collective-permute-start | bytes 3145736 | tf_op jit(solution)/shard_map/ppermute | solution.py:414
  84.1 0.7 slice.57
  84.8 2.2 %collective-permute-done.8.refs_9_ = bf16[16,128,256]{2,1,0:T(8,128)(2,1)} collective-permute-done((bf16[16,128,256]{2,1,0:T(8,128)(2,1)}, bf16[16,128,256]{2,1,0:T(8,128)(2,1)}, u32[]{:S(2)}, u32[]{:S(2)}) %collective-permute-start.8) | collective-permute-done | bytes 1048608 | tf_op jit(solution)/shard_map/ppermute | solution.py:414
  88.2 5.9 %shard_map.100 = (bf16[1024,640]{1,0:T(8,128)(2,1)S(1)}, bf16[4096,640]{1,0:T(8,128)(2,1)S(1)}) custom-call(s32[2]{0:T(128)S(1)} %pad_add_fusion.scalars, bf16[1024,4096]{1,0:T(8,128)(2,1)} %all-gather.6.cloned.1.call-done.tok_ref, bf16[2,392,256]{2,1,0:T(8,128)(2,1)} %copy-done.1, bf16[2,392,256]{2,1,0:T(8,128)(2,1)} %copy-done.4, ...), custom_call_target="tpu_custom_call" | custom-call | flops 1342177280 | bytes 12582912 | tf_op jit(solution)/shard_map/pallas_call | solution.py:273
  94.1 3.2 %collective-permute-start.9 = (bf16[8,512]{1,0:T(8,128)(2,1)S(1)}, bf16[8,512]{1,0:T(8,128)(2,1)S(1)}, u32[]{:S(2)}, u32[]{:S(2)}) collective-permute-start(bf16[8,512]{1,0:T(8,128)(2,1)S(1)} %slice.56), channel_id=1, source_target_pairs={{0,32},{32,64},{64,96},{96,128},{128,160},{160,192},{192,224},{224... | collective-permute-start | bytes 24584 | tf_op jit(solution)/shard_map/ppermute | solution.py:30
  97.3 7.2 %shard_map.101.proj_ref = bf16[1024,640]{1,0:T(8,128)(2,1)S(1)} custom-call(bf16[1024,4096]{1,0:T(8,128)(2,1)} %all-gather.6.cloned.1.call-done.tok_ref, bf16[4096,640]{1,0:T(8,128)(2,1)S(1)} %get-tuple-element.20.w_ref, bf16[1024,640]{1,0:T(8,128)(2,1)S(1)} %get-tuple-element.21._), custom_call_target="tpu_custom_call", output_to_operand_aliasing={{}: (2, {})} | custom-call | flops 4026531840 | bytes 8388608 | tf_op jit(solution)/shard_map/pallas_call | solution.py:288
  104.6 5.6 %shard_map.102 = (bf16[1024,512]{1,0:T(8,128)(2,1)S(1)}, f32[1024,128]{1,0:T(8,128)S(1)}, f32[1024,128]{1,0:T(8,128)S(1)}, f32[4,128,256]{2,1,0:T(8,128)S(1)}, f...) custom-call(s32[16]{0:T(128)S(1)} %sub.7.starts, s32[1]{0:T(128)} %bitcast.3.base, ...), custom_call_target="tpu_custom_call" | custom-call | flops 67108864 | bytes 4194304 | tf_op jit(solution)/shard_map/pallas_call | solution.py:303
  110.9 4.6 %shard_map.104 = (f32[1024,256]{1,0:T(8,128)}, f32[1024,256]{1,0:T(8,128)}) custom-call(s32[16]{0:T(128)S(1)} %sub.7.starts, s32[1]{0:T(128)} %bitcast.3.base, bf16[1024,512]{1,0:T(8,128)(2,1)S(1)} %get-tuple-element.23.act_ref, f32[1024,128]{1,0:T(8,128)S(1)} %get-tuple-element.24.cum_ref, f32[1024,128]{1,0:T(8,128)S(1)} %get-tuple-element.25.step_ref, ...), custom_call_target="tpu_custom_call" | custom-call | flops 536870912 | bytes 5242880 | tf_op jit(solution)/shard_map/pallas_call | solution.py:336
  115.5 37.7 %all-gather.1 = bf16[1152,256]{1,0:T(8,128)(2,1)S(1)} all-gather(bf16[144,256]{1,0:T(8,128)(2,1)S(1)} %shard_map.103), channel_id=3, replica_groups=mesh['yh'=2,'z'=8,'x'=4,'y'=4,'c'=2] {'z'}, dimensions={0}, use_global_device_ids=true | all-gather | bytes 663552 | tf_op jit(solution)/shard_map/all_gather | solution.py:431
  153.2 8.2 %shard_map.105 = bf16[1024,256]{1,0:T(8,128)(2,1)} custom-call(s32[2]{0:T(128)S(1)} %pad_add_fusion.scalars, bf16[144,256]{1,0:T(8,128)(2,1)S(1)} %collective-permute-done.10.before_ref, bf16[8,144,256]{2,1,0:T(8,128)(2,1)S(1)} %bitcast.14, bf16[1024,512]{1,0:T(8,128)(2,1)S(1)} %get-tuple-element.23.act_ref, f32[1024,256]{1,0:T(8,128)} %get-tuple-element.28.y_ref, ...), custom_call_target="tpu_custom_call" | custom-call | flops 2214592512 | bytes 13631488 | tf_op jit(solution)/shard_map/pallas_call | solution.py:367
  (64 shorter events, 9.0 us)
Async XLA Ops:
  6.5 80.5 %all-gather.6.cloned.1.call-start = ((), (), s32[]{:S(2)}) async-start(), calls=%async_computation | async-start | bytes 8650752 | tf_op jit(solution)/shard_map/all_gather | solution.py:405
  7.3 145.9 %all-gather.8.cloned.1.call-start = ((), (), s32[]{:S(2)}) async-start(), calls=%async_computation.1 | async-start | bytes 2359296 | tf_op jit(solution)/shard_map/all_gather | solution.py:417
  29.5 57.6 %copy-start.11 = (s32[16]{0:T(128)S(1)}, s32[16]{0:T(128)}, u32[]{:S(2)}) copy-start(s32[16]{0:T(128)} %param.11) | copy-start | bytes 196
  29.5 58.6 %copy-start.12 = (f32[4]{0:T(128)S(1)}, f32[4]{0:T(128)}, u32[]{:S(2)}) copy-start(f32[4]{0:T(128)} %param.19) | copy-start | bytes 52
  29.5 58.6 %copy-start.13 = (f32[4]{0:T(128)S(1)}, f32[4]{0:T(128)}, u32[]{:S(2)}) copy-start(f32[4]{0:T(128)} %param.18) | copy-start | bytes 52
  29.5 58.6 %copy-start.10 = (f32[4,256]{1,0:T(4,128)S(1)}, f32[4,256]{1,0:T(4,128)}, u32[]{:S(2)}) copy-start(f32[4,256]{1,0:T(4,128)} %param.16) | copy-start | bytes 12292
  29.5 58.6 %copy-start.1 = (bf16[2,392,256]{2,1,0:T(8,128)(2,1)}, bf16[2,392,256]{2,1,0:T(8,128)(2,1)S(1)}, u32[]{:S(2)}) copy-start(bf16[2,392,256]{2,1,0:T(8,128)(2,1)S(1)} %slice.59.refs_0_) | copy-start | bytes 1204228
  29.5 16.1 %collective-permute-start = (bf16[2,392,256]{2,1,0:T(8,128)(2,1)S(1)}, bf16[2,392,256]{2,1,0:T(8,128)(2,1)S(1)}, u32[]{:S(2)}, u32[]{:S(2)}) collective-permute-start(bf16[2,392,256]{2,1,0:T(8,128)(2,1)S(1)} %slice.59.refs_0_), channel_id=1, source_target_pairs={{0,32},{32,64},{64,96},{96,128},{128,160},{160,192},{192,224},{224... | collective-permute-start | bytes 1204232 | tf_op jit(solution)/shard_map/ppermute | solution.py:37
  33.8 13.7 %collective-permute-start.1 = (bf16[2,392,256]{2,1,0:T(8,128)(2,1)S(1)}, bf16[2,392,256]{2,1,0:T(8,128)(2,1)S(1)}, u32[]{:S(2)}, u32[]{:S(2)}) collective-permute-start(bf16[2,392,256]{2,1,0:T(8,128)(2,1)S(1)} %slice.59.refs_0_), channel_id=1, source_target_pairs={{0,224},{32,0},{64,32},{96,64},{128,96},{160,128},{192,160},{224,1... | collective-permute-start | bytes 1204232 | tf_op jit(solution)/shard_map/ppermute | solution.py:38
  45.6 42.5 %copy-start.4 = (bf16[2,392,256]{2,1,0:T(8,128)(2,1)}, bf16[2,392,256]{2,1,0:T(8,128)(2,1)S(1)}, u32[]{:S(2)}) copy-start(bf16[2,392,256]{2,1,0:T(8,128)(2,1)S(1)} %collective-permute-done.refs_1_) | copy-start | bytes 1204228
  45.6 12.0 %collective-permute-start.2 = (bf16[2,392,256]{2,1,0:T(8,128)(2,1)S(1)}, bf16[2,392,256]{2,1,0:T(8,128)(2,1)S(1)}, u32[]{:S(2)}, u32[]{:S(2)}) collective-permute-start(bf16[2,392,256]{2,1,0:T(8,128)(2,1)S(1)} %collective-permute-done.refs_1_), channel_id=1, source_target_pairs={{0,32},{32,64},{64,96},{96,128},{128,160},{160,192},{192,224},{224... | collective-permute-start | bytes 1204232 | tf_op jit(solution)/shard_map/ppermute | solution.py:37
  47.5 12.0 %copy-start.5 = (bf16[2,392,256]{2,1,0:T(8,128)(2,1)}, bf16[2,392,256]{2,1,0:T(8,128)(2,1)S(1)}, u32[]{:S(2)}) copy-start(bf16[2,392,256]{2,1,0:T(8,128)(2,1)S(1)} %collective-permute-done.1.refs_2_) | copy-start | bytes 1204228
  47.5 12.0 %collective-permute-start.3 = (bf16[2,392,256]{2,1,0:T(8,128)(2,1)S(1)}, bf16[2,392,256]{2,1,0:T(8,128)(2,1)S(1)}, u32[]{:S(2)}, u32[]{:S(2)}) collective-permute-start(bf16[2,392,256]{2,1,0:T(8,128)(2,1)S(1)} %collective-permute-done.1.refs_2_), channel_id=1, source_target_pairs={{0,224},{32,0},{64,32},{96,64},{128,96},{160,128},{192,160},{224,1... | collective-permute-start | bytes 1204232 | tf_op jit(solution)/shard_map/ppermute | solution.py:38
  57.6 15.1 %copy-start.6 = (bf16[2,392,256]{2,1,0:T(8,128)(2,1)}, bf16[2,392,256]{2,1,0:T(8,128)(2,1)S(1)}, u32[]{:S(2)}) copy-start(bf16[2,392,256]{2,1,0:T(8,128)(2,1)S(1)} %collective-permute-done.2.refs_3_) | copy-start | bytes 1204228
  57.6 13.1 %collective-permute-start.4 = (bf16[2,392,256]{2,1,0:T(8,128)(2,1)S(1)}, bf16[2,392,256]{2,1,0:T(8,128)(2,1)S(1)}, u32[]{:S(2)}, u32[]{:S(2)}) collective-permute-start(bf16[2,392,256]{2,1,0:T(8,128)(2,1)S(1)} %collective-permute-done.2.refs_3_), channel_id=1, source_target_pairs={{0,32},{32,64},{64,96},{96,128},{128,160},{160,192},{192,224},{224... | collective-permute-start | bytes 1204232 | tf_op jit(solution)/shard_map/ppermute | solution.py:37
  59.6 13.2 %copy-start.7 = (bf16[2,392,256]{2,1,0:T(8,128)(2,1)}, bf16[2,392,256]{2,1,0:T(8,128)(2,1)S(1)}, u32[]{:S(2)}) copy-start(bf16[2,392,256]{2,1,0:T(8,128)(2,1)S(1)} %collective-permute-done.3.refs_4_) | copy-start | bytes 1204228
  59.6 13.1 %collective-permute-start.5 = (bf16[2,392,256]{2,1,0:T(8,128)(2,1)S(1)}, bf16[2,392,256]{2,1,0:T(8,128)(2,1)S(1)}, u32[]{:S(2)}, u32[]{:S(2)}) collective-permute-start(bf16[2,392,256]{2,1,0:T(8,128)(2,1)S(1)} %collective-permute-done.3.refs_4_), channel_id=1, source_target_pairs={{0,224},{32,0},{64,32},{96,64},{128,96},{160,128},{192,160},{224,1... | collective-permute-start | bytes 1204232 | tf_op jit(solution)/shard_map/ppermute | solution.py:38
  70.7 17.4 %copy-start.2 = (bf16[2,392,256]{2,1,0:T(8,128)(2,1)}, bf16[2,392,256]{2,1,0:T(8,128)(2,1)S(1)}, u32[]{:S(2)}) copy-start(bf16[2,392,256]{2,1,0:T(8,128)(2,1)S(1)} %collective-permute-done.4.refs_5_) | copy-start | bytes 1204228
  70.8 8.8 %collective-permute-start.6 = (bf16[1,392,256]{2,1,0:T(8,128)(2,1)S(1)}, bf16[1,392,256]{2,1,0:T(8,128)(2,1)S(1)}, u32[]{:S(2)}, u32[]{:S(2)}) collective-permute-start(bf16[1,392,256]{2,1,0:T(8,128)(2,1)S(1)} %slice.66), channel_id=1, source_target_pairs={{0,32},{32,64},{64,96},{96,128},{128,160},{160,192},{192,224},{224... | collective-permute-start | bytes 602120 | tf_op jit(solution)/shard_map/ppermute | solution.py:40
  72.7 15.5 %copy-start.3 = (bf16[2,392,256]{2,1,0:T(8,128)(2,1)}, bf16[2,392,256]{2,1,0:T(8,128)(2,1)S(1)}, u32[]{:S(2)}) copy-start(bf16[2,392,256]{2,1,0:T(8,128)(2,1)S(1)} %collective-permute-done.5.refs_6_) | copy-start | bytes 1204228
  72.7 8.7 %collective-permute-start.7 = (bf16[1,392,256]{2,1,0:T(8,128)(2,1)S(1)}, bf16[1,392,256]{2,1,0:T(8,128)(2,1)S(1)}, u32[]{:S(2)}, u32[]{:S(2)}) collective-permute-start(bf16[1,392,256]{2,1,0:T(8,128)(2,1)S(1)} %slice.68), channel_id=1, source_target_pairs={{0,224},{32,0},{64,32},{96,64},{128,96},{160,128},{192,160},{224,1... | collective-permute-start | bytes 602120 | tf_op jit(solution)/shard_map/ppermute | solution.py:41
  82.1 4.9 %collective-permute-start.8 = (bf16[16,128,256]{2,1,0:T(8,128)(2,1)}, bf16[16,128,256]{2,1,0:T(8,128)(2,1)}, u32[]{:S(2)}, u32[]{:S(2)}) collective-permute-start(bf16[16,128,256]{2,1,0:T(8,128)(2,1)} %slice_dynamic-update-slice_fusion.7), channel_id=1, source_target_pairs={{0,1},{1,0},{2,3},{3,2},{4,5},{5,4},{6,7},{7,6},{8,9},{9,8},{10,11... | collective-permute-start | bytes 3145736 | tf_op jit(solution)/shard_map/ppermute | solution.py:414
  94.1 10.5 %collective-permute-start.9 = (bf16[8,512]{1,0:T(8,128)(2,1)S(1)}, bf16[8,512]{1,0:T(8,128)(2,1)S(1)}, u32[]{:S(2)}, u32[]{:S(2)}) collective-permute-start(bf16[8,512]{1,0:T(8,128)(2,1)S(1)} %slice.56), channel_id=1, source_target_pairs={{0,32},{32,64},{64,96},{96,128},{128,160},{160,192},{192,224},{224... | collective-permute-start | bytes 24584 | tf_op jit(solution)/shard_map/ppermute | solution.py:30
  110.2 5.2 %collective-permute-start.10 = (bf16[144,256]{1,0:T(8,128)(2,1)S(1)}, bf16[144,256]{1,0:T(8,128)(2,1)S(1)}, u32[]{:S(2)}, u32[]{:S(2)}) collective-permute-start(bf16[144,256]{1,0:T(8,128)(2,1)S(1)} %get-tuple-element.22.own_ref), channel_id=1, source_target_pairs={{224,256},{225,257},{226,258},{227,259},{228,260},{229,261},{230,2... | collective-permute-start | bytes 221192 | tf_op jit(solution)/shard_map/ppermute | solution.py:428
  (3 other events, 16.5 us)
Sparse Core Ops, SparseCore 0:
  9.5 75.6 all-gather.5
  87.2 50.3 all-gather.7

commit v4 on v3

--- a/solution.py
+++ b/solution.py
@@ -20,6 +20,7 @@
 BF16 = jnp.bfloat16
 MIB = 1024 * 1024
 FAR = -1e30
+CHUNK = 1024
 
 
 def ring(count, step):
@@ -106,8 +107,23 @@
     ).astype(BF16)
 
 
-def rest_kernel(tok_ref, w_ref, _, out_ref):
-    project(tok_ref, w_ref, out_ref)
+def rest_kernel(tok_ref, w_ref, _, out_ref, total):
+    step = pl.program_id(0)
+    part = jnp.dot(
+        tok_ref[...], w_ref[pl.ds(step * CHUNK, CHUNK), :], preferred_element_type=F32
+    )
+
+    @pl.when(step == 0)
+    def _():
+        total[...] = part
+
+    @pl.when(step > 0)
+    def _():
+        total[...] += part
+
+    @pl.when(step == pl.num_programs(0) - 1)
+    def _():
+        out_ref[...] = total[...].astype(BF16)
 
 
 def spread(columns):
@@ -236,9 +252,32 @@
 
 def finish_kernel(
     scalars, before_ref, shards_ref, act_ref, y_ref, reach_ref, tok_ref, w_ref, out_ref,
-    entering, weights,
+    total, weights,
 ):
-    @pl.when(pl.program_id(0) == 0)
+    step = pl.program_id(0)
+
+    @pl.when(step == 0)
+    def _():
+        for k in range(Z):
+            for slot in range(YH):
+                row = ((scalars[2] + slot) % YH * Z + k) * 256
+                weights[pl.ds(pl.multiple_of(row, 256), 256), :] = w_ref[k, slot]
+
+    part = jnp.dot(
+        tok_ref[...],
+        weights[pl.ds(pl.multiple_of(step * CHUNK, CHUNK), CHUNK), :],
+        preferred_element_type=F32,
+    )
+
+    @pl.when(step == 0)
+    def _():
+        total[...] = part
+
+    @pl.when(step > 0)
+    def _():
+        total[...] += part
+
+    @pl.when(step == pl.num_programs(0) - 1)
     def _():
         z = scalars[0]
         state = jnp.zeros((STATE, 256), F32)
@@ -246,15 +285,10 @@
             piece = shards_ref[k]
             later = gain_of(piece)[0:1] * state + piece[0:STATE].astype(F32)
             state = jnp.where(k < z, later, state)
-        entering[...] = (state + before_ref[0:STATE, :].astype(F32)).astype(BF16)
-        for k in range(Z):
-            for yh in range(YH):
-                weights[pl.ds((yh * Z + k) * 256, 256), :] = w_ref[k, yh]
-
-    gate = jnp.dot(tok_ref[...], weights[...], preferred_element_type=F32).astype(BF16)
-    carried = jnp.dot(act_ref[...], entering[...], preferred_element_type=F32)
-    total = y_ref[...] + reach_ref[...] * carried
-    out_ref[...] = (total * jax.nn.silu(gate.astype(F32))).astype(BF16)
+        entering = (state + before_ref[0:STATE, :].astype(F32)).astype(BF16)
+        carried = jnp.dot(act_ref[...], entering, preferred_element_type=F32)
+        gate = total[...].astype(BF16).astype(F32)
+        out_ref[...] = ((y_ref[...] + reach_ref[...] * carried) * jax.nn.silu(gate)).astype(BF16)
 
 
 def shape(dims, dtype):
@@ -284,14 +318,19 @@
 
 def run_rest(gathered, weights, proj):
     rows, depth = gathered.shape
-    count = rows // BLOCK - 1
+    count = rows - BLOCK
     return call(
         rest_kernel,
-        (count,),
-        [rows_of((BLOCK, depth)), held(weights), pl.BlockSpec(memory_space=pl.ANY)],
-        rows_of((BLOCK, 640)),
+        (depth // CHUNK,),
+        [
+            pl.BlockSpec((count, CHUNK), lambda k: (0, k)),
+            held(weights),
+            pl.BlockSpec(memory_space=pl.ANY),
+        ],
+        pl.BlockSpec((count, 640), lambda k: (0, 0)),
         shape((rows, 640), BF16),
-        cost=work(2 * count * BLOCK * depth * 640, 8 << 20),
+        scratch=[pltpu.VMEM((count, 640), F32)],
+        cost=work(2 * count * depth * 640, 8 << 20),
         room=16,
         aliases={2: 0},
     )(gathered, weights, proj)
@@ -366,22 +405,22 @@
     rows, depth = gathered.shape
     return call(
         finish_kernel,
-        (rows // BLOCK,),
+        (depth // CHUNK,),
         [
             held(before),
             held(shards),
-            pl.BlockSpec((BLOCK, 128), lambda i, *_: (i, 3)),
-            rows_of((BLOCK, 256)),
-            rows_of((BLOCK, 256)),
-            rows_of((BLOCK, depth)),
+            pl.BlockSpec((rows, 128), lambda *_: (0, 3)),
+            whole((rows, 256)),
+            whole((rows, 256)),
+            pl.BlockSpec((rows, CHUNK), lambda k, *_: (0, k)),
             whole(gate_all.shape),
         ],
-        rows_of((BLOCK, 256)),
+        whole((rows, 256)),
         shape((rows, 256), BF16),
-        scratch=[pltpu.VMEM((STATE, 256), BF16), pltpu.VMEM((depth, 256), BF16)],
+        scratch=[pltpu.VMEM((rows, 256), F32), pltpu.VMEM((depth, 256), BF16)],
         prefetch=1,
         cost=work(2 * rows * (128 + depth) * 256, 13 << 20),
-        room=20,
+        room=28,
     )(scalars, before, shards, act, y, reach, gathered, gate_all)
 
 
@@ -407,13 +446,16 @@
     state_half = lax.dynamic_slice(state_weight, (group, core * 128, 0), (1, 128, 256))[0]
     conv_own = lax.dynamic_index_in_dim(state_conv, group, 0, keepdims=False)
     step_rows = jnp.pad(step_weight.T, ((0, 8 - heads_here), (0, 0)))
-    pack = jnp.concatenate([value_weight, state_half, step_rows, gate_weight], axis=0)
+    pack = jnp.concatenate([value_weight, state_half, step_rows], axis=0)
     both = lax.all_gather(pack, "yh", axis=0, tiled=False)
-    pieces = ring_gather(both[:, :392])
+    pieces = ring_gather(both)
+    gate_own, _ = lax.optimization_barrier((gate_weight, pieces[2][2]))
+    gate_far = lax.ppermute(gate_own, "yh", ring(YH, 1))
     halves = jnp.concatenate([piece[:, 256:384] for _, _, piece in pieces], axis=0)
     halves = lax.ppermute(halves, "c", [(0, 1), (1, 0)])
-    scalars = jnp.stack([z, core]).astype(jnp.int32)
-    gate_part, gathered, halves = lax.optimization_barrier((both[:, 392:], gathered, halves))
+    scalars = jnp.stack([z, core, lax.axis_index("yh")]).astype(jnp.int32)
+    gate_part = jnp.stack([gate_own, gate_far])
+    gate_part, gathered, halves = lax.optimization_barrier((gate_part, gathered, halves))
     gate_all = lax.all_gather(gate_part, "z", axis=0, tiled=False)
     gathered = in_hbm(gathered)
     proj, weights = run_first(gathered, pieces, halves, scalars)

time: 170 us -> 175 us (1.029)
  the two profiles are of different devices: /device:TPU:6 before, /device:TPU:62 now
where the time goes in v4:
time: 175 us
  blocking collectives  41.6 us (24%)
  starting transfers between devices  41.1 us (23%)
  waiting for transfers between devices  35.8 us (20%)
  Pallas kernels  33.1 us (19%)
  between operations  13.8 us (8%)
  local copies, waits for them, and re-layouts  7.33 us (4%)
  other arithmetic  1.92 us (1%)
    all_gather x1, blocking collectives, local(): shards = lax.all_gather(carried, 'z', axis=0, tiled=False)  25.8 us
    ppermute x3, starting transfers between devices, ring_gather(): left = lax.ppermute(left, 'z', ring(Z, -1))  18.9 us
    all_gather x1, blocking collectives, local(): both = lax.all_gather(pack, 'yh', axis=0, tiled=False)  15.8 us
    ppermute x3, waiting for transfers between devices, ring_gather(): right = lax.ppermute(right, 'z', ring(Z, 1))  15.8 us
    ppermute x1, waiting for transfers between devices, local(): gate_far = lax.ppermute(gate_own, 'yh', ring(YH, 1))  9.77 us
    pallas_call x1, Pallas kernels, run_finish(): call(finish_kernel, (depth // CHUNK,), [held(before), held(shards), pl.Bl...  9.08 us
    ppermute x3, starting transfers between devices, ring_gather(): right = lax.ppermute(right, 'z', ring(Z, 1))  8.09 us
    pallas_call x1, Pallas kernels, run_rest(): call(rest_kernel, (depth // CHUNK,), [pl.BlockSpec((count, CHUNK), lambda...  7.94 us
  transfers between devices with their start and end apart: 14, of which 8 were waited for; matrix products, arithmetic and copies ran while one was open for 5% of the time, Pallas kernels for 14%

profile of v4, /device:TPU:62, one launch (start us, length us, event | category | flops | bytes accessed | tf_op | source)
XLA Modules:
  0.0 174.5 jit_solution(2461578292540923545)
XLA Ops:
  8.8 15.8 %all-gather = bf16[784,256]{1,0:T(8,128)(2,1)S(1)} all-gather(bf16[392,256]{1,0:T(8,128)(2,1)S(1)} %fusion.1), channel_id=2, replica_groups=mesh['yh'=2,'z'=8,'x'=4,'y'=4,'c'=2] {'yh'}, dimensions={0}, use_global_device_ids=true | all-gather | bytes 602112 | tf_op jit(solution)/shard_map/all_gather | solution.py:450
  24.5 4.3 %collective-permute-start.2 = (bf16[2,392,256]{2,1,0:T(8,128)(2,1)S(1)}, bf16[2,392,256]{2,1,0:T(8,128)(2,1)S(1)}, u32[]{:S(2)}, u32[]{:S(2)}) collective-permute-start(bf16[2,392,256]{2,1,0:T(8,128)(2,1)S(1)} %bitcast.18), channel_id=1, source_target_pairs={{0,32},{32,64},{64,96},{96,128},{128,160},{160,192},{192,224},{224... | collective-permute-start | bytes 1204232 | tf_op jit(solution)/shard_map/ppermute | solution.py:38
  28.8 8.6 %collective-permute-start = (bf16[2,392,256]{2,1,0:T(8,128)(2,1)S(1)}, bf16[2,392,256]{2,1,0:T(8,128)(2,1)S(1)}, u32[]{:S(2)}, u32[]{:S(2)}) collective-permute-start(bf16[2,392,256]{2,1,0:T(8,128)(2,1)S(1)} %bitcast.19), channel_id=1, source_target_pairs={{0,224},{32,0},{64,32},{96,64},{128,96},{160,128},{192,160},{224,1... | collective-permute-start | bytes 1204232 | tf_op jit(solution)/shard_map/ppermute | solution.py:39
  38.1 6.6 %collective-permute-done.2.refs_1_ = bf16[2,392,256]{2,1,0:T(8,128)(2,1)S(1)} collective-permute-done((bf16[2,392,256]{2,1,0:T(8,128)(2,1)S(1)}, bf16[2,392,256]{2,1,0:T(8,128)(2,1)S(1)}, u32[]{:S(2)}, u32[]{:S(2)}) %collective-permute-start.2) | collective-permute-done | bytes 401440 | tf_op jit(solution)/shard_map/ppermute | solution.py:38
  44.7 1.9 %collective-permute-start.3 = (bf16[2,392,256]{2,1,0:T(8,128)(2,1)S(1)}, bf16[2,392,256]{2,1,0:T(8,128)(2,1)S(1)}, u32[]{:S(2)}, u32[]{:S(2)}) collective-permute-start(bf16[2,392,256]{2,1,0:T(8,128)(2,1)S(1)} %collective-permute-done.2.refs_1_), channel_id=1, source_target_pairs={{0,32},{32,64},{64,96},{96,128},{128,160},{160,192},{192,224},{224... | collective-permute-start | bytes 1204232 | tf_op jit(solution)/shard_map/ppermute | solution.py:38
  46.6 5.1 %collective-permute-start.4 = (bf16[2,392,256]{2,1,0:T(8,128)(2,1)S(1)}, bf16[2,392,256]{2,1,0:T(8,128)(2,1)S(1)}, u32[]{:S(2)}, u32[]{:S(2)}) collective-permute-start(bf16[2,392,256]{2,1,0:T(8,128)(2,1)S(1)} %collective-permute-done.refs_2_), channel_id=1, source_target_pairs={{0,224},{32,0},{64,32},{96,64},{128,96},{160,128},{192,160},{224,1... | collective-permute-start | bytes 1204232 | tf_op jit(solution)/shard_map/ppermute | solution.py:39
  53.1 5.0 %collective-permute-done.3.refs_3_ = bf16[2,392,256]{2,1,0:T(8,128)(2,1)S(1)} collective-permute-done((bf16[2,392,256]{2,1,0:T(8,128)(2,1)S(1)}, bf16[2,392,256]{2,1,0:T(8,128)(2,1)S(1)}, u32[]{:S(2)}, u32[]{:S(2)}) %collective-permute-start.3) | collective-permute-done | bytes 401440 | tf_op jit(solution)/shard_map/ppermute | solution.py:38
  58.2 1.9 %collective-permute-start.5 = (bf16[2,392,256]{2,1,0:T(8,128)(2,1)S(1)}, bf16[2,392,256]{2,1,0:T(8,128)(2,1)S(1)}, u32[]{:S(2)}, u32[]{:S(2)}) collective-permute-start(bf16[2,392,256]{2,1,0:T(8,128)(2,1)S(1)} %collective-permute-done.3.refs_3_), channel_id=1, source_target_pairs={{0,32},{32,64},{64,96},{96,128},{128,160},{160,192},{192,224},{224... | collective-permute-start | bytes 1204232 | tf_op jit(solution)/shard_map/ppermute | solution.py:38
  60.1 5.1 %collective-permute-start.6 = (bf16[2,392,256]{2,1,0:T(8,128)(2,1)S(1)}, bf16[2,392,256]{2,1,0:T(8,128)(2,1)S(1)}, u32[]{:S(2)}, u32[]{:S(2)}) collective-permute-start(bf16[2,392,256]{2,1,0:T(8,128)(2,1)S(1)} %collective-permute-done.4.refs_4_), channel_id=1, source_target_pairs={{0,224},{32,0},{64,32},{96,64},{128,96},{160,128},{192,160},{224,1... | collective-permute-start | bytes 1204232 | tf_op jit(solution)/shard_map/ppermute | solution.py:39
  66.6 4.1 %collective-permute-done.5.refs_5_ = bf16[2,392,256]{2,1,0:T(8,128)(2,1)S(1)} collective-permute-done((bf16[2,392,256]{2,1,0:T(8,128)(2,1)S(1)}, bf16[2,392,256]{2,1,0:T(8,128)(2,1)S(1)}, u32[]{:S(2)}, u32[]{:S(2)}) %collective-permute-start.5) | collective-permute-done | bytes 401440 | tf_op jit(solution)/shard_map/ppermute | solution.py:38
  70.7 1.9 %collective-permute-start.7 = (bf16[1,392,256]{2,1,0:T(8,128)(2,1)S(1)}, bf16[1,392,256]{2,1,0:T(8,128)(2,1)S(1)}, u32[]{:S(2)}, u32[]{:S(2)}) collective-permute-start(bf16[1,392,256]{2,1,0:T(8,128)(2,1)S(1)} %slice.55), channel_id=1, source_target_pairs={{0,32},{32,64},{64,96},{96,128},{128,160},{160,192},{192,224},{224... | collective-permute-start | bytes 602120 | tf_op jit(solution)/shard_map/ppermute | solution.py:41
  72.7 5.1 %collective-permute-start.8 = (bf16[1,392,256]{2,1,0:T(8,128)(2,1)S(1)}, bf16[1,392,256]{2,1,0:T(8,128)(2,1)S(1)}, u32[]{:S(2)}, u32[]{:S(2)}) collective-permute-start(bf16[1,392,256]{2,1,0:T(8,128)(2,1)S(1)} %slice.57), channel_id=1, source_target_pairs={{0,224},{32,0},{64,32},{96,64},{128,96},{160,128},{192,160},{224,1... | collective-permute-start | bytes 602120 | tf_op jit(solution)/shard_map/ppermute | solution.py:42
  81.8 1.9 %collective-permute-start.9 = (bf16[16,128,256]{2,1,0:T(8,128)(2,1)}, bf16[16,128,256]{2,1,0:T(8,128)(2,1)}, u32[]{:S(2)}, u32[]{:S(2)}) collective-permute-start(bf16[16,128,256]{2,1,0:T(8,128)(2,1)} %slice_dynamic-update-slice_fusion.7), channel_id=1, source_target_pairs={{0,1},{1,0},{2,3},{3,2},{4,5},{5,4},{6,7},{7,6},{8,9},{9,8},{10,11... | collective-permute-start | bytes 3145736 | tf_op jit(solution)/shard_map/ppermute | solution.py:455
  83.7 1.9 %collective-permute-start.1 = (bf16[256,256]{1,0:T(8,128)(2,1)S(1)}, bf16[256,256]{1,0:T(8,128)(2,1)S(1)}, u32[]{:S(2)}, u32[]{:S(2)}) collective-permute-start(bf16[256,256]{1,0:T(8,128)(2,1)S(1)} %copy-done.10), channel_id=1, source_target_pairs={{0,256},{256,0},{1,257},{257,1},{2,258},{258,2},{3,259},{259,3},{4... | collective-permute-start | bytes 393224 | tf_op jit(solution)/shard_map/ppermute | solution.py:453
  85.6 9.8 %collective-permute-done.1 = bf16[256,256]{1,0:T(8,128)(2,1)S(1)} collective-permute-done((bf16[256,256]{1,0:T(8,128)(2,1)S(1)}, bf16[256,256]{1,0:T(8,128)(2,1)S(1)}, u32[]{:S(2)}, u32[]{:S(2)}) %collective-permute-start.1) | collective-permute-done | bytes 131104 | tf_op jit(solution)/shard_map/ppermute | solution.py:453
  97.3 5.9 %shard_map.100 = (bf16[1024,640]{1,0:T(8,128)(2,1)S(1)}, bf16[4096,640]{1,0:T(8,128)(2,1)S(1)}) custom-call(s32[3]{0:T(128)S(1)} %pad_add_fusion.scalars, bf16[1024,4096]{1,0:T(8,128)(2,1)} %all-gather.6.cloned.1.call-done.tok_ref, bf16[2,392,256]{2,1,0:T(8,128)(2,1)} %bitcast.21, bf16[2,392,256]{2,1,0:T(8,128)(2,1)} %copy-done.4, ...), custom_call_target="tpu_custom_call" | custom-call | flops 1342177280 | bytes 12582912 | tf_op jit(solution)/shard_map/pallas_call | solution.py:307
  103.2 1.9 %collective-permute-start.10 = (bf16[8,512]{1,0:T(8,128)(2,1)S(1)}, bf16[8,512]{1,0:T(8,128)(2,1)S(1)}, u32[]{:S(2)}, u32[]{:S(2)}) collective-permute-start(bf16[8,512]{1,0:T(8,128)(2,1)S(1)} %slice.47), channel_id=1, source_target_pairs={{0,32},{32,64},{64,96},{96,128},{128,160},{160,192},{192,224},{224... | collective-permute-start | bytes 24584 | tf_op jit(solution)/shard_map/ppermute | solution.py:31
  105.1 7.9 %shard_map.101.proj_ref = bf16[1024,640]{1,0:T(8,128)(2,1)S(1)} custom-call(bf16[1024,4096]{1,0:T(8,128)(2,1)} %all-gather.6.cloned.1.call-done.tok_ref, bf16[4096,640]{1,0:T(8,128)(2,1)S(1)} %get-tuple-element.22.w_ref, bf16[1024,640]{1,0:T(8,128)(2,1)S(1)} %get-tuple-element.23._), custom_call_target="tpu_custom_call", output_to_operand_aliasing={{}: (2, {})} | custom-call | flops 4026531840 | bytes 8388608 | tf_op jit(solution)/shard_map/pallas_call | solution.py:322
  113.0 1.8 %collective-permute-done.10.rim_ref = bf16[8,512]{1,0:T(8,128)(2,1)S(1)} collective-permute-done((bf16[8,512]{1,0:T(8,128)(2,1)S(1)}, bf16[8,512]{1,0:T(8,128)(2,1)S(1)}, u32[]{:S(2)}, u32[]{:S(2)}) %collective-permute-start.10) | collective-permute-done | bytes 8224 | tf_op jit(solution)/shard_map/ppermute | solution.py:31
  114.8 5.6 %shard_map.102 = (bf16[1024,512]{1,0:T(8,128)(2,1)S(1)}, f32[1024,128]{1,0:T(8,128)S(1)}, f32[1024,128]{1,0:T(8,128)S(1)}, f32[4,128,256]{2,1,0:T(8,128)S(1)}, f...) custom-call(s32[16]{0:T(128)S(1)} %sub.7.starts, s32[1]{0:T(128)} %bitcast.4.base, ...), custom_call_target="tpu_custom_call" | custom-call | flops 67108864 | bytes 4194304 | tf_op jit(solution)/shard_map/pallas_call | solution.py:342
  121.8 4.6 %shard_map.104 = (f32[1024,256]{1,0:T(8,128)}, f32[1024,256]{1,0:T(8,128)}) custom-call(s32[16]{0:T(128)S(1)} %sub.7.starts, s32[1]{0:T(128)} %bitcast.4.base, bf16[1024,512]{1,0:T(8,128)(2,1)S(1)} %get-tuple-element.25.act_ref, f32[1024,128]{1,0:T(8,128)S(1)} %get-tuple-element.26.cum_ref, f32[1024,128]{1,0:T(8,128)S(1)} %get-tuple-element.27.step_ref, ...), custom_call_target="tpu_custom_call" | custom-call | flops 536870912 | bytes 5242880 | tf_op jit(solution)/shard_map/pallas_call | solution.py:375
  126.3 6.5 %collective-permute-done.11.before_ref = bf16[144,256]{1,0:T(8,128)(2,1)S(1)} collective-permute-done((bf16[144,256]{1,0:T(8,128)(2,1)S(1)}, bf16[144,256]{1,0:T(8,128)(2,1)S(1)}, u32[]{:S(2)}, u32[]{:S(2)}) %collective-permute-start.11) | collective-permute-done | bytes 73760 | tf_op jit(solution)/shard_map/ppermute | solution.py:470
  132.9 25.8 %all-gather.1 = bf16[1152,256]{1,0:T(8,128)(2,1)S(1)} all-gather(bf16[144,256]{1,0:T(8,128)(2,1)S(1)} %shard_map.103), channel_id=3, replica_groups=mesh['yh'=2,'z'=8,'x'=4,'y'=4,'c'=2] {'z'}, dimensions={0}, use_global_device_ids=true | all-gather | bytes 663552 | tf_op jit(solution)/shard_map/all_gather | solution.py:473
  158.6 9.1 %shard_map.105 = bf16[1024,256]{1,0:T(8,128)(2,1)} custom-call(s32[3]{0:T(128)S(1)} %pad_add_fusion.scalars, bf16[144,256]{1,0:T(8,128)(2,1)S(1)} %collective-permute-done.11.before_ref, bf16[8,144,256]{2,1,0:T(8,128)(2,1)S(1)} %bitcast.17, bf16[1024,512]{1,0:T(8,128)(2,1)S(1)} %get-tuple-element.25.act_ref, f32[1024,256]{1,0:T(8,128)} %get-tuple-element.30.y_ref, ...), custom_call_target="tpu_custom_call" | custom-call | flops 2214592512 | bytes 13631488 | tf_op jit(solution)/shard_map/pallas_call | solution.py:406
  (67 shorter events, 12.6 us)
Async XLA Ops:
  6.5 89.6 %all-gather.6.cloned.1.call-start = ((), (), s32[]{:S(2)}) async-start(), calls=%async_computation | async-start | bytes 8650752 | tf_op jit(solution)/shard_map/all_gather | solution.py:444
  7.3 76.4 %copy-start.10 = (bf16[256,256]{1,0:T(8,128)(2,1)S(1)}, bf16[256,256]{1,0:T(8,128)(2,1)}, u32[]{:S(2)}) copy-start(bf16[256,256]{1,0:T(8,128)(2,1)} %param.13) | copy-start | bytes 393220
  7.3 151.4 %all-gather.8.cloned.1.call-start = ((), (), s32[]{:S(2)}) async-start(), calls=%async_computation.1 | async-start | bytes 2359296 | tf_op jit(solution)/shard_map/all_gather | solution.py:459
  8.7 87.4 %copy-start.12 = (s32[16]{0:T(128)S(1)}, s32[16]{0:T(128)}, u32[]{:S(2)}) copy-start(s32[16]{0:T(128)} %param.11) | copy-start | bytes 196
  8.7 88.5 %copy-start.13 = (f32[4]{0:T(128)S(1)}, f32[4]{0:T(128)}, u32[]{:S(2)}) copy-start(f32[4]{0:T(128)} %param.19) | copy-start | bytes 52
  8.7 88.5 %copy-start.14 = (f32[4]{0:T(128)S(1)}, f32[4]{0:T(128)}, u32[]{:S(2)}) copy-start(f32[4]{0:T(128)} %param.18) | copy-start | bytes 52
  8.7 88.5 %copy-start.11 = (f32[4,256]{1,0:T(4,128)S(1)}, f32[4,256]{1,0:T(4,128)}, u32[]{:S(2)}) copy-start(f32[4,256]{1,0:T(4,128)} %param.16) | copy-start | bytes 12292
  24.5 72.7 %copy-start.1 = (bf16[784,256]{1,0:T(8,128)(2,1)}, bf16[784,256]{1,0:T(8,128)(2,1)S(1)}, u32[]{:S(2)}) copy-start(bf16[784,256]{1,0:T(8,128)(2,1)S(1)} %all-gather) | copy-start | bytes 1204228
  24.5 20.1 %collective-permute-start.2 = (bf16[2,392,256]{2,1,0:T(8,128)(2,1)S(1)}, bf16[2,392,256]{2,1,0:T(8,128)(2,1)S(1)}, u32[]{:S(2)}, u32[]{:S(2)}) collective-permute-start(bf16[2,392,256]{2,1,0:T(8,128)(2,1)S(1)} %bitcast.18), channel_id=1, source_target_pairs={{0,32},{32,64},{64,96},{96,128},{128,160},{160,192},{192,224},{224... | collective-permute-start | bytes 1204232 | tf_op jit(solution)/shard_map/ppermute | solution.py:38
  28.8 17.8 %collective-permute-start = (bf16[2,392,256]{2,1,0:T(8,128)(2,1)S(1)}, bf16[2,392,256]{2,1,0:T(8,128)(2,1)S(1)}, u32[]{:S(2)}, u32[]{:S(2)}) collective-permute-start(bf16[2,392,256]{2,1,0:T(8,128)(2,1)S(1)} %bitcast.19), channel_id=1, source_target_pairs={{0,224},{32,0},{64,32},{96,64},{128,96},{160,128},{192,160},{224,1... | collective-permute-start | bytes 1204232 | tf_op jit(solution)/shard_map/ppermute | solution.py:39
  44.7 52.5 %copy-start.4 = (bf16[2,392,256]{2,1,0:T(8,128)(2,1)}, bf16[2,392,256]{2,1,0:T(8,128)(2,1)S(1)}, u32[]{:S(2)}) copy-start(bf16[2,392,256]{2,1,0:T(8,128)(2,1)S(1)} %collective-permute-done.2.refs_1_) | copy-start | bytes 1204228
  44.7 13.5 %collective-permute-start.3 = (bf16[2,392,256]{2,1,0:T(8,128)(2,1)S(1)}, bf16[2,392,256]{2,1,0:T(8,128)(2,1)S(1)}, u32[]{:S(2)}, u32[]{:S(2)}) collective-permute-start(bf16[2,392,256]{2,1,0:T(8,128)(2,1)S(1)} %collective-permute-done.2.refs_1_), channel_id=1, source_target_pairs={{0,32},{32,64},{64,96},{96,128},{128,160},{160,192},{192,224},{224... | collective-permute-start | bytes 1204232 | tf_op jit(solution)/shard_map/ppermute | solution.py:38
  46.6 13.5 %collective-permute-start.4 = (bf16[2,392,256]{2,1,0:T(8,128)(2,1)S(1)}, bf16[2,392,256]{2,1,0:T(8,128)(2,1)S(1)}, u32[]{:S(2)}, u32[]{:S(2)}) collective-permute-start(bf16[2,392,256]{2,1,0:T(8,128)(2,1)S(1)} %collective-permute-done.refs_2_), channel_id=1, source_target_pairs={{0,224},{32,0},{64,32},{96,64},{128,96},{160,128},{192,160},{224,1... | collective-permute-start | bytes 1204232 | tf_op jit(solution)/shard_map/ppermute | solution.py:39
  58.2 12.5 %collective-permute-start.5 = (bf16[2,392,256]{2,1,0:T(8,128)(2,1)S(1)}, bf16[2,392,256]{2,1,0:T(8,128)(2,1)S(1)}, u32[]{:S(2)}, u32[]{:S(2)}) collective-permute-start(bf16[2,392,256]{2,1,0:T(8,128)(2,1)S(1)} %collective-permute-done.3.refs_3_), channel_id=1, source_target_pairs={{0,32},{32,64},{64,96},{96,128},{128,160},{160,192},{192,224},{224... | collective-permute-start | bytes 1204232 | tf_op jit(solution)/shard_map/ppermute | solution.py:38
  60.1 12.6 %collective-permute-start.6 = (bf16[2,392,256]{2,1,0:T(8,128)(2,1)S(1)}, bf16[2,392,256]{2,1,0:T(8,128)(2,1)S(1)}, u32[]{:S(2)}, u32[]{:S(2)}) collective-permute-start(bf16[2,392,256]{2,1,0:T(8,128)(2,1)S(1)} %collective-permute-done.4.refs_4_), channel_id=1, source_target_pairs={{0,224},{32,0},{64,32},{96,64},{128,96},{160,128},{192,160},{224,1... | collective-permute-start | bytes 1204232 | tf_op jit(solution)/shard_map/ppermute | solution.py:39
  70.7 26.5 %copy-start.2 = (bf16[2,392,256]{2,1,0:T(8,128)(2,1)}, bf16[2,392,256]{2,1,0:T(8,128)(2,1)S(1)}, u32[]{:S(2)}) copy-start(bf16[2,392,256]{2,1,0:T(8,128)(2,1)S(1)} %collective-permute-done.5.refs_5_) | copy-start | bytes 1204228
  70.7 8.8 %collective-permute-start.7 = (bf16[1,392,256]{2,1,0:T(8,128)(2,1)S(1)}, bf16[1,392,256]{2,1,0:T(8,128)(2,1)S(1)}, u32[]{:S(2)}, u32[]{:S(2)}) collective-permute-start(bf16[1,392,256]{2,1,0:T(8,128)(2,1)S(1)} %slice.55), channel_id=1, source_target_pairs={{0,32},{32,64},{64,96},{96,128},{128,160},{160,192},{192,224},{224... | collective-permute-start | bytes 602120 | tf_op jit(solution)/shard_map/ppermute | solution.py:41
  72.7 24.6 %copy-start.3 = (bf16[2,392,256]{2,1,0:T(8,128)(2,1)}, bf16[2,392,256]{2,1,0:T(8,128)(2,1)S(1)}, u32[]{:S(2)}) copy-start(bf16[2,392,256]{2,1,0:T(8,128)(2,1)S(1)} %collective-permute-done.6.refs_6_) | copy-start | bytes 1204228
  72.7 8.4 %collective-permute-start.8 = (bf16[1,392,256]{2,1,0:T(8,128)(2,1)S(1)}, bf16[1,392,256]{2,1,0:T(8,128)(2,1)S(1)}, u32[]{:S(2)}, u32[]{:S(2)}) collective-permute-start(bf16[1,392,256]{2,1,0:T(8,128)(2,1)S(1)} %slice.57), channel_id=1, source_target_pairs={{0,224},{32,0},{64,32},{96,64},{128,96},{160,128},{192,160},{224,1... | collective-permute-start | bytes 602120 | tf_op jit(solution)/shard_map/ppermute | solution.py:42
  79.5 17.7 %copy-start.8 = (bf16[1,392,256]{2,1,0:T(8,128)(2,1)}, bf16[1,392,256]{2,1,0:T(8,128)(2,1)S(1)}, u32[]{:S(2)}) copy-start(bf16[1,392,256]{2,1,0:T(8,128)(2,1)S(1)} %collective-permute-done.7.refs_7_) | copy-start | bytes 602116
  81.8 14.4 %collective-permute-start.9 = (bf16[16,128,256]{2,1,0:T(8,128)(2,1)}, bf16[16,128,256]{2,1,0:T(8,128)(2,1)}, u32[]{:S(2)}, u32[]{:S(2)}) collective-permute-start(bf16[16,128,256]{2,1,0:T(8,128)(2,1)} %slice_dynamic-update-slice_fusion.7), channel_id=1, source_target_pairs={{0,1},{1,0},{2,3},{3,2},{4,5},{5,4},{6,7},{7,6},{8,9},{9,8},{10,11... | collective-permute-start | bytes 3145736 | tf_op jit(solution)/shard_map/ppermute | solution.py:455
  83.7 11.7 %collective-permute-start.1 = (bf16[256,256]{1,0:T(8,128)(2,1)S(1)}, bf16[256,256]{1,0:T(8,128)(2,1)S(1)}, u32[]{:S(2)}, u32[]{:S(2)}) collective-permute-start(bf16[256,256]{1,0:T(8,128)(2,1)S(1)} %copy-done.10), channel_id=1, source_target_pairs={{0,256},{256,0},{1,257},{257,1},{2,258},{258,2},{3,259},{259,3},{4... | collective-permute-start | bytes 393224 | tf_op jit(solution)/shard_map/ppermute | solution.py:453
  103.2 11.7 %collective-permute-start.10 = (bf16[8,512]{1,0:T(8,128)(2,1)S(1)}, bf16[8,512]{1,0:T(8,128)(2,1)S(1)}, u32[]{:S(2)}, u32[]{:S(2)}) collective-permute-start(bf16[8,512]{1,0:T(8,128)(2,1)S(1)} %slice.47), channel_id=1, source_target_pairs={{0,32},{32,64},{64,96},{96,128},{128,160},{160,192},{192,224},{224... | collective-permute-start | bytes 24584 | tf_op jit(solution)/shard_map/ppermute | solution.py:31
  120.5 12.4 %collective-permute-start.11 = (bf16[144,256]{1,0:T(8,128)(2,1)S(1)}, bf16[144,256]{1,0:T(8,128)(2,1)S(1)}, u32[]{:S(2)}, u32[]{:S(2)}) collective-permute-start(bf16[144,256]{1,0:T(8,128)(2,1)S(1)} %get-tuple-element.24.own_ref), channel_id=1, source_target_pairs={{224,256},{225,257},{226,258},{227,259},{228,260},{229,261},{230,2... | collective-permute-start | bytes 221192 | tf_op jit(solution)/shard_map/ppermute | solution.py:470
  (5 other events, 58.0 us)
Sparse Core Ops, SparseCore 0:
  9.5 74.6 all-gather.5
  96.3 44.6 all-gather.7

commit v5 on v3

--- a/solution.py
+++ b/solution.py
@@ -20,6 +20,7 @@
 BF16 = jnp.bfloat16
 MIB = 1024 * 1024
 FAR = -1e30
+TALL = 512
 
 
 def ring(count, step):
@@ -30,16 +31,21 @@
     return lax.ppermute(value, SEQ, [(i, i + step) for i in range(YH * Z - step)])
 
 
-def ring_gather(block):
+def ring_gather(block, gate):
     pieces = [(0, 0, block)]
     right = left = block
     for step in range(1, 4):
+        if step == 3:
+            left, far = lax.optimization_barrier((left, far))
         right = lax.ppermute(right, "z", ring(Z, 1))
         left = lax.ppermute(left, "z", ring(Z, -1))
         pieces += [(Z - step, 0, right), (step, 0, left)]
+        if step == 1:
+            gate, right = lax.optimization_barrier((gate, right))
+            far = lax.ppermute(gate, "yh", ring(YH, 1))
     right = lax.ppermute(right[:1], "z", ring(Z, 1))
     left = lax.ppermute(left[1:], "z", ring(Z, -1))
-    return pieces + [(4, 0, right), (4, 1, left)]
+    return pieces + [(4, 0, right), (4, 1, left)], far
 
 
 def call(
@@ -248,8 +254,9 @@
             state = jnp.where(k < z, later, state)
         entering[...] = (state + before_ref[0:STATE, :].astype(F32)).astype(BF16)
         for k in range(Z):
-            for yh in range(YH):
-                weights[pl.ds((yh * Z + k) * 256, 256), :] = w_ref[k, yh]
+            for slot in range(YH):
+                row = ((scalars[2] + slot) % YH * Z + k) * 256
+                weights[pl.ds(pl.multiple_of(row, 256), 256), :] = w_ref[k, slot]
 
     gate = jnp.dot(tok_ref[...], weights[...], preferred_element_type=F32).astype(BF16)
     carried = jnp.dot(act_ref[...], entering[...], preferred_element_type=F32)
@@ -284,15 +291,15 @@
 
 def run_rest(gathered, weights, proj):
     rows, depth = gathered.shape
-    count = rows // BLOCK - 1
+    tile = (rows - BLOCK) // 2
     return call(
         rest_kernel,
-        (count,),
-        [rows_of((BLOCK, depth)), held(weights), pl.BlockSpec(memory_space=pl.ANY)],
-        rows_of((BLOCK, 640)),
+        (2,),
+        [rows_of((tile, depth)), held(weights), pl.BlockSpec(memory_space=pl.ANY)],
+        rows_of((tile, 640)),
         shape((rows, 640), BF16),
-        cost=work(2 * count * BLOCK * depth * 640, 8 << 20),
-        room=16,
+        cost=work(2 * (rows - BLOCK) * depth * 640, 8 << 20),
+        room=20,
         aliases={2: 0},
     )(gathered, weights, proj)
 
@@ -366,22 +373,22 @@
     rows, depth = gathered.shape
     return call(
         finish_kernel,
-        (rows // BLOCK,),
+        (rows // TALL,),
         [
             held(before),
             held(shards),
-            pl.BlockSpec((BLOCK, 128), lambda i, *_: (i, 3)),
-            rows_of((BLOCK, 256)),
-            rows_of((BLOCK, 256)),
-            rows_of((BLOCK, depth)),
+            pl.BlockSpec((TALL, 128), lambda i, *_: (i, 3)),
+            rows_of((TALL, 256)),
+            rows_of((TALL, 256)),
+            rows_of((TALL, depth)),
             whole(gate_all.shape),
         ],
-        rows_of((BLOCK, 256)),
+        rows_of((TALL, 256)),
         shape((rows, 256), BF16),
         scratch=[pltpu.VMEM((STATE, 256), BF16), pltpu.VMEM((depth, 256), BF16)],
         prefetch=1,
         cost=work(2 * rows * (128 + depth) * 256, 13 << 20),
-        room=20,
+        room=28,
     )(scalars, before, shards, act, y, reach, gathered, gate_all)
 
 
@@ -407,13 +414,14 @@
     state_half = lax.dynamic_slice(state_weight, (group, core * 128, 0), (1, 128, 256))[0]
     conv_own = lax.dynamic_index_in_dim(state_conv, group, 0, keepdims=False)
     step_rows = jnp.pad(step_weight.T, ((0, 8 - heads_here), (0, 0)))
-    pack = jnp.concatenate([value_weight, state_half, step_rows, gate_weight], axis=0)
+    pack = jnp.concatenate([value_weight, state_half, step_rows], axis=0)
     both = lax.all_gather(pack, "yh", axis=0, tiled=False)
-    pieces = ring_gather(both[:, :392])
+    pieces, gate_far = ring_gather(both, gate_weight)
     halves = jnp.concatenate([piece[:, 256:384] for _, _, piece in pieces], axis=0)
     halves = lax.ppermute(halves, "c", [(0, 1), (1, 0)])
-    scalars = jnp.stack([z, core]).astype(jnp.int32)
-    gate_part, gathered, halves = lax.optimization_barrier((both[:, 392:], gathered, halves))
+    scalars = jnp.stack([z, core, lax.axis_index("yh")]).astype(jnp.int32)
+    gate_part = jnp.stack([gate_weight, gate_far])
+    gate_part, gathered, halves = lax.optimization_barrier((gate_part, gathered, halves))
     gate_all = lax.all_gather(gate_part, "z", axis=0, tiled=False)
     gathered = in_hbm(gathered)
     proj, weights = run_first(gathered, pieces, halves, scalars)

time: 170 us -> 174 us (1.024)
  the two profiles are of different devices: /device:TPU:6 before, /device:TPU:52 now
where the time goes in v5:
time: 174 us; the launch traced here: 173 us
  starting transfers between devices  45.3 us (26%)
  blocking collectives  41.1 us (24%)
  waiting for transfers between devices  32.7 us (19%)
  Pallas kernels  31.1 us (18%)
  between operations  13.8 us (8%)
  local copies, waits for them, and re-layouts  7.33 us (4%)
  other arithmetic  1.92 us (1%)
    all_gather x1, blocking collectives, local(): shards = lax.all_gather(carried, 'z', axis=0, tiled=False)  25.5 us
    ppermute x3, starting transfers between devices, ring_gather(): left = lax.ppermute(left, 'z', ring(Z, -1))  19.3 us
    all_gather x1, blocking collectives, local(): both = lax.all_gather(pack, 'yh', axis=0, tiled=False)  15.6 us
    ppermute x3, waiting for transfers between devices, ring_gather(): right = lax.ppermute(right, 'z', ring(Z, 1))  13.8 us
    ppermute x3, starting transfers between devices, ring_gather(): right = lax.ppermute(right, 'z', ring(Z, 1))  8.1 us
    pallas_call x1, Pallas kernels, run_rest(): call(rest_kernel, (2,), [rows_of((tile, depth)), held(weights), pl.BlockS...  7.54 us
    pallas_call x1, Pallas kernels, run_finish(): call(finish_kernel, (rows // TALL,), [held(before), held(shards), pl.Bloc...  7.44 us
    ppermute x1, waiting for transfers between devices, local(): before = lax.ppermute(packed, SEQ, [(Z - 1, Z)])  6.46 us
  transfers between devices with their start and end apart: 14, of which 9 were waited for; matrix products, arithmetic and copies ran while one was open for 5% of the time, Pallas kernels for 14%

profile of v5, /device:TPU:52, one launch (start us, length us, event | category | flops | bytes accessed | tf_op | source)
XLA Modules:
  0.0 173.1 jit_solution(9428581852161068579)
XLA Ops:
  8.8 15.6 %all-gather = bf16[784,256]{1,0:T(8,128)(2,1)S(1)} all-gather(bf16[392,256]{1,0:T(8,128)(2,1)S(1)} %fusion.1), channel_id=2, replica_groups=mesh['yh'=2,'z'=8,'x'=4,'y'=4,'c'=2] {'yh'}, dimensions={0}, use_global_device_ids=true | all-gather | bytes 602112 | tf_op jit(solution)/shard_map/all_gather | solution.py:418
  24.3 4.3 %collective-permute-start.2 = (bf16[2,392,256]{2,1,0:T(8,128)(2,1)S(1)}, bf16[2,392,256]{2,1,0:T(8,128)(2,1)S(1)}, u32[]{:S(2)}, u32[]{:S(2)}) collective-permute-start(bf16[2,392,256]{2,1,0:T(8,128)(2,1)S(1)} %bitcast.18), channel_id=1, source_target_pairs={{0,32},{32,64},{64,96},{96,128},{128,160},{160,192},{192,224},{224... | collective-permute-start | bytes 1204232 | tf_op jit(solution)/shard_map/ppermute | solution.py:40
  28.6 8.6 %collective-permute-start = (bf16[2,392,256]{2,1,0:T(8,128)(2,1)S(1)}, bf16[2,392,256]{2,1,0:T(8,128)(2,1)S(1)}, u32[]{:S(2)}, u32[]{:S(2)}) collective-permute-start(bf16[2,392,256]{2,1,0:T(8,128)(2,1)S(1)} %bitcast.19), channel_id=1, source_target_pairs={{0,224},{32,0},{64,32},{96,64},{128,96},{160,128},{192,160},{224,1... | collective-permute-start | bytes 1204232 | tf_op jit(solution)/shard_map/ppermute | solution.py:41
  37.9 5.1 %collective-permute-done.2.refs_1_ = bf16[2,392,256]{2,1,0:T(8,128)(2,1)S(1)} collective-permute-done((bf16[2,392,256]{2,1,0:T(8,128)(2,1)S(1)}, bf16[2,392,256]{2,1,0:T(8,128)(2,1)S(1)}, u32[]{:S(2)}, u32[]{:S(2)}) %collective-permute-start.2) | collective-permute-done | bytes 401440 | tf_op jit(solution)/shard_map/ppermute | solution.py:40
  43.0 1.9 %collective-permute-start.4 = (bf16[2,392,256]{2,1,0:T(8,128)(2,1)S(1)}, bf16[2,392,256]{2,1,0:T(8,128)(2,1)S(1)}, u32[]{:S(2)}, u32[]{:S(2)}) collective-permute-start(bf16[2,392,256]{2,1,0:T(8,128)(2,1)S(1)} %collective-permute-done.2.refs_1_), channel_id=1, source_target_pairs={{0,32},{32,64},{64,96},{96,128},{128,160},{160,192},{192,224},{224... | collective-permute-start | bytes 1204232 | tf_op jit(solution)/shard_map/ppermute | solution.py:40
  44.9 5.6 %collective-permute-start.3 = (bf16[256,256]{1,0:T(8,128)(2,1)}, bf16[256,256]{1,0:T(8,128)(2,1)S(1)}, u32[]{:S(2)}, u32[]{:S(2)}) collective-permute-start(bf16[256,256]{1,0:T(8,128)(2,1)} %param.13), channel_id=1, source_target_pairs={{0,256},{256,0},{1,257},{257,1},{2,258},{258,2},{3,259},{259,3},{4... | collective-permute-start | bytes 393224 | tf_op jit(solution)/shard_map/ppermute | solution.py:45
  50.6 5.1 %collective-permute-start.1 = (bf16[2,392,256]{2,1,0:T(8,128)(2,1)S(1)}, bf16[2,392,256]{2,1,0:T(8,128)(2,1)S(1)}, u32[]{:S(2)}, u32[]{:S(2)}) collective-permute-start(bf16[2,392,256]{2,1,0:T(8,128)(2,1)S(1)} %collective-permute-done.refs_2_), channel_id=1, source_target_pairs={{0,224},{32,0},{64,32},{96,64},{128,96},{160,128},{192,160},{224,1... | collective-permute-start | bytes 1204232 | tf_op jit(solution)/shard_map/ppermute | solution.py:41
  57.3 5.9 %collective-permute-done.1.refs_4_ = bf16[2,392,256]{2,1,0:T(8,128)(2,1)S(1)} collective-permute-done((bf16[2,392,256]{2,1,0:T(8,128)(2,1)S(1)}, bf16[2,392,256]{2,1,0:T(8,128)(2,1)S(1)}, u32[]{:S(2)}, u32[]{:S(2)}) %collective-permute-start.1) | collective-permute-done | bytes 401440 | tf_op jit(solution)/shard_map/ppermute | solution.py:41
  63.2 5.6 %collective-permute-start.6 = (bf16[2,392,256]{2,1,0:T(8,128)(2,1)S(1)}, bf16[2,392,256]{2,1,0:T(8,128)(2,1)S(1)}, u32[]{:S(2)}, u32[]{:S(2)}) collective-permute-start(bf16[2,392,256]{2,1,0:T(8,128)(2,1)S(1)} %collective-permute-done.1.refs_4_), channel_id=1, source_target_pairs={{0,224},{32,0},{64,32},{96,64},{128,96},{160,128},{192,160},{224,1... | collective-permute-start | bytes 1204232 | tf_op jit(solution)/shard_map/ppermute | solution.py:41
  68.9 1.9 %collective-permute-start.5 = (bf16[2,392,256]{2,1,0:T(8,128)(2,1)S(1)}, bf16[2,392,256]{2,1,0:T(8,128)(2,1)S(1)}, u32[]{:S(2)}, u32[]{:S(2)}) collective-permute-start(bf16[2,392,256]{2,1,0:T(8,128)(2,1)S(1)} %collective-permute-done.4.refs_3_), channel_id=1, source_target_pairs={{0,32},{32,64},{64,96},{96,128},{128,160},{160,192},{192,224},{224... | collective-permute-start | bytes 1204232 | tf_op jit(solution)/shard_map/ppermute | solution.py:40
  72.1 8.7 %collective-permute-done.5.refs_5_ = bf16[2,392,256]{2,1,0:T(8,128)(2,1)S(1)} collective-permute-done((bf16[2,392,256]{2,1,0:T(8,128)(2,1)S(1)}, bf16[2,392,256]{2,1,0:T(8,128)(2,1)S(1)}, u32[]{:S(2)}, u32[]{:S(2)}) %collective-permute-start.5) | collective-permute-done | bytes 401440 | tf_op jit(solution)/shard_map/ppermute | solution.py:40
  80.8 1.9 %collective-permute-start.7 = (bf16[1,392,256]{2,1,0:T(8,128)(2,1)S(1)}, bf16[1,392,256]{2,1,0:T(8,128)(2,1)S(1)}, u32[]{:S(2)}, u32[]{:S(2)}) collective-permute-start(bf16[1,392,256]{2,1,0:T(8,128)(2,1)S(1)} %slice.55), channel_id=1, source_target_pairs={{0,32},{32,64},{64,96},{96,128},{128,160},{160,192},{192,224},{224... | collective-permute-start | bytes 602120 | tf_op jit(solution)/shard_map/ppermute | solution.py:46
  82.8 5.1 %collective-permute-start.8 = (bf16[1,392,256]{2,1,0:T(8,128)(2,1)S(1)}, bf16[1,392,256]{2,1,0:T(8,128)(2,1)S(1)}, u32[]{:S(2)}, u32[]{:S(2)}) collective-permute-start(bf16[1,392,256]{2,1,0:T(8,128)(2,1)S(1)} %slice.57), channel_id=1, source_target_pairs={{0,224},{32,0},{64,32},{96,64},{128,96},{160,128},{192,160},{224,1... | collective-permute-start | bytes 602120 | tf_op jit(solution)/shard_map/ppermute | solution.py:47
  91.8 1.9 %collective-permute-start.9 = (bf16[16,128,256]{2,1,0:T(8,128)(2,1)}, bf16[16,128,256]{2,1,0:T(8,128)(2,1)}, u32[]{:S(2)}, u32[]{:S(2)}) collective-permute-start(bf16[16,128,256]{2,1,0:T(8,128)(2,1)} %slice_dynamic-update-slice_fusion.7), channel_id=1, source_target_pairs={{0,1},{1,0},{2,3},{3,2},{4,5},{5,4},{6,7},{7,6},{8,9},{9,8},{10,11... | collective-permute-start | bytes 3145736 | tf_op jit(solution)/shard_map/ppermute | solution.py:421
  94.5 2.2 %collective-permute-done.9.refs_9_ = bf16[16,128,256]{2,1,0:T(8,128)(2,1)} collective-permute-done((bf16[16,128,256]{2,1,0:T(8,128)(2,1)}, bf16[16,128,256]{2,1,0:T(8,128)(2,1)}, u32[]{:S(2)}, u32[]{:S(2)}) %collective-permute-start.9) | collective-permute-done | bytes 1048608 | tf_op jit(solution)/shard_map/ppermute | solution.py:421
  97.9 5.9 %shard_map.100 = (bf16[1024,640]{1,0:T(8,128)(2,1)S(1)}, bf16[4096,640]{1,0:T(8,128)(2,1)S(1)}) custom-call(s32[3]{0:T(128)S(1)} %pad_add_fusion.scalars, bf16[1024,4096]{1,0:T(8,128)(2,1)} %all-gather.6.cloned.1.call-done.tok_ref, bf16[2,392,256]{2,1,0:T(8,128)(2,1)} %bitcast.21, bf16[2,392,256]{2,1,0:T(8,128)(2,1)} %copy-done.4, ...), custom_call_target="tpu_custom_call" | custom-call | flops 1342177280 | bytes 12582912 | tf_op jit(solution)/shard_map/pallas_call | solution.py:280
  103.8 1.9 %collective-permute-start.10 = (bf16[8,512]{1,0:T(8,128)(2,1)S(1)}, bf16[8,512]{1,0:T(8,128)(2,1)S(1)}, u32[]{:S(2)}, u32[]{:S(2)}) collective-permute-start(bf16[8,512]{1,0:T(8,128)(2,1)S(1)} %slice.47), channel_id=1, source_target_pairs={{0,32},{32,64},{64,96},{96,128},{128,160},{160,192},{192,224},{224... | collective-permute-start | bytes 24584 | tf_op jit(solution)/shard_map/ppermute | solution.py:31
  105.7 7.5 %shard_map.101.proj_ref = bf16[1024,640]{1,0:T(8,128)(2,1)S(1)} custom-call(bf16[1024,4096]{1,0:T(8,128)(2,1)} %all-gather.6.cloned.1.call-done.tok_ref, bf16[4096,640]{1,0:T(8,128)(2,1)S(1)} %get-tuple-element.28.w_ref, bf16[1024,640]{1,0:T(8,128)(2,1)S(1)} %get-tuple-element.29._), custom_call_target="tpu_custom_call", output_to_operand_aliasing={{}: (2, {})} | custom-call | flops 4026531840 | bytes 8388608 | tf_op jit(solution)/shard_map/pallas_call | solution.py:295
  113.3 2.1 %collective-permute-done.10.rim_ref = bf16[8,512]{1,0:T(8,128)(2,1)S(1)} collective-permute-done((bf16[8,512]{1,0:T(8,128)(2,1)S(1)}, bf16[8,512]{1,0:T(8,128)(2,1)S(1)}, u32[]{:S(2)}, u32[]{:S(2)}) %collective-permute-start.10) | collective-permute-done | bytes 8224 | tf_op jit(solution)/shard_map/ppermute | solution.py:31
  115.3 5.6 %shard_map.102 = (bf16[1024,512]{1,0:T(8,128)(2,1)S(1)}, f32[1024,128]{1,0:T(8,128)S(1)}, f32[1024,128]{1,0:T(8,128)S(1)}, f32[4,128,256]{2,1,0:T(8,128)S(1)}, f...) custom-call(s32[16]{0:T(128)S(1)} %sub.7.starts, s32[1]{0:T(128)} %bitcast.4.base, ...), custom_call_target="tpu_custom_call" | custom-call | flops 67108864 | bytes 4194304 | tf_op jit(solution)/shard_map/pallas_call | solution.py:310
  122.3 4.6 %shard_map.104 = (f32[1024,256]{1,0:T(8,128)}, f32[1024,256]{1,0:T(8,128)}) custom-call(s32[16]{0:T(128)S(1)} %sub.7.starts, s32[1]{0:T(128)} %bitcast.4.base, bf16[1024,512]{1,0:T(8,128)(2,1)S(1)} %get-tuple-element.31.act_ref, f32[1024,128]{1,0:T(8,128)S(1)} %get-tuple-element.32.cum_ref, f32[1024,128]{1,0:T(8,128)S(1)} %get-tuple-element.33.step_ref, ...), custom_call_target="tpu_custom_call" | custom-call | flops 536870912 | bytes 5242880 | tf_op jit(solution)/shard_map/pallas_call | solution.py:343
  126.8 6.5 %collective-permute-done.11.before_ref = bf16[144,256]{1,0:T(8,128)(2,1)S(1)} collective-permute-done((bf16[144,256]{1,0:T(8,128)(2,1)S(1)}, bf16[144,256]{1,0:T(8,128)(2,1)S(1)}, u32[]{:S(2)}, u32[]{:S(2)}) %collective-permute-start.11) | collective-permute-done | bytes 73760 | tf_op jit(solution)/shard_map/ppermute | solution.py:436
  133.3 25.5 %all-gather.1 = bf16[1152,256]{1,0:T(8,128)(2,1)S(1)} all-gather(bf16[144,256]{1,0:T(8,128)(2,1)S(1)} %shard_map.103), channel_id=3, replica_groups=mesh['yh'=2,'z'=8,'x'=4,'y'=4,'c'=2] {'z'}, dimensions={0}, use_global_device_ids=true | all-gather | bytes 663552 | tf_op jit(solution)/shard_map/all_gather | solution.py:439
  158.9 7.4 %shard_map.105 = bf16[1024,256]{1,0:T(8,128)(2,1)} custom-call(s32[3]{0:T(128)S(1)} %pad_add_fusion.scalars, bf16[144,256]{1,0:T(8,128)(2,1)S(1)} %collective-permute-done.11.before_ref, bf16[8,144,256]{2,1,0:T(8,128)(2,1)S(1)} %bitcast.17, bf16[1024,512]{1,0:T(8,128)(2,1)S(1)} %get-tuple-element.31.act_ref, f32[1024,256]{1,0:T(8,128)} %get-tuple-element.36.y_ref, ...), custom_call_target="tpu_custom_call" | custom-call | flops 2214592512 | bytes 13631488 | tf_op jit(solution)/shard_map/pallas_call | solution.py:374
  (67 shorter events, 12.8 us)
Async XLA Ops:
  6.5 90.2 %all-gather.6.cloned.1.call-start = ((), (), s32[]{:S(2)}) async-start(), calls=%async_computation | async-start | bytes 8650752 | tf_op jit(solution)/shard_map/all_gather | solution.py:412
  7.3 86.5 %copy-start.10 = (bf16[256,256]{1,0:T(8,128)(2,1)S(1)}, bf16[256,256]{1,0:T(8,128)(2,1)}, u32[]{:S(2)}) copy-start(bf16[256,256]{1,0:T(8,128)(2,1)} %param.13) | copy-start | bytes 393220
  7.3 151.6 %all-gather.8.cloned.1.call-start = ((), (), s32[]{:S(2)}) async-start(), calls=%async_computation.1 | async-start | bytes 2359296 | tf_op jit(solution)/shard_map/all_gather | solution.py:425
  8.7 88.0 %copy-start.12 = (s32[16]{0:T(128)S(1)}, s32[16]{0:T(128)}, u32[]{:S(2)}) copy-start(s32[16]{0:T(128)} %param.11) | copy-start | bytes 196
  8.7 89.1 %copy-start.13 = (f32[4]{0:T(128)S(1)}, f32[4]{0:T(128)}, u32[]{:S(2)}) copy-start(f32[4]{0:T(128)} %param.19) | copy-start | bytes 52
  8.7 89.0 %copy-start.14 = (f32[4]{0:T(128)S(1)}, f32[4]{0:T(128)}, u32[]{:S(2)}) copy-start(f32[4]{0:T(128)} %param.18) | copy-start | bytes 52
  8.7 89.1 %copy-start.11 = (f32[4,256]{1,0:T(4,128)S(1)}, f32[4,256]{1,0:T(4,128)}, u32[]{:S(2)}) copy-start(f32[4,256]{1,0:T(4,128)} %param.16) | copy-start | bytes 12292
  24.3 73.5 %copy-start.1 = (bf16[784,256]{1,0:T(8,128)(2,1)}, bf16[784,256]{1,0:T(8,128)(2,1)S(1)}, u32[]{:S(2)}) copy-start(bf16[784,256]{1,0:T(8,128)(2,1)S(1)} %all-gather) | copy-start | bytes 1204228
  24.3 18.7 %collective-permute-start.2 = (bf16[2,392,256]{2,1,0:T(8,128)(2,1)S(1)}, bf16[2,392,256]{2,1,0:T(8,128)(2,1)S(1)}, u32[]{:S(2)}, u32[]{:S(2)}) collective-permute-start(bf16[2,392,256]{2,1,0:T(8,128)(2,1)S(1)} %bitcast.18), channel_id=1, source_target_pairs={{0,32},{32,64},{64,96},{96,128},{128,160},{160,192},{192,224},{224... | collective-permute-start | bytes 1204232 | tf_op jit(solution)/shard_map/ppermute | solution.py:40
  28.6 22.0 %collective-permute-start = (bf16[2,392,256]{2,1,0:T(8,128)(2,1)S(1)}, bf16[2,392,256]{2,1,0:T(8,128)(2,1)S(1)}, u32[]{:S(2)}, u32[]{:S(2)}) collective-permute-start(bf16[2,392,256]{2,1,0:T(8,128)(2,1)S(1)} %bitcast.19), channel_id=1, source_target_pairs={{0,224},{32,0},{64,32},{96,64},{128,96},{160,128},{192,160},{224,1... | collective-permute-start | bytes 1204232 | tf_op jit(solution)/shard_map/ppermute | solution.py:41
  43.0 54.8 %copy-start.4 = (bf16[2,392,256]{2,1,0:T(8,128)(2,1)}, bf16[2,392,256]{2,1,0:T(8,128)(2,1)S(1)}, u32[]{:S(2)}) copy-start(bf16[2,392,256]{2,1,0:T(8,128)(2,1)S(1)} %collective-permute-done.2.refs_1_) | copy-start | bytes 1204228
  43.0 25.8 %collective-permute-start.4 = (bf16[2,392,256]{2,1,0:T(8,128)(2,1)S(1)}, bf16[2,392,256]{2,1,0:T(8,128)(2,1)S(1)}, u32[]{:S(2)}, u32[]{:S(2)}) collective-permute-start(bf16[2,392,256]{2,1,0:T(8,128)(2,1)S(1)} %collective-permute-done.2.refs_1_), channel_id=1, source_target_pairs={{0,32},{32,64},{64,96},{96,128},{128,160},{160,192},{192,224},{224... | collective-permute-start | bytes 1204232 | tf_op jit(solution)/shard_map/ppermute | solution.py:40
  44.9 12.4 %collective-permute-start.3 = (bf16[256,256]{1,0:T(8,128)(2,1)}, bf16[256,256]{1,0:T(8,128)(2,1)S(1)}, u32[]{:S(2)}, u32[]{:S(2)}) collective-permute-start(bf16[256,256]{1,0:T(8,128)(2,1)} %param.13), channel_id=1, source_target_pairs={{0,256},{256,0},{1,257},{257,1},{2,258},{258,2},{3,259},{259,3},{4... | collective-permute-start | bytes 393224 | tf_op jit(solution)/shard_map/ppermute | solution.py:45
  50.6 12.6 %collective-permute-start.1 = (bf16[2,392,256]{2,1,0:T(8,128)(2,1)S(1)}, bf16[2,392,256]{2,1,0:T(8,128)(2,1)S(1)}, u32[]{:S(2)}, u32[]{:S(2)}) collective-permute-start(bf16[2,392,256]{2,1,0:T(8,128)(2,1)S(1)} %collective-permute-done.refs_2_), channel_id=1, source_target_pairs={{0,224},{32,0},{64,32},{96,64},{128,96},{160,128},{192,160},{224,1... | collective-permute-start | bytes 1204232 | tf_op jit(solution)/shard_map/ppermute | solution.py:41
  63.2 19.5 %copy-start.7 = (bf16[2,392,256]{2,1,0:T(8,128)(2,1)}, bf16[2,392,256]{2,1,0:T(8,128)(2,1)S(1)}, u32[]{:S(2)}) copy-start(bf16[2,392,256]{2,1,0:T(8,128)(2,1)S(1)} %collective-permute-done.1.refs_4_) | copy-start | bytes 1204228
  63.2 19.5 %collective-permute-start.6 = (bf16[2,392,256]{2,1,0:T(8,128)(2,1)S(1)}, bf16[2,392,256]{2,1,0:T(8,128)(2,1)S(1)}, u32[]{:S(2)}, u32[]{:S(2)}) collective-permute-start(bf16[2,392,256]{2,1,0:T(8,128)(2,1)S(1)} %collective-permute-done.1.refs_4_), channel_id=1, source_target_pairs={{0,224},{32,0},{64,32},{96,64},{128,96},{160,128},{192,160},{224,1... | collective-permute-start | bytes 1204232 | tf_op jit(solution)/shard_map/ppermute | solution.py:41
  68.9 11.9 %collective-permute-start.5 = (bf16[2,392,256]{2,1,0:T(8,128)(2,1)S(1)}, bf16[2,392,256]{2,1,0:T(8,128)(2,1)S(1)}, u32[]{:S(2)}, u32[]{:S(2)}) collective-permute-start(bf16[2,392,256]{2,1,0:T(8,128)(2,1)S(1)} %collective-permute-done.4.refs_3_), channel_id=1, source_target_pairs={{0,32},{32,64},{64,96},{96,128},{128,160},{160,192},{192,224},{224... | collective-permute-start | bytes 1204232 | tf_op jit(solution)/shard_map/ppermute | solution.py:40
  80.8 17.1 %copy-start.3 = (bf16[2,392,256]{2,1,0:T(8,128)(2,1)}, bf16[2,392,256]{2,1,0:T(8,128)(2,1)S(1)}, u32[]{:S(2)}) copy-start(bf16[2,392,256]{2,1,0:T(8,128)(2,1)S(1)} %collective-permute-done.5.refs_5_) | copy-start | bytes 1204228
  80.8 8.8 %collective-permute-start.7 = (bf16[1,392,256]{2,1,0:T(8,128)(2,1)S(1)}, bf16[1,392,256]{2,1,0:T(8,128)(2,1)S(1)}, u32[]{:S(2)}, u32[]{:S(2)}) collective-permute-start(bf16[1,392,256]{2,1,0:T(8,128)(2,1)S(1)} %slice.55), channel_id=1, source_target_pairs={{0,32},{32,64},{64,96},{96,128},{128,160},{160,192},{192,224},{224... | collective-permute-start | bytes 602120 | tf_op jit(solution)/shard_map/ppermute | solution.py:46
  82.7 15.1 %copy-start.2 = (bf16[2,392,256]{2,1,0:T(8,128)(2,1)}, bf16[2,392,256]{2,1,0:T(8,128)(2,1)S(1)}, u32[]{:S(2)}) copy-start(bf16[2,392,256]{2,1,0:T(8,128)(2,1)S(1)} %collective-permute-done.6.refs_6_) | copy-start | bytes 1204228
  82.8 8.4 %collective-permute-start.8 = (bf16[1,392,256]{2,1,0:T(8,128)(2,1)S(1)}, bf16[1,392,256]{2,1,0:T(8,128)(2,1)S(1)}, u32[]{:S(2)}, u32[]{:S(2)}) collective-permute-start(bf16[1,392,256]{2,1,0:T(8,128)(2,1)S(1)} %slice.57), channel_id=1, source_target_pairs={{0,224},{32,0},{64,32},{96,64},{128,96},{160,128},{192,160},{224,1... | collective-permute-start | bytes 602120 | tf_op jit(solution)/shard_map/ppermute | solution.py:47
  91.8 4.9 %collective-permute-start.9 = (bf16[16,128,256]{2,1,0:T(8,128)(2,1)}, bf16[16,128,256]{2,1,0:T(8,128)(2,1)}, u32[]{:S(2)}, u32[]{:S(2)}) collective-permute-start(bf16[16,128,256]{2,1,0:T(8,128)(2,1)} %slice_dynamic-update-slice_fusion.7), channel_id=1, source_target_pairs={{0,1},{1,0},{2,3},{3,2},{4,5},{5,4},{6,7},{7,6},{8,9},{9,8},{10,11... | collective-permute-start | bytes 3145736 | tf_op jit(solution)/shard_map/ppermute | solution.py:421
  103.8 11.6 %collective-permute-start.10 = (bf16[8,512]{1,0:T(8,128)(2,1)S(1)}, bf16[8,512]{1,0:T(8,128)(2,1)S(1)}, u32[]{:S(2)}, u32[]{:S(2)}) collective-permute-start(bf16[8,512]{1,0:T(8,128)(2,1)S(1)} %slice.47), channel_id=1, source_target_pairs={{0,32},{32,64},{64,96},{96,128},{128,160},{160,192},{192,224},{224... | collective-permute-start | bytes 24584 | tf_op jit(solution)/shard_map/ppermute | solution.py:31
  121.0 12.3 %collective-permute-start.11 = (bf16[144,256]{1,0:T(8,128)(2,1)S(1)}, bf16[144,256]{1,0:T(8,128)(2,1)S(1)}, u32[]{:S(2)}, u32[]{:S(2)}) collective-permute-start(bf16[144,256]{1,0:T(8,128)(2,1)S(1)} %get-tuple-element.30.own_ref), channel_id=1, source_target_pairs={{224,256},{225,257},{226,258},{227,259},{228,260},{229,261},{230,2... | collective-permute-start | bytes 221192 | tf_op jit(solution)/shard_map/ppermute | solution.py:436
  (5 other events, 36.8 us)
Sparse Core Ops, SparseCore 0:
  9.5 79.3 all-gather.5
  96.9 41.7 all-gather.7

commit v6 on v3

--- a/solution.py
+++ b/solution.py
@@ -14,12 +14,15 @@
 STATE = 128
 WIDTH = 64
 YH, Z, X, Y, C = 2, 8, 4, 4, 2
-SEQ = ("yh", "z")
+PAIRS = Z // 2
+RING = ("zh", "zc")
+SEQ = ("yh",) + RING
 HEAD = ("x", "y", "c")
 F32 = jnp.float32
 BF16 = jnp.bfloat16
 MIB = 1024 * 1024
 FAR = -1e30
+TALL = 512
 
 
 def ring(count, step):
@@ -34,11 +37,11 @@
     pieces = [(0, 0, block)]
     right = left = block
     for step in range(1, 4):
-        right = lax.ppermute(right, "z", ring(Z, 1))
-        left = lax.ppermute(left, "z", ring(Z, -1))
+        right = lax.ppermute(right, RING, ring(Z, 1))
+        left = lax.ppermute(left, RING, ring(Z, -1))
         pieces += [(Z - step, 0, right), (step, 0, left)]
-    right = lax.ppermute(right[:1], "z", ring(Z, 1))
-    left = lax.ppermute(left[1:], "z", ring(Z, -1))
+    right = lax.ppermute(right[:1], RING, ring(Z, 1))
+    left = lax.ppermute(left[1:], RING, ring(Z, -1))
     return pieces + [(4, 0, right), (4, 1, left)]
 
 
@@ -227,26 +230,33 @@
     return packed[STATE : STATE + 8].astype(F32) + packed[STATE + 8 : STATE + 16].astype(F32)
 
 
-def carry_kernel(own_ref, before_ref, out_ref):
-    own, before = own_ref[...], before_ref[...]
-    total = own[0:STATE].astype(F32) + gain_of(own)[0:1] * before[0:STATE].astype(F32)
+def pair_kernel(pair_ref, eight_ref, nine_ref, out_ref):
+    even, odd = pair_ref[0], pair_ref[1]
+    before = eight_ref[0:STATE, :].astype(F32) + nine_ref[0:STATE, :].astype(F32)
+    total = even[0:STATE].astype(F32) + gain_of(even)[0:1] * before
+    total = odd[0:STATE].astype(F32) + gain_of(odd)[0:1] * total
+    gain = gain_of(even) * gain_of(odd)
+    high = gain.astype(BF16)
+    low = (gain - high.astype(F32)).astype(BF16)
     out_ref[0:STATE, :] = total.astype(BF16)
-    out_ref[STATE : STATE + 16, :] = own[STATE : STATE + 16]
+    out_ref[STATE : STATE + 16, :] = jnp.concatenate([high, low], axis=0)
 
 
 def finish_kernel(
-    scalars, before_ref, shards_ref, act_ref, y_ref, reach_ref, tok_ref, w_ref, out_ref,
-    entering, weights,
+    scalars, eight_ref, nine_ref, own_ref, pairs_ref, act_ref, y_ref, reach_ref, tok_ref, w_ref,
+    out_ref, entering, weights,
 ):
     @pl.when(pl.program_id(0) == 0)
     def _():
-        z = scalars[0]
-        state = jnp.zeros((STATE, 256), F32)
-        for k in range(Z - 1):
-            piece = shards_ref[k]
+        pair, odd = scalars[0] // 2, scalars[0] % 2
+        state = eight_ref[0:STATE, :].astype(F32) + nine_ref[0:STATE, :].astype(F32)
+        for k in range(PAIRS - 1):
+            piece = pairs_ref[k]
             later = gain_of(piece)[0:1] * state + piece[0:STATE].astype(F32)
-            state = jnp.where(k < z, later, state)
-        entering[...] = (state + before_ref[0:STATE, :].astype(F32)).astype(BF16)
+            state = jnp.where(k < pair, later, state)
+        even = own_ref[0]
+        later = gain_of(even)[0:1] * state + even[0:STATE].astype(F32)
+        entering[...] = jnp.where(odd == 1, later, state).astype(BF16)
         for k in range(Z):
             for yh in range(YH):
                 weights[pl.ds((yh * Z + k) * 256, 256), :] = w_ref[k, yh]
@@ -350,39 +360,41 @@
     )(starts, base, act, cum, step, inside, gains)
 
 
-def run_carry(own, before):
-    return call(
-        carry_kernel,
+def run_pair(pair, eight, nine):
+    return call(
+        pair_kernel,
         (1,),
-        [held(own), held(before)],
-        held(own),
-        shape(own.shape, BF16),
+        [held(pair), held(eight), held(nine)],
+        held(eight),
+        shape(eight.shape, BF16),
         cost=work(1 << 17, 1 << 18),
         room=4,
-    )(own, before)
-
-
-def run_finish(scalars, before, shards, act, y, reach, gathered, gate_all):
+    )(pair, eight, nine)
+
+
+def run_finish(scalars, eight, nine, own, pairs, act, y, reach, gathered, gate_all):
     rows, depth = gathered.shape
     return call(
         finish_kernel,
-        (rows // BLOCK,),
+        (rows // TALL,),
         [
-            held(before),
-            held(shards),
-            pl.BlockSpec((BLOCK, 128), lambda i, *_: (i, 3)),
-            rows_of((BLOCK, 256)),
-            rows_of((BLOCK, 256)),
-            rows_of((BLOCK, depth)),
+            held(eight),
+            held(nine),
+            held(own),
+            held(pairs),
+            pl.BlockSpec((TALL, 128), lambda i, *_: (i, 3)),
+            rows_of((TALL, 256)),
+            rows_of((TALL, 256)),
+            rows_of((TALL, depth)),
             whole(gate_all.shape),
         ],
-        rows_of((BLOCK, 256)),
+        rows_of((TALL, 256)),
         shape((rows, 256), BF16),
         scratch=[pltpu.VMEM((STATE, 256), BF16), pltpu.VMEM((depth, 256), BF16)],
         prefetch=1,
         cost=work(2 * rows * (128 + depth) * 256, 13 << 20),
-        room=20,
-    )(scalars, before, shards, act, y, reach, gathered, gate_all)
+        room=28,
+    )(scalars, eight, nine, own, pairs, act, y, reach, gathered, gate_all)
 
 
 def local(
@@ -400,7 +412,7 @@
     tok_dev = tokens.shape[0] * X * Y * C
     heads_here = step_weight.shape[1]
     core = lax.axis_index("c")
-    z = lax.axis_index("z")
+    z = lax.axis_index(RING)
     group = lax.axis_index("x") * 2 + lax.axis_index("y") // 2
     gathered = lax.all_gather(tokens, HEAD, axis=0, tiled=True)
 
@@ -414,7 +426,7 @@
     halves = lax.ppermute(halves, "c", [(0, 1), (1, 0)])
     scalars = jnp.stack([z, core]).astype(jnp.int32)
     gate_part, gathered, halves = lax.optimization_barrier((both[:, 392:], gathered, halves))
-    gate_all = lax.all_gather(gate_part, "z", axis=0, tiled=False)
+    gate_all = lax.all_gather(gate_part, RING, axis=0, tiled=False)
     gathered = in_hbm(gathered)
     proj, weights = run_first(gathered, pieces, halves, scalars)
     rim = along_seq(proj[-8:, :512], 1)
@@ -425,17 +437,20 @@
     taps = jnp.concatenate([value_conv, conv_own], axis=1)
     small = jnp.pad(jnp.stack([step_bias, log_rate]), ((0, 6), (0, 128 - heads_here)))
     act, cum, step, inside, gains, packed = run_state(starts, base, proj, rim, taps, small)
-    before = lax.ppermute(packed, SEQ, [(Z - 1, Z)])
+    eight = lax.ppermute(packed, SEQ, [(Z - 1, Z)])
+    nine = lax.ppermute(packed, SEQ, [(Z - 1, Z + 1)])
     y, reach = run_blocks(starts, base, act, cum, step, inside, gains)
-    carried = run_carry(packed, before)
-    shards = lax.all_gather(carried, "z", axis=0, tiled=False)
+    packed, y, reach = lax.optimization_barrier((packed, y, reach))
+    own = lax.all_gather(packed, "zc", axis=0, tiled=False)
+    own, eight, nine = lax.optimization_barrier((own, eight, nine))
+    pairs = lax.all_gather(run_pair(own, eight, nine), "zh", axis=0, tiled=False)
     return run_finish(
-        scalars, before, shards, act, in_hbm(y), in_hbm(reach), gathered, in_hbm(gate_all)
+        scalars, eight, nine, own, pairs, act, in_hbm(y), in_hbm(reach), gathered, in_hbm(gate_all)
     )
 
 
 def solution(mesh):
-    grid = Mesh(mesh.devices.reshape(YH, Z, X, Y, C), SEQ + HEAD)
+    grid = Mesh(mesh.devices.reshape(YH, PAIRS, 2, X, Y, C), SEQ + HEAD)
     return jax.shard_map(
         local,
         mesh=grid,

time: 170 us -> 163 us (0.959)
  blocking collectives: 58.4 us -> 52.3 us
    all_gather x1 -> x2, blocking collectives: 37.7 us -> 31.6 us  [the longest x1 23.7 us: local(): lax.all_gather(run_pair(own, eight, nine), 'zh', axis=0, tiled=False)]
    ppermute x9 -> x10, starting transfers between devices: 34.9 us -> 35.6 us  [the longest x3 18.7 us: ring_gather(): left = lax.ppermute(left, RING, ring(Z, -1))]
    ppermute x9 -> x10, waiting for transfers between devices: 12.2 us -> 12.2 us  [the longest x3 11 us: ring_gather(): right = lax.ppermute(right, RING, ring(Z, 1))]
  transfers between devices with their start and end apart: 13 -> 14, of which waited for: 5 -> 5; matrix products, arithmetic and copies ran while one was open for 5% -> 5% of each run, Pallas kernels for 14% -> 14%
where the time goes in v6:
time: 163 us
  blocking collectives  52.3 us (32%)
  starting transfers between devices  40.8 us (25%)
  Pallas kernels  30.7 us (19%)
  waiting for transfers between devices  15.2 us (9%)
  between operations  13.8 us (8%)
  local copies, waits for them, and re-layouts  8.64 us (5%)
    all_gather x1, blocking collectives, local(): lax.all_gather(run_pair(own, eight, nine), 'zh', axis=0, tiled=False)  23.7 us
    all_gather x1, blocking collectives, local(): both = lax.all_gather(pack, 'yh', axis=0, tiled=False)  20.7 us
    ppermute x3, starting transfers between devices, ring_gather(): left = lax.ppermute(left, RING, ring(Z, -1))  18.7 us
    ppermute x3, waiting for transfers between devices, ring_gather(): right = lax.ppermute(right, RING, ring(Z, 1))  11 us
    ppermute x3, starting transfers between devices, ring_gather(): right = lax.ppermute(right, RING, ring(Z, 1))  8.1 us
    all_gather x1, blocking collectives, local(): own = lax.all_gather(packed, 'zc', axis=0, tiled=False)  7.87 us
    pallas_call x1, Pallas kernels, run_finish(): call(finish_kernel, (rows // TALL,), [held(eight), held(nine), held(own),...  7.38 us
    pallas_call x1, Pallas kernels, run_rest(): call(rest_kernel, (count,), [rows_of((BLOCK, depth)), held(weights), pl.B...  7.22 us
  transfers between devices with their start and end apart: 14, of which 5 were waited for; matrix products, arithmetic and copies ran while one was open for 5% of the time, Pallas kernels for 14%

profile of v6, /device:TPU:6, one launch (start us, length us, event | category | flops | bytes accessed | tf_op | source)
XLA Modules:
  0.0 162.7 jit_solution(15008106765549178828)
XLA Ops:
  7.8 1.0 fusion.3
  8.8 20.7 %all-gather = bf16[1296,256]{1,0:T(8,128)(2,1)S(1)} all-gather(bf16[648,256]{1,0:T(8,128)(2,1)S(1)} %fusion.3), channel_id=2, replica_groups=mesh['yh'=2,'zh'=4,'zc'=2,'x'=4,'y'=4,'c'=2] {'yh'}, dimensions={0}, use_global_device_ids=true | all-gather | bytes 995328 | tf_op jit(solution)/shard_map/all_gather | solution.py:423
  29.5 4.3 %collective-permute-start = (bf16[2,392,256]{2,1,0:T(8,128)(2,1)S(1)}, bf16[2,392,256]{2,1,0:T(8,128)(2,1)S(1)}, u32[]{:S(2)}, u32[]{:S(2)}) collective-permute-start(bf16[2,392,256]{2,1,0:T(8,128)(2,1)S(1)} %slice.59.refs_0_), channel_id=1, source_target_pairs={{0,32},{32,64},{64,96},{96,128},{128,160},{160,192},{192,224},{224... | collective-permute-start | bytes 1204232 | tf_op jit(solution)/shard_map/ppermute | solution.py:40
  33.8 7.9 %collective-permute-start.1 = (bf16[2,392,256]{2,1,0:T(8,128)(2,1)S(1)}, bf16[2,392,256]{2,1,0:T(8,128)(2,1)S(1)}, u32[]{:S(2)}, u32[]{:S(2)}) collective-permute-start(bf16[2,392,256]{2,1,0:T(8,128)(2,1)S(1)} %slice.59.refs_0_), channel_id=1, source_target_pairs={{0,224},{32,0},{64,32},{96,64},{128,96},{160,128},{192,160},{224,1... | collective-permute-start | bytes 1204232 | tf_op jit(solution)/shard_map/ppermute | solution.py:41
  42.4 3.2 %collective-permute-done.refs_1_ = bf16[2,392,256]{2,1,0:T(8,128)(2,1)S(1)} collective-permute-done((bf16[2,392,256]{2,1,0:T(8,128)(2,1)S(1)}, bf16[2,392,256]{2,1,0:T(8,128)(2,1)S(1)}, u32[]{:S(2)}, u32[]{:S(2)}) %collective-permute-start) | collective-permute-done | bytes 401440 | tf_op jit(solution)/shard_map/ppermute | solution.py:40
  45.6 1.9 %collective-permute-start.2 = (bf16[2,392,256]{2,1,0:T(8,128)(2,1)S(1)}, bf16[2,392,256]{2,1,0:T(8,128)(2,1)S(1)}, u32[]{:S(2)}, u32[]{:S(2)}) collective-permute-start(bf16[2,392,256]{2,1,0:T(8,128)(2,1)S(1)} %collective-permute-done.refs_1_), channel_id=1, source_target_pairs={{0,32},{32,64},{64,96},{96,128},{128,160},{160,192},{192,224},{224... | collective-permute-start | bytes 1204232 | tf_op jit(solution)/shard_map/ppermute | solution.py:40
  47.5 5.3 %collective-permute-start.3 = (bf16[2,392,256]{2,1,0:T(8,128)(2,1)S(1)}, bf16[2,392,256]{2,1,0:T(8,128)(2,1)S(1)}, u32[]{:S(2)}, u32[]{:S(2)}) collective-permute-start(bf16[2,392,256]{2,1,0:T(8,128)(2,1)S(1)} %collective-permute-done.1.refs_2_), channel_id=1, source_target_pairs={{0,224},{32,0},{64,32},{96,64},{128,96},{160,128},{192,160},{224,1... | collective-permute-start | bytes 1204232 | tf_op jit(solution)/shard_map/ppermute | solution.py:41
  54.2 3.4 %collective-permute-done.2.refs_3_ = bf16[2,392,256]{2,1,0:T(8,128)(2,1)S(1)} collective-permute-done((bf16[2,392,256]{2,1,0:T(8,128)(2,1)S(1)}, bf16[2,392,256]{2,1,0:T(8,128)(2,1)S(1)}, u32[]{:S(2)}, u32[]{:S(2)}) %collective-permute-start.2) | collective-permute-done | bytes 401440 | tf_op jit(solution)/shard_map/ppermute | solution.py:40
  57.6 1.9 %collective-permute-start.4 = (bf16[2,392,256]{2,1,0:T(8,128)(2,1)S(1)}, bf16[2,392,256]{2,1,0:T(8,128)(2,1)S(1)}, u32[]{:S(2)}, u32[]{:S(2)}) collective-permute-start(bf16[2,392,256]{2,1,0:T(8,128)(2,1)S(1)} %collective-permute-done.2.refs_3_), channel_id=1, source_target_pairs={{0,32},{32,64},{64,96},{96,128},{128,160},{160,192},{192,224},{224... | collective-permute-start | bytes 1204232 | tf_op jit(solution)/shard_map/ppermute | solution.py:40
  59.6 5.5 %collective-permute-start.5 = (bf16[2,392,256]{2,1,0:T(8,128)(2,1)S(1)}, bf16[2,392,256]{2,1,0:T(8,128)(2,1)S(1)}, u32[]{:S(2)}, u32[]{:S(2)}) collective-permute-start(bf16[2,392,256]{2,1,0:T(8,128)(2,1)S(1)} %collective-permute-done.3.refs_4_), channel_id=1, source_target_pairs={{0,224},{32,0},{64,32},{96,64},{128,96},{160,128},{192,160},{224,1... | collective-permute-start | bytes 1204232 | tf_op jit(solution)/shard_map/ppermute | solution.py:41
  66.4 4.3 %collective-permute-done.4.refs_5_ = bf16[2,392,256]{2,1,0:T(8,128)(2,1)S(1)} collective-permute-done((bf16[2,392,256]{2,1,0:T(8,128)(2,1)S(1)}, bf16[2,392,256]{2,1,0:T(8,128)(2,1)S(1)}, u32[]{:S(2)}, u32[]{:S(2)}) %collective-permute-start.4) | collective-permute-done | bytes 401440 | tf_op jit(solution)/shard_map/ppermute | solution.py:40
  70.8 1.9 %collective-permute-start.6 = (bf16[1,392,256]{2,1,0:T(8,128)(2,1)S(1)}, bf16[1,392,256]{2,1,0:T(8,128)(2,1)S(1)}, u32[]{:S(2)}, u32[]{:S(2)}) collective-permute-start(bf16[1,392,256]{2,1,0:T(8,128)(2,1)S(1)} %slice.66), channel_id=1, source_target_pairs={{0,32},{32,64},{64,96},{96,128},{128,160},{160,192},{192,224},{224... | collective-permute-start | bytes 602120 | tf_op jit(solution)/shard_map/ppermute | solution.py:43
  72.7 5.5 %collective-permute-start.7 = (bf16[1,392,256]{2,1,0:T(8,128)(2,1)S(1)}, bf16[1,392,256]{2,1,0:T(8,128)(2,1)S(1)}, u32[]{:S(2)}, u32[]{:S(2)}) collective-permute-start(bf16[1,392,256]{2,1,0:T(8,128)(2,1)S(1)} %slice.68), channel_id=1, source_target_pairs={{0,224},{32,0},{64,32},{96,64},{128,96},{160,128},{192,160},{224,1... | collective-permute-start | bytes 602120 | tf_op jit(solution)/shard_map/ppermute | solution.py:44
  80.3 1.2 collective-permute-done.7.refs_8_
  82.8 1.9 %collective-permute-start.8 = (bf16[16,128,256]{2,1,0:T(8,128)(2,1)}, bf16[16,128,256]{2,1,0:T(8,128)(2,1)}, u32[]{:S(2)}, u32[]{:S(2)}) collective-permute-start(bf16[16,128,256]{2,1,0:T(8,128)(2,1)} %slice_dynamic-update-slice_fusion.7), channel_id=1, source_target_pairs={{0,1},{1,0},{2,3},{3,2},{4,5},{5,4},{6,7},{7,6},{8,9},{9,8},{10,11... | collective-permute-start | bytes 3145736 | tf_op jit(solution)/shard_map/ppermute | solution.py:426
  85.4 2.3 %collective-permute-done.8.refs_9_ = bf16[16,128,256]{2,1,0:T(8,128)(2,1)} collective-permute-done((bf16[16,128,256]{2,1,0:T(8,128)(2,1)}, bf16[16,128,256]{2,1,0:T(8,128)(2,1)}, u32[]{:S(2)}, u32[]{:S(2)}) %collective-permute-start.8) | collective-permute-done | bytes 1048608 | tf_op jit(solution)/shard_map/ppermute | solution.py:426
  88.9 5.9 %shard_map.100 = (bf16[1024,640]{1,0:T(8,128)(2,1)S(1)}, bf16[4096,640]{1,0:T(8,128)(2,1)S(1)}) custom-call(s32[2]{0:T(128)S(1)} %pad_add_fusion.scalars, bf16[1024,4096]{1,0:T(8,128)(2,1)} %all-gather.7.cloned.1.call-done.tok_ref, bf16[2,392,256]{2,1,0:T(8,128)(2,1)} %copy-done.1, bf16[2,392,256]{2,1,0:T(8,128)(2,1)} %copy-done.4, ...), custom_call_target="tpu_custom_call" | custom-call | flops 1342177280 | bytes 12582912 | tf_op jit(solution)/shard_map/pallas_call | solution.py:283
  94.8 3.2 %collective-permute-start.9 = (bf16[8,512]{1,0:T(8,128)(2,1)S(1)}, bf16[8,512]{1,0:T(8,128)(2,1)S(1)}, u32[]{:S(2)}, u32[]{:S(2)}) collective-permute-start(bf16[8,512]{1,0:T(8,128)(2,1)S(1)} %slice.56), channel_id=1, source_target_pairs={{0,32},{32,64},{64,96},{96,128},{128,160},{160,192},{192,224},{224... | collective-permute-start | bytes 24584 | tf_op jit(solution)/shard_map/ppermute | solution.py:33
  98.0 7.2 %shard_map.101.proj_ref = bf16[1024,640]{1,0:T(8,128)(2,1)S(1)} custom-call(bf16[1024,4096]{1,0:T(8,128)(2,1)} %all-gather.7.cloned.1.call-done.tok_ref, bf16[4096,640]{1,0:T(8,128)(2,1)S(1)} %get-tuple-element.26.w_ref, bf16[1024,640]{1,0:T(8,128)(2,1)S(1)} %get-tuple-element.27._), custom_call_target="tpu_custom_call", output_to_operand_aliasing={{}: (2, {})} | custom-call | flops 4026531840 | bytes 8388608 | tf_op jit(solution)/shard_map/pallas_call | solution.py:298
  105.2 5.6 %shard_map.102 = (bf16[1024,512]{1,0:T(8,128)(2,1)S(1)}, f32[1024,128]{1,0:T(8,128)S(1)}, f32[1024,128]{1,0:T(8,128)S(1)}, f32[4,128,256]{2,1,0:T(8,128)S(1)}, f...) custom-call(s32[16]{0:T(128)S(1)} %sub.7.starts, s32[1]{0:T(128)} %bitcast.3.base, ...), custom_call_target="tpu_custom_call" | custom-call | flops 67108864 | bytes 4194304 | tf_op jit(solution)/shard_map/pallas_call | solution.py:313
  112.2 4.6 %shard_map.103 = (f32[1024,256]{1,0:T(8,128)}, f32[1024,256]{1,0:T(8,128)}) custom-call(s32[16]{0:T(128)S(1)} %sub.7.starts, s32[1]{0:T(128)} %bitcast.3.base, bf16[1024,512]{1,0:T(8,128)(2,1)S(1)} %get-tuple-element.29.act_ref, f32[1024,128]{1,0:T(8,128)S(1)} %get-tuple-element.30.cum_ref, f32[1024,128]{1,0:T(8,128)S(1)} %get-tuple-element.31.step_ref, ...), custom_call_target="tpu_custom_call" | custom-call | flops 536870912 | bytes 5242880 | tf_op jit(solution)/shard_map/pallas_call | solution.py:346
  116.8 7.9 %all-gather.1 = bf16[288,256]{1,0:T(8,128)(2,1)S(1)} all-gather(bf16[144,256]{1,0:T(8,128)(2,1)S(1)} %get-tuple-element.36), channel_id=3, replica_groups=mesh['yh'=2,'zh'=4,'zc'=2,'x'=4,'y'=4,'c'=2] {'zc'}, dimensions={0}, use_global_device_ids=true | all-gather | bytes 221184 | tf_op jit(solution)/shard_map/all_gather | solution.py:444
  124.7 23.7 %all-gather.2 = bf16[576,256]{1,0:T(8,128)(2,1)S(1)} all-gather(bf16[144,256]{1,0:T(8,128)(2,1)S(1)} %shard_map.104), channel_id=4, replica_groups=mesh['yh'=2,'zh'=4,'zc'=2,'x'=4,'y'=4,'c'=2] {'zh'}, dimensions={0}, use_global_device_ids=true | all-gather | bytes 368640 | tf_op jit(solution)/shard_map/all_gather | solution.py:446
  148.5 7.4 %shard_map.105 = bf16[1024,256]{1,0:T(8,128)(2,1)} custom-call(s32[2]{0:T(128)S(1)} %pad_add_fusion.scalars, bf16[144,256]{1,0:T(8,128)(2,1)S(1)} %collective-permute-done.10.eight_ref, bf16[144,256]{1,0:T(8,128)(2,1)S(1)} %collective-permute-done.11.nine_ref, bf16[2,144,256]{2,1,0:T(8,128)(2,1)S(1)} %bitcast.16, bf16[4,144,256]{2,1,0:T(8,128)(2,1)S(1)} %bitcast.17, ...), custom_call_target="tpu_custom_call" | custom-call | flops 2214592512 | bytes 13631488 | tf_op jit(solution)/shard_map/pallas_call | solution.py:377
  (67 shorter events, 11.1 us)
Async XLA Ops:
  6.5 81.2 %all-gather.7.cloned.1.call-start = ((), (), s32[]{:S(2)}) async-start(), calls=%async_computation | async-start | bytes 8650752 | tf_op jit(solution)/shard_map/all_gather | solution.py:417
  7.3 141.2 %all-gather.9.cloned.1.call-start = ((), (), s32[]{:S(2)}) async-start(), calls=%async_computation.1 | async-start | bytes 2359296 | tf_op jit(solution)/shard_map/all_gather | solution.py:429
  29.5 58.3 %copy-start.11 = (s32[16]{0:T(128)S(1)}, s32[16]{0:T(128)}, u32[]{:S(2)}) copy-start(s32[16]{0:T(128)} %param.11) | copy-start | bytes 196
  29.5 59.3 %copy-start.12 = (f32[4]{0:T(128)S(1)}, f32[4]{0:T(128)}, u32[]{:S(2)}) copy-start(f32[4]{0:T(128)} %param.19) | copy-start | bytes 52
  29.5 59.3 %copy-start.13 = (f32[4]{0:T(128)S(1)}, f32[4]{0:T(128)}, u32[]{:S(2)}) copy-start(f32[4]{0:T(128)} %param.18) | copy-start | bytes 52
  29.5 59.3 %copy-start.10 = (f32[4,256]{1,0:T(4,128)S(1)}, f32[4,256]{1,0:T(4,128)}, u32[]{:S(2)}) copy-start(f32[4,256]{1,0:T(4,128)} %param.16) | copy-start | bytes 12292
  29.5 59.3 %copy-start.1 = (bf16[2,392,256]{2,1,0:T(8,128)(2,1)}, bf16[2,392,256]{2,1,0:T(8,128)(2,1)S(1)}, u32[]{:S(2)}) copy-start(bf16[2,392,256]{2,1,0:T(8,128)(2,1)S(1)} %slice.59.refs_0_) | copy-start | bytes 1204228
  29.5 16.1 %collective-permute-start = (bf16[2,392,256]{2,1,0:T(8,128)(2,1)S(1)}, bf16[2,392,256]{2,1,0:T(8,128)(2,1)S(1)}, u32[]{:S(2)}, u32[]{:S(2)}) collective-permute-start(bf16[2,392,256]{2,1,0:T(8,128)(2,1)S(1)} %slice.59.refs_0_), channel_id=1, source_target_pairs={{0,32},{32,64},{64,96},{96,128},{128,160},{160,192},{192,224},{224... | collective-permute-start | bytes 1204232 | tf_op jit(solution)/shard_map/ppermute | solution.py:40
  33.8 13.7 %collective-permute-start.1 = (bf16[2,392,256]{2,1,0:T(8,128)(2,1)S(1)}, bf16[2,392,256]{2,1,0:T(8,128)(2,1)S(1)}, u32[]{:S(2)}, u32[]{:S(2)}) collective-permute-start(bf16[2,392,256]{2,1,0:T(8,128)(2,1)S(1)} %slice.59.refs_0_), channel_id=1, source_target_pairs={{0,224},{32,0},{64,32},{96,64},{128,96},{160,128},{192,160},{224,1... | collective-permute-start | bytes 1204232 | tf_op jit(solution)/shard_map/ppermute | solution.py:41
  45.6 43.2 %copy-start.4 = (bf16[2,392,256]{2,1,0:T(8,128)(2,1)}, bf16[2,392,256]{2,1,0:T(8,128)(2,1)S(1)}, u32[]{:S(2)}) copy-start(bf16[2,392,256]{2,1,0:T(8,128)(2,1)S(1)} %collective-permute-done.refs_1_) | copy-start | bytes 1204228
  45.6 12.0 %collective-permute-start.2 = (bf16[2,392,256]{2,1,0:T(8,128)(2,1)S(1)}, bf16[2,392,256]{2,1,0:T(8,128)(2,1)S(1)}, u32[]{:S(2)}, u32[]{:S(2)}) collective-permute-start(bf16[2,392,256]{2,1,0:T(8,128)(2,1)S(1)} %collective-permute-done.refs_1_), channel_id=1, source_target_pairs={{0,32},{32,64},{64,96},{96,128},{128,160},{160,192},{192,224},{224... | collective-permute-start | bytes 1204232 | tf_op jit(solution)/shard_map/ppermute | solution.py:40
  47.5 41.3 %copy-start.5 = (bf16[2,392,256]{2,1,0:T(8,128)(2,1)}, bf16[2,392,256]{2,1,0:T(8,128)(2,1)S(1)}, u32[]{:S(2)}) copy-start(bf16[2,392,256]{2,1,0:T(8,128)(2,1)S(1)} %collective-permute-done.1.refs_2_) | copy-start | bytes 1204228
  47.5 12.0 %collective-permute-start.3 = (bf16[2,392,256]{2,1,0:T(8,128)(2,1)S(1)}, bf16[2,392,256]{2,1,0:T(8,128)(2,1)S(1)}, u32[]{:S(2)}, u32[]{:S(2)}) collective-permute-start(bf16[2,392,256]{2,1,0:T(8,128)(2,1)S(1)} %collective-permute-done.1.refs_2_), channel_id=1, source_target_pairs={{0,224},{32,0},{64,32},{96,64},{128,96},{160,128},{192,160},{224,1... | collective-permute-start | bytes 1204232 | tf_op jit(solution)/shard_map/ppermute | solution.py:41
  57.6 15.1 %copy-start.6 = (bf16[2,392,256]{2,1,0:T(8,128)(2,1)}, bf16[2,392,256]{2,1,0:T(8,128)(2,1)S(1)}, u32[]{:S(2)}) copy-start(bf16[2,392,256]{2,1,0:T(8,128)(2,1)S(1)} %collective-permute-done.2.refs_3_) | copy-start | bytes 1204228
  57.6 13.1 %collective-permute-start.4 = (bf16[2,392,256]{2,1,0:T(8,128)(2,1)S(1)}, bf16[2,392,256]{2,1,0:T(8,128)(2,1)S(1)}, u32[]{:S(2)}, u32[]{:S(2)}) collective-permute-start(bf16[2,392,256]{2,1,0:T(8,128)(2,1)S(1)} %collective-permute-done.2.refs_3_), channel_id=1, source_target_pairs={{0,32},{32,64},{64,96},{96,128},{128,160},{160,192},{192,224},{224... | collective-permute-start | bytes 1204232 | tf_op jit(solution)/shard_map/ppermute | solution.py:40
  59.6 13.1 %collective-permute-start.5 = (bf16[2,392,256]{2,1,0:T(8,128)(2,1)S(1)}, bf16[2,392,256]{2,1,0:T(8,128)(2,1)S(1)}, u32[]{:S(2)}, u32[]{:S(2)}) collective-permute-start(bf16[2,392,256]{2,1,0:T(8,128)(2,1)S(1)} %collective-permute-done.3.refs_4_), channel_id=1, source_target_pairs={{0,224},{32,0},{64,32},{96,64},{128,96},{160,128},{192,160},{224,1... | collective-permute-start | bytes 1204232 | tf_op jit(solution)/shard_map/ppermute | solution.py:41
  70.7 18.1 %copy-start.2 = (bf16[2,392,256]{2,1,0:T(8,128)(2,1)}, bf16[2,392,256]{2,1,0:T(8,128)(2,1)S(1)}, u32[]{:S(2)}) copy-start(bf16[2,392,256]{2,1,0:T(8,128)(2,1)S(1)} %collective-permute-done.4.refs_5_) | copy-start | bytes 1204228
  70.8 8.8 %collective-permute-start.6 = (bf16[1,392,256]{2,1,0:T(8,128)(2,1)S(1)}, bf16[1,392,256]{2,1,0:T(8,128)(2,1)S(1)}, u32[]{:S(2)}, u32[]{:S(2)}) collective-permute-start(bf16[1,392,256]{2,1,0:T(8,128)(2,1)S(1)} %slice.66), channel_id=1, source_target_pairs={{0,32},{32,64},{64,96},{96,128},{128,160},{160,192},{192,224},{224... | collective-permute-start | bytes 602120 | tf_op jit(solution)/shard_map/ppermute | solution.py:43
  72.7 16.1 %copy-start.3 = (bf16[2,392,256]{2,1,0:T(8,128)(2,1)}, bf16[2,392,256]{2,1,0:T(8,128)(2,1)S(1)}, u32[]{:S(2)}) copy-start(bf16[2,392,256]{2,1,0:T(8,128)(2,1)S(1)} %collective-permute-done.5.refs_6_) | copy-start | bytes 1204228
  72.7 8.7 %collective-permute-start.7 = (bf16[1,392,256]{2,1,0:T(8,128)(2,1)S(1)}, bf16[1,392,256]{2,1,0:T(8,128)(2,1)S(1)}, u32[]{:S(2)}, u32[]{:S(2)}) collective-permute-start(bf16[1,392,256]{2,1,0:T(8,128)(2,1)S(1)} %slice.68), channel_id=1, source_target_pairs={{0,224},{32,0},{64,32},{96,64},{128,96},{160,128},{192,160},{224,1... | collective-permute-start | bytes 602120 | tf_op jit(solution)/shard_map/ppermute | solution.py:44
  82.8 4.9 %collective-permute-start.8 = (bf16[16,128,256]{2,1,0:T(8,128)(2,1)}, bf16[16,128,256]{2,1,0:T(8,128)(2,1)}, u32[]{:S(2)}, u32[]{:S(2)}) collective-permute-start(bf16[16,128,256]{2,1,0:T(8,128)(2,1)} %slice_dynamic-update-slice_fusion.7), channel_id=1, source_target_pairs={{0,1},{1,0},{2,3},{3,2},{4,5},{5,4},{6,7},{7,6},{8,9},{9,8},{10,11... | collective-permute-start | bytes 3145736 | tf_op jit(solution)/shard_map/ppermute | solution.py:426
  94.8 10.5 %collective-permute-start.9 = (bf16[8,512]{1,0:T(8,128)(2,1)S(1)}, bf16[8,512]{1,0:T(8,128)(2,1)S(1)}, u32[]{:S(2)}, u32[]{:S(2)}) collective-permute-start(bf16[8,512]{1,0:T(8,128)(2,1)S(1)} %slice.56), channel_id=1, source_target_pairs={{0,32},{32,64},{64,96},{96,128},{128,160},{160,192},{192,224},{224... | collective-permute-start | bytes 24584 | tf_op jit(solution)/shard_map/ppermute | solution.py:33
  110.9 13.8 %collective-permute-start.10 = (bf16[144,256]{1,0:T(8,128)(2,1)S(1)}, bf16[144,256]{1,0:T(8,128)(2,1)S(1)}, u32[]{:S(2)}, u32[]{:S(2)}) collective-permute-start(bf16[144,256]{1,0:T(8,128)(2,1)S(1)} %get-tuple-element.36), channel_id=1, source_target_pairs={{224,256},{225,257},{226,258},{227,259},{228,260},{229,261},{230,2... | collective-permute-start | bytes 221192 | tf_op jit(solution)/shard_map/ppermute | solution.py:440
  111.5 13.1 %collective-permute-start.11 = (bf16[144,256]{1,0:T(8,128)(2,1)S(1)}, bf16[144,256]{1,0:T(8,128)(2,1)S(1)}, u32[]{:S(2)}, u32[]{:S(2)}) collective-permute-start(bf16[144,256]{1,0:T(8,128)(2,1)S(1)} %get-tuple-element.36), channel_id=1, source_target_pairs={{224,288},{225,289},{226,290},{227,291},{228,292},{229,293},{230,2... | collective-permute-start | bytes 221192 | tf_op jit(solution)/shard_map/ppermute | solution.py:441
  (4 other events, 24.3 us)
Sparse Core Ops, SparseCore 0:
  9.5 75.6 all-gather.6
  87.8 51.1 all-gather.8

commit v7 on v6

--- a/solution.py
+++ b/solution.py
@@ -149,7 +149,7 @@
     ext[8 : 8 + BLOCK, :] = tile
     positions = first + lax.broadcasted_iota(jnp.int32, (BLOCK, 128), 0)
     start = doc_start(starts, positions)
-    depth = (positions - start)[:, 0:1]
+    depth = jnp.concatenate([positions - start] * 4, axis=1)
     summed = taps_ref[3:4, :] * tile
     for lag in (1, 2, 3):
         window = ext[8 - lag : 8 - lag + BLOCK, :]
@@ -205,7 +205,7 @@
     start = doc_start(starts, first + lax.broadcasted_iota(jnp.int32, (BLOCK, 128), 0))
     row = lax.broadcasted_iota(jnp.int32, (BLOCK, BLOCK), 0)
     column = lax.broadcasted_iota(jnp.int32, (BLOCK, BLOCK), 1)
-    allowed = (column <= row) & (first + column >= start[:, 0:1])
+    allowed = (column <= row) & (first + column >= jnp.concatenate([start] * 2, axis=1))
     parts = []
     for h in range(4):
         gap = cumulative[:, h : h + 1] - cum_rows[h : h + 1, :]
@@ -230,8 +230,10 @@
     return packed[STATE : STATE + 8].astype(F32) + packed[STATE + 8 : STATE + 16].astype(F32)
 
 
-def pair_kernel(pair_ref, eight_ref, nine_ref, out_ref):
-    even, odd = pair_ref[0], pair_ref[1]
+def pair_kernel(scalars, own_ref, other_ref, eight_ref, nine_ref, out_ref):
+    own, other = own_ref[...], other_ref[...]
+    is_odd = scalars[0] % 2 == 1
+    even, odd = jnp.where(is_odd, other, own), jnp.where(is_odd, own, other)
     before = eight_ref[0:STATE, :].astype(F32) + nine_ref[0:STATE, :].astype(F32)
     total = even[0:STATE].astype(F32) + gain_of(even)[0:1] * before
     total = odd[0:STATE].astype(F32) + gain_of(odd)[0:1] * total
@@ -243,7 +245,7 @@
 
 
 def finish_kernel(
-    scalars, eight_ref, nine_ref, own_ref, pairs_ref, act_ref, y_ref, reach_ref, tok_ref, w_ref,
+    scalars, eight_ref, nine_ref, other_ref, pairs_ref, act_ref, y_ref, reach_ref, tok_ref, w_ref,
     out_ref, entering, weights,
 ):
     @pl.when(pl.program_id(0) == 0)
@@ -254,7 +256,7 @@
             piece = pairs_ref[k]
             later = gain_of(piece)[0:1] * state + piece[0:STATE].astype(F32)
             state = jnp.where(k < pair, later, state)
-        even = own_ref[0]
+        even = other_ref[...]
         later = gain_of(even)[0:1] * state + even[0:STATE].astype(F32)
         entering[...] = jnp.where(odd == 1, later, state).astype(BF16)
         for k in range(Z):
@@ -360,19 +362,20 @@
     )(starts, base, act, cum, step, inside, gains)
 
 
-def run_pair(pair, eight, nine):
+def run_pair(scalars, own, other, eight, nine):
     return call(
         pair_kernel,
         (1,),
-        [held(pair), held(eight), held(nine)],
-        held(eight),
-        shape(eight.shape, BF16),
+        [held(own)] * 4,
+        held(own),
+        shape(own.shape, BF16),
+        prefetch=1,
         cost=work(1 << 17, 1 << 18),
         room=4,
-    )(pair, eight, nine)
-
-
-def run_finish(scalars, eight, nine, own, pairs, act, y, reach, gathered, gate_all):
+    )(scalars, own, other, eight, nine)
+
+
+def run_finish(scalars, eight, nine, other, pairs, act, y, reach, gathered, gate_all):
     rows, depth = gathered.shape
     return call(
         finish_kernel,
@@ -380,7 +383,7 @@
         [
             held(eight),
             held(nine),
-            held(own),
+            held(other),
             held(pairs),
             pl.BlockSpec((TALL, 128), lambda i, *_: (i, 3)),
             rows_of((TALL, 256)),
@@ -394,7 +397,7 @@
         prefetch=1,
         cost=work(2 * rows * (128 + depth) * 256, 13 << 20),
         room=28,
-    )(scalars, eight, nine, own, pairs, act, y, reach, gathered, gate_all)
+    )(scalars, eight, nine, other, pairs, act, y, reach, gathered, gate_all)
 
 
 def local(
@@ -439,13 +442,15 @@
     act, cum, step, inside, gains, packed = run_state(starts, base, proj, rim, taps, small)
     eight = lax.ppermute(packed, SEQ, [(Z - 1, Z)])
     nine = lax.ppermute(packed, SEQ, [(Z - 1, Z + 1)])
+    other = lax.ppermute(packed, "zc", ring(2, 1))
     y, reach = run_blocks(starts, base, act, cum, step, inside, gains)
-    packed, y, reach = lax.optimization_barrier((packed, y, reach))
-    own = lax.all_gather(packed, "zc", axis=0, tiled=False)
-    own, eight, nine = lax.optimization_barrier((own, eight, nine))
-    pairs = lax.all_gather(run_pair(own, eight, nine), "zh", axis=0, tiled=False)
+    packed, other, eight, nine, y, reach = lax.optimization_barrier(
+        (packed, other, eight, nine, y, reach)
+    )
+    pair = run_pair(scalars, packed, other, eight, nine)
+    pairs = lax.all_gather(pair, "zh", axis=0, tiled=False)
     return run_finish(
-        scalars, eight, nine, own, pairs, act, in_hbm(y), in_hbm(reach), gathered, in_hbm(gate_all)
+        scalars, eight, nine, other, pairs, act, in_hbm(y), in_hbm(reach), gathered, in_hbm(gate_all)
     )
 
 

time: 163 us -> 165 us (1.012)
  the two profiles are of different devices: /device:TPU:6 before, /device:TPU:118 now
where the time goes in v7:
time: 165 us; the launch traced here: 164 us
  starting transfers between devices  49.4 us (30%)
  blocking collectives  35.1 us (21%)
  Pallas kernels  31.3 us (19%)
  waiting for transfers between devices  24.8 us (15%)
  between operations  13.8 us (8%)
  local copies, waits for them, and re-layouts  8.71 us (5%)
    all_gather x1, blocking collectives, local(): both = lax.all_gather(pack, 'yh', axis=0, tiled=False)  21 us
    ppermute x3, starting transfers between devices, ring_gather(): left = lax.ppermute(left, RING, ring(Z, -1))  15.6 us
    all_gather x1, blocking collectives, local(): pairs = lax.all_gather(pair, 'zh', axis=0, tiled=False)  14.1 us
    ppermute x3, starting transfers between devices, ring_gather(): right = lax.ppermute(right, RING, ring(Z, 1))  11.3 us
    ppermute x1, waiting for transfers between devices, local(): nine = lax.ppermute(packed, SEQ, [(Z - 1, Z + 1)])  10.4 us
    ppermute x3, waiting for transfers between devices, ring_gather(): right = lax.ppermute(right, RING, ring(Z, 1))  9.78 us
    pallas_call x1, Pallas kernels, run_finish(): call(finish_kernel, (rows // TALL,), [held(eight), held(nine), held(other...  7.37 us
    pallas_call x1, Pallas kernels, run_rest(): call(rest_kernel, (count,), [rows_of((BLOCK, depth)), held(weights), pl.B...  7.22 us
  transfers between devices with their start and end apart: 15, of which 8 were waited for; matrix products, arithmetic and copies ran while one was open for 5% of the time, Pallas kernels for 15%

profile of v7, /device:TPU:118, one launch (start us, length us, event | category | flops | bytes accessed | tf_op | source)
XLA Modules:
  0.0 164.3 jit_solution(9426355501702930692)
XLA Ops:
  8.8 21.0 %all-gather = bf16[1296,256]{1,0:T(8,128)(2,1)S(1)} all-gather(bf16[648,256]{1,0:T(8,128)(2,1)S(1)} %fusion.3), channel_id=2, replica_groups=mesh['yh'=2,'zh'=4,'zc'=2,'x'=4,'y'=4,'c'=2] {'yh'}, dimensions={0}, use_global_device_ids=true | all-gather | bytes 995328 | tf_op jit(solution)/shard_map/all_gather | solution.py:426
  29.8 5.1 %collective-permute-start = (bf16[2,392,256]{2,1,0:T(8,128)(2,1)S(1)}, bf16[2,392,256]{2,1,0:T(8,128)(2,1)S(1)}, u32[]{:S(2)}, u32[]{:S(2)}) collective-permute-start(bf16[2,392,256]{2,1,0:T(8,128)(2,1)S(1)} %slice.59.refs_0_), channel_id=1, source_target_pairs={{0,32},{32,64},{64,96},{96,128},{128,160},{160,192},{192,224},{224... | collective-permute-start | bytes 1204232 | tf_op jit(solution)/shard_map/ppermute | solution.py:40
  34.9 1.9 %collective-permute-start.1 = (bf16[2,392,256]{2,1,0:T(8,128)(2,1)S(1)}, bf16[2,392,256]{2,1,0:T(8,128)(2,1)S(1)}, u32[]{:S(2)}, u32[]{:S(2)}) collective-permute-start(bf16[2,392,256]{2,1,0:T(8,128)(2,1)S(1)} %slice.59.refs_0_), channel_id=1, source_target_pairs={{0,224},{32,0},{64,32},{96,64},{128,96},{160,128},{192,160},{224,1... | collective-permute-start | bytes 1204232 | tf_op jit(solution)/shard_map/ppermute | solution.py:41
  37.5 4.4 %collective-permute-done.refs_1_ = bf16[2,392,256]{2,1,0:T(8,128)(2,1)S(1)} collective-permute-done((bf16[2,392,256]{2,1,0:T(8,128)(2,1)S(1)}, bf16[2,392,256]{2,1,0:T(8,128)(2,1)S(1)}, u32[]{:S(2)}, u32[]{:S(2)}) %collective-permute-start) | collective-permute-done | bytes 401440 | tf_op jit(solution)/shard_map/ppermute | solution.py:40
  41.9 4.4 %collective-permute-start.2 = (bf16[2,392,256]{2,1,0:T(8,128)(2,1)S(1)}, bf16[2,392,256]{2,1,0:T(8,128)(2,1)S(1)}, u32[]{:S(2)}, u32[]{:S(2)}) collective-permute-start(bf16[2,392,256]{2,1,0:T(8,128)(2,1)S(1)} %collective-permute-done.refs_1_), channel_id=1, source_target_pairs={{0,32},{32,64},{64,96},{96,128},{128,160},{160,192},{192,224},{224... | collective-permute-start | bytes 1204232 | tf_op jit(solution)/shard_map/ppermute | solution.py:40
  46.7 8.5 %collective-permute-start.3 = (bf16[2,392,256]{2,1,0:T(8,128)(2,1)S(1)}, bf16[2,392,256]{2,1,0:T(8,128)(2,1)S(1)}, u32[]{:S(2)}, u32[]{:S(2)}) collective-permute-start(bf16[2,392,256]{2,1,0:T(8,128)(2,1)S(1)} %collective-permute-done.1.refs_2_), channel_id=1, source_target_pairs={{0,224},{32,0},{64,32},{96,64},{128,96},{160,128},{192,160},{224,1... | collective-permute-start | bytes 1204232 | tf_op jit(solution)/shard_map/ppermute | solution.py:41
  56.6 2.5 %collective-permute-done.2.refs_3_ = bf16[2,392,256]{2,1,0:T(8,128)(2,1)S(1)} collective-permute-done((bf16[2,392,256]{2,1,0:T(8,128)(2,1)S(1)}, bf16[2,392,256]{2,1,0:T(8,128)(2,1)S(1)}, u32[]{:S(2)}, u32[]{:S(2)}) %collective-permute-start.2) | collective-permute-done | bytes 401440 | tf_op jit(solution)/shard_map/ppermute | solution.py:40
  59.1 1.9 %collective-permute-start.4 = (bf16[2,392,256]{2,1,0:T(8,128)(2,1)S(1)}, bf16[2,392,256]{2,1,0:T(8,128)(2,1)S(1)}, u32[]{:S(2)}, u32[]{:S(2)}) collective-permute-start(bf16[2,392,256]{2,1,0:T(8,128)(2,1)S(1)} %collective-permute-done.2.refs_3_), channel_id=1, source_target_pairs={{0,32},{32,64},{64,96},{96,128},{128,160},{160,192},{192,224},{224... | collective-permute-start | bytes 1204232 | tf_op jit(solution)/shard_map/ppermute | solution.py:40
  61.0 5.1 %collective-permute-start.5 = (bf16[2,392,256]{2,1,0:T(8,128)(2,1)S(1)}, bf16[2,392,256]{2,1,0:T(8,128)(2,1)S(1)}, u32[]{:S(2)}, u32[]{:S(2)}) collective-permute-start(bf16[2,392,256]{2,1,0:T(8,128)(2,1)S(1)} %collective-permute-done.3.refs_4_), channel_id=1, source_target_pairs={{0,224},{32,0},{64,32},{96,64},{128,96},{160,128},{192,160},{224,1... | collective-permute-start | bytes 1204232 | tf_op jit(solution)/shard_map/ppermute | solution.py:41
  67.5 2.8 %collective-permute-done.4.refs_5_ = bf16[2,392,256]{2,1,0:T(8,128)(2,1)S(1)} collective-permute-done((bf16[2,392,256]{2,1,0:T(8,128)(2,1)S(1)}, bf16[2,392,256]{2,1,0:T(8,128)(2,1)S(1)}, u32[]{:S(2)}, u32[]{:S(2)}) %collective-permute-start.4) | collective-permute-done | bytes 401440 | tf_op jit(solution)/shard_map/ppermute | solution.py:40
  70.4 1.9 %collective-permute-start.6 = (bf16[1,392,256]{2,1,0:T(8,128)(2,1)S(1)}, bf16[1,392,256]{2,1,0:T(8,128)(2,1)S(1)}, u32[]{:S(2)}, u32[]{:S(2)}) collective-permute-start(bf16[1,392,256]{2,1,0:T(8,128)(2,1)S(1)} %slice.66), channel_id=1, source_target_pairs={{0,32},{32,64},{64,96},{96,128},{128,160},{160,192},{192,224},{224... | collective-permute-start | bytes 602120 | tf_op jit(solution)/shard_map/ppermute | solution.py:43
  72.4 5.4 %collective-permute-start.7 = (bf16[1,392,256]{2,1,0:T(8,128)(2,1)S(1)}, bf16[1,392,256]{2,1,0:T(8,128)(2,1)S(1)}, u32[]{:S(2)}, u32[]{:S(2)}) collective-permute-start(bf16[1,392,256]{2,1,0:T(8,128)(2,1)S(1)} %slice.68), channel_id=1, source_target_pairs={{0,224},{32,0},{64,32},{96,64},{128,96},{160,128},{192,160},{224,1... | collective-permute-start | bytes 602120 | tf_op jit(solution)/shard_map/ppermute | solution.py:44
  82.3 1.9 %collective-permute-start.8 = (bf16[16,128,256]{2,1,0:T(8,128)(2,1)}, bf16[16,128,256]{2,1,0:T(8,128)(2,1)}, u32[]{:S(2)}, u32[]{:S(2)}) collective-permute-start(bf16[16,128,256]{2,1,0:T(8,128)(2,1)} %slice_dynamic-update-slice_fusion.7), channel_id=1, source_target_pairs={{0,1},{1,0},{2,3},{3,2},{4,5},{5,4},{6,7},{7,6},{8,9},{9,8},{10,11... | collective-permute-start | bytes 3145736 | tf_op jit(solution)/shard_map/ppermute | solution.py:429
  84.9 2.2 %collective-permute-done.8.refs_9_ = bf16[16,128,256]{2,1,0:T(8,128)(2,1)} collective-permute-done((bf16[16,128,256]{2,1,0:T(8,128)(2,1)}, bf16[16,128,256]{2,1,0:T(8,128)(2,1)}, u32[]{:S(2)}, u32[]{:S(2)}) %collective-permute-start.8) | collective-permute-done | bytes 1048608 | tf_op jit(solution)/shard_map/ppermute | solution.py:429
  88.4 5.9 %shard_map.100 = (bf16[1024,640]{1,0:T(8,128)(2,1)S(1)}, bf16[4096,640]{1,0:T(8,128)(2,1)S(1)}) custom-call(s32[2]{0:T(128)S(1)} %pad_add_fusion.scalars, bf16[1024,4096]{1,0:T(8,128)(2,1)} %all-gather.6.cloned.1.call-done.tok_ref, bf16[2,392,256]{2,1,0:T(8,128)(2,1)} %copy-done.1, bf16[2,392,256]{2,1,0:T(8,128)(2,1)} %copy-done.4, ...), custom_call_target="tpu_custom_call" | custom-call | flops 1342177280 | bytes 12582912 | tf_op jit(solution)/shard_map/pallas_call | solution.py:285
  94.3 4.9 %collective-permute-start.9 = (bf16[8,512]{1,0:T(8,128)(2,1)S(1)}, bf16[8,512]{1,0:T(8,128)(2,1)S(1)}, u32[]{:S(2)}, u32[]{:S(2)}) collective-permute-start(bf16[8,512]{1,0:T(8,128)(2,1)S(1)} %slice.56), channel_id=1, source_target_pairs={{0,32},{32,64},{64,96},{96,128},{128,160},{160,192},{192,224},{224... | collective-permute-start | bytes 24584 | tf_op jit(solution)/shard_map/ppermute | solution.py:33
  99.1 7.2 %shard_map.101.proj_ref = bf16[1024,640]{1,0:T(8,128)(2,1)S(1)} custom-call(bf16[1024,4096]{1,0:T(8,128)(2,1)} %all-gather.6.cloned.1.call-done.tok_ref, bf16[4096,640]{1,0:T(8,128)(2,1)S(1)} %get-tuple-element.26.w_ref, bf16[1024,640]{1,0:T(8,128)(2,1)S(1)} %get-tuple-element.27._), custom_call_target="tpu_custom_call", output_to_operand_aliasing={{}: (2, {})} | custom-call | flops 4026531840 | bytes 8388608 | tf_op jit(solution)/shard_map/pallas_call | solution.py:300
  106.4 5.6 %shard_map.102 = (bf16[1024,512]{1,0:T(8,128)(2,1)S(1)}, f32[1024,128]{1,0:T(8,128)S(1)}, f32[1024,128]{1,0:T(8,128)S(1)}, f32[4,128,256]{2,1,0:T(8,128)S(1)}, f...) custom-call(s32[16]{0:T(128)S(1)} %sub.7.starts, s32[1]{0:T(128)} %bitcast.3.base, ...), custom_call_target="tpu_custom_call" | custom-call | flops 67108864 | bytes 4194304 | tf_op jit(solution)/shard_map/pallas_call | solution.py:315
  112.0 6.4 %collective-permute-start.10 = (bf16[144,256]{1,0:T(8,128)(2,1)S(1)}, bf16[144,256]{1,0:T(8,128)(2,1)S(1)}, u32[]{:S(2)}, u32[]{:S(2)}) collective-permute-start(bf16[144,256]{1,0:T(8,128)(2,1)S(1)} %get-tuple-element.39.own_ref), channel_id=1, source_target_pairs={{0,32},{32,0},{1,33},{33,1},{2,34},{34,2},{3,35},{35,3},{4,36},{36... | collective-permute-start | bytes 221192 | tf_op jit(solution)/shard_map/ppermute | solution.py:445
  119.0 1.3 collective-permute-start.12
  120.3 4.6 %shard_map.103 = (f32[1024,256]{1,0:T(8,128)}, f32[1024,256]{1,0:T(8,128)}) custom-call(s32[16]{0:T(128)S(1)} %sub.7.starts, s32[1]{0:T(128)} %bitcast.3.base, bf16[1024,512]{1,0:T(8,128)(2,1)S(1)} %get-tuple-element.29.act_ref, f32[1024,128]{1,0:T(8,128)S(1)} %get-tuple-element.30.cum_ref, f32[1024,128]{1,0:T(8,128)S(1)} %get-tuple-element.31.step_ref, ...), custom_call_target="tpu_custom_call" | custom-call | flops 536870912 | bytes 5242880 | tf_op jit(solution)/shard_map/pallas_call | solution.py:348
  124.9 10.4 %collective-permute-done.12.nine_ref = bf16[144,256]{1,0:T(8,128)(2,1)S(1)} collective-permute-done((bf16[144,256]{1,0:T(8,128)(2,1)S(1)}, bf16[144,256]{1,0:T(8,128)(2,1)S(1)}, u32[]{:S(2)}, u32[]{:S(2)}) %collective-permute-start.12) | collective-permute-done | bytes 73760 | tf_op jit(solution)/shard_map/ppermute | solution.py:444
  136.0 14.1 %all-gather.1 = bf16[576,256]{1,0:T(8,128)(2,1)S(1)} all-gather(bf16[144,256]{1,0:T(8,128)(2,1)S(1)} %shard_map.104), channel_id=3, replica_groups=mesh['yh'=2,'zh'=4,'zc'=2,'x'=4,'y'=4,'c'=2] {'zh'}, dimensions={0}, use_global_device_ids=true | all-gather | bytes 368640 | tf_op jit(solution)/shard_map/all_gather | solution.py:451
  150.1 7.4 %shard_map.105 = bf16[1024,256]{1,0:T(8,128)(2,1)} custom-call(s32[2]{0:T(128)S(1)} %pad_add_fusion.scalars, bf16[144,256]{1,0:T(8,128)(2,1)S(1)} %collective-permute-done.11.eight_ref, bf16[144,256]{1,0:T(8,128)(2,1)S(1)} %collective-permute-done.12.nine_ref, bf16[144,256]{1,0:T(8,128)(2,1)S(1)} %collective-permute-done.10.other_ref, ...), custom_call_target="tpu_custom_call" | custom-call | flops 2214592512 | bytes 13631488 | tf_op jit(solution)/shard_map/pallas_call | solution.py:380
  (68 shorter events, 13.6 us)
Async XLA Ops:
  6.5 80.7 %all-gather.6.cloned.1.call-start = ((), (), s32[]{:S(2)}) async-start(), calls=%async_computation | async-start | bytes 8650752 | tf_op jit(solution)/shard_map/all_gather | solution.py:420
  7.3 142.8 %all-gather.8.cloned.1.call-start = ((), (), s32[]{:S(2)}) async-start(), calls=%async_computation.1 | async-start | bytes 2359296 | tf_op jit(solution)/shard_map/all_gather | solution.py:432
  29.8 57.4 %copy-start.11 = (s32[16]{0:T(128)S(1)}, s32[16]{0:T(128)}, u32[]{:S(2)}) copy-start(s32[16]{0:T(128)} %param.11) | copy-start | bytes 196
  29.8 58.5 %copy-start.12 = (f32[4]{0:T(128)S(1)}, f32[4]{0:T(128)}, u32[]{:S(2)}) copy-start(f32[4]{0:T(128)} %param.19) | copy-start | bytes 52
  29.8 58.5 %copy-start.13 = (f32[4]{0:T(128)S(1)}, f32[4]{0:T(128)}, u32[]{:S(2)}) copy-start(f32[4]{0:T(128)} %param.18) | copy-start | bytes 52
  29.8 58.5 %copy-start.10 = (f32[4,256]{1,0:T(4,128)S(1)}, f32[4,256]{1,0:T(4,128)}, u32[]{:S(2)}) copy-start(f32[4,256]{1,0:T(4,128)} %param.16) | copy-start | bytes 12292
  29.8 58.5 %copy-start.1 = (bf16[2,392,256]{2,1,0:T(8,128)(2,1)}, bf16[2,392,256]{2,1,0:T(8,128)(2,1)S(1)}, u32[]{:S(2)}) copy-start(bf16[2,392,256]{2,1,0:T(8,128)(2,1)S(1)} %slice.59.refs_0_) | copy-start | bytes 1204228
  29.8 12.1 %collective-permute-start = (bf16[2,392,256]{2,1,0:T(8,128)(2,1)S(1)}, bf16[2,392,256]{2,1,0:T(8,128)(2,1)S(1)}, u32[]{:S(2)}, u32[]{:S(2)}) collective-permute-start(bf16[2,392,256]{2,1,0:T(8,128)(2,1)S(1)} %slice.59.refs_0_), channel_id=1, source_target_pairs={{0,32},{32,64},{64,96},{96,128},{128,160},{160,192},{192,224},{224... | collective-permute-start | bytes 1204232 | tf_op jit(solution)/shard_map/ppermute | solution.py:40
  34.9 11.8 %collective-permute-start.1 = (bf16[2,392,256]{2,1,0:T(8,128)(2,1)S(1)}, bf16[2,392,256]{2,1,0:T(8,128)(2,1)S(1)}, u32[]{:S(2)}, u32[]{:S(2)}) collective-permute-start(bf16[2,392,256]{2,1,0:T(8,128)(2,1)S(1)} %slice.59.refs_0_), channel_id=1, source_target_pairs={{0,224},{32,0},{64,32},{96,64},{128,96},{160,128},{192,160},{224,1... | collective-permute-start | bytes 1204232 | tf_op jit(solution)/shard_map/ppermute | solution.py:41
  41.9 46.4 %copy-start.4 = (bf16[2,392,256]{2,1,0:T(8,128)(2,1)}, bf16[2,392,256]{2,1,0:T(8,128)(2,1)S(1)}, u32[]{:S(2)}) copy-start(bf16[2,392,256]{2,1,0:T(8,128)(2,1)S(1)} %collective-permute-done.refs_1_) | copy-start | bytes 1204228
  41.9 17.2 %collective-permute-start.2 = (bf16[2,392,256]{2,1,0:T(8,128)(2,1)S(1)}, bf16[2,392,256]{2,1,0:T(8,128)(2,1)S(1)}, u32[]{:S(2)}, u32[]{:S(2)}) collective-permute-start(bf16[2,392,256]{2,1,0:T(8,128)(2,1)S(1)} %collective-permute-done.refs_1_), channel_id=1, source_target_pairs={{0,32},{32,64},{64,96},{96,128},{128,160},{160,192},{192,224},{224... | collective-permute-start | bytes 1204232 | tf_op jit(solution)/shard_map/ppermute | solution.py:40
  46.7 41.7 %copy-start.5 = (bf16[2,392,256]{2,1,0:T(8,128)(2,1)}, bf16[2,392,256]{2,1,0:T(8,128)(2,1)S(1)}, u32[]{:S(2)}) copy-start(bf16[2,392,256]{2,1,0:T(8,128)(2,1)S(1)} %collective-permute-done.1.refs_2_) | copy-start | bytes 1204228
  46.7 14.3 %collective-permute-start.3 = (bf16[2,392,256]{2,1,0:T(8,128)(2,1)S(1)}, bf16[2,392,256]{2,1,0:T(8,128)(2,1)S(1)}, u32[]{:S(2)}, u32[]{:S(2)}) collective-permute-start(bf16[2,392,256]{2,1,0:T(8,128)(2,1)S(1)} %collective-permute-done.1.refs_2_), channel_id=1, source_target_pairs={{0,224},{32,0},{64,32},{96,64},{128,96},{160,128},{192,160},{224,1... | collective-permute-start | bytes 1204232 | tf_op jit(solution)/shard_map/ppermute | solution.py:41
  59.1 11.3 %collective-permute-start.4 = (bf16[2,392,256]{2,1,0:T(8,128)(2,1)S(1)}, bf16[2,392,256]{2,1,0:T(8,128)(2,1)S(1)}, u32[]{:S(2)}, u32[]{:S(2)}) collective-permute-start(bf16[2,392,256]{2,1,0:T(8,128)(2,1)S(1)} %collective-permute-done.2.refs_3_), channel_id=1, source_target_pairs={{0,32},{32,64},{64,96},{96,128},{128,160},{160,192},{192,224},{224... | collective-permute-start | bytes 1204232 | tf_op jit(solution)/shard_map/ppermute | solution.py:40
  61.0 11.3 %collective-permute-start.5 = (bf16[2,392,256]{2,1,0:T(8,128)(2,1)S(1)}, bf16[2,392,256]{2,1,0:T(8,128)(2,1)S(1)}, u32[]{:S(2)}, u32[]{:S(2)}) collective-permute-start(bf16[2,392,256]{2,1,0:T(8,128)(2,1)S(1)} %collective-permute-done.3.refs_4_), channel_id=1, source_target_pairs={{0,224},{32,0},{64,32},{96,64},{128,96},{160,128},{192,160},{224,1... | collective-permute-start | bytes 1204232 | tf_op jit(solution)/shard_map/ppermute | solution.py:41
  70.3 18.0 %copy-start.2 = (bf16[2,392,256]{2,1,0:T(8,128)(2,1)}, bf16[2,392,256]{2,1,0:T(8,128)(2,1)S(1)}, u32[]{:S(2)}) copy-start(bf16[2,392,256]{2,1,0:T(8,128)(2,1)S(1)} %collective-permute-done.4.refs_5_) | copy-start | bytes 1204228
  70.4 9.1 %collective-permute-start.6 = (bf16[1,392,256]{2,1,0:T(8,128)(2,1)S(1)}, bf16[1,392,256]{2,1,0:T(8,128)(2,1)S(1)}, u32[]{:S(2)}, u32[]{:S(2)}) collective-permute-start(bf16[1,392,256]{2,1,0:T(8,128)(2,1)S(1)} %slice.66), channel_id=1, source_target_pairs={{0,32},{32,64},{64,96},{96,128},{128,160},{160,192},{192,224},{224... | collective-permute-start | bytes 602120 | tf_op jit(solution)/shard_map/ppermute | solution.py:43
  72.3 16.0 %copy-start.3 = (bf16[2,392,256]{2,1,0:T(8,128)(2,1)}, bf16[2,392,256]{2,1,0:T(8,128)(2,1)S(1)}, u32[]{:S(2)}) copy-start(bf16[2,392,256]{2,1,0:T(8,128)(2,1)S(1)} %collective-permute-done.5.refs_6_) | copy-start | bytes 1204228
  72.4 8.6 %collective-permute-start.7 = (bf16[1,392,256]{2,1,0:T(8,128)(2,1)S(1)}, bf16[1,392,256]{2,1,0:T(8,128)(2,1)S(1)}, u32[]{:S(2)}, u32[]{:S(2)}) collective-permute-start(bf16[1,392,256]{2,1,0:T(8,128)(2,1)S(1)} %slice.68), channel_id=1, source_target_pairs={{0,224},{32,0},{64,32},{96,64},{128,96},{160,128},{192,160},{224,1... | collective-permute-start | bytes 602120 | tf_op jit(solution)/shard_map/ppermute | solution.py:44
  82.3 4.9 %collective-permute-start.8 = (bf16[16,128,256]{2,1,0:T(8,128)(2,1)}, bf16[16,128,256]{2,1,0:T(8,128)(2,1)}, u32[]{:S(2)}, u32[]{:S(2)}) collective-permute-start(bf16[16,128,256]{2,1,0:T(8,128)(2,1)} %slice_dynamic-update-slice_fusion.7), channel_id=1, source_target_pairs={{0,1},{1,0},{2,3},{3,2},{4,5},{5,4},{6,7},{7,6},{8,9},{9,8},{10,11... | collective-permute-start | bytes 3145736 | tf_op jit(solution)/shard_map/ppermute | solution.py:429
  94.3 12.1 %collective-permute-start.9 = (bf16[8,512]{1,0:T(8,128)(2,1)S(1)}, bf16[8,512]{1,0:T(8,128)(2,1)S(1)}, u32[]{:S(2)}, u32[]{:S(2)}) collective-permute-start(bf16[8,512]{1,0:T(8,128)(2,1)S(1)} %slice.56), channel_id=1, source_target_pairs={{0,32},{32,64},{64,96},{96,128},{128,160},{160,192},{192,224},{224... | collective-permute-start | bytes 24584 | tf_op jit(solution)/shard_map/ppermute | solution.py:33
  112.0 12.9 %collective-permute-start.10 = (bf16[144,256]{1,0:T(8,128)(2,1)S(1)}, bf16[144,256]{1,0:T(8,128)(2,1)S(1)}, u32[]{:S(2)}, u32[]{:S(2)}) collective-permute-start(bf16[144,256]{1,0:T(8,128)(2,1)S(1)} %get-tuple-element.39.own_ref), channel_id=1, source_target_pairs={{0,32},{32,0},{1,33},{33,1},{2,34},{34,2},{3,35},{35,3},{4,36},{36... | collective-permute-start | bytes 221192 | tf_op jit(solution)/shard_map/ppermute | solution.py:445
  118.4 6.5 %collective-permute-start.11 = (bf16[144,256]{1,0:T(8,128)(2,1)S(1)}, bf16[144,256]{1,0:T(8,128)(2,1)S(1)}, u32[]{:S(2)}, u32[]{:S(2)}) collective-permute-start(bf16[144,256]{1,0:T(8,128)(2,1)S(1)} %get-tuple-element.39.own_ref), channel_id=1, source_target_pairs={{224,256},{225,257},{226,258},{227,259},{228,260},{229,261},{230,2... | collective-permute-start | bytes 221192 | tf_op jit(solution)/shard_map/ppermute | solution.py:443
  119.0 16.3 %collective-permute-start.12 = (bf16[144,256]{1,0:T(8,128)(2,1)S(1)}, bf16[144,256]{1,0:T(8,128)(2,1)S(1)}, u32[]{:S(2)}, u32[]{:S(2)}) collective-permute-start(bf16[144,256]{1,0:T(8,128)(2,1)S(1)} %get-tuple-element.39.own_ref), channel_id=1, source_target_pairs={{224,288},{225,289},{226,290},{227,291},{228,292},{229,293},{230,2... | collective-permute-start | bytes 221192 | tf_op jit(solution)/shard_map/ppermute | solution.py:444
  (5 other events, 35.3 us)
Sparse Core Ops, SparseCore 0:
  9.5 73.5 all-gather.5
  87.3 49.3 all-gather.7

commit v8 on v6

--- a/solution.py
+++ b/solution.py
@@ -258,8 +258,9 @@
         later = gain_of(even)[0:1] * state + even[0:STATE].astype(F32)
         entering[...] = jnp.where(odd == 1, later, state).astype(BF16)
         for k in range(Z):
-            for yh in range(YH):
-                weights[pl.ds((yh * Z + k) * 256, 256), :] = w_ref[k, yh]
+            for slot in range(YH):
+                row = ((scalars[2] + slot) % YH * Z + k) * 256
+                weights[pl.ds(pl.multiple_of(row, 256), 256), :] = w_ref[k, slot]
 
     gate = jnp.dot(tok_ref[...], weights[...], preferred_element_type=F32).astype(BF16)
     carried = jnp.dot(act_ref[...], entering[...], preferred_element_type=F32)
@@ -419,16 +420,18 @@
     state_half = lax.dynamic_slice(state_weight, (group, core * 128, 0), (1, 128, 256))[0]
     conv_own = lax.dynamic_index_in_dim(state_conv, group, 0, keepdims=False)
     step_rows = jnp.pad(step_weight.T, ((0, 8 - heads_here), (0, 0)))
-    pack = jnp.concatenate([value_weight, state_half, step_rows, gate_weight], axis=0)
+    pack = jnp.concatenate([value_weight, state_half, step_rows], axis=0)
     both = lax.all_gather(pack, "yh", axis=0, tiled=False)
-    pieces = ring_gather(both[:, :392])
+    pieces = ring_gather(both)
     halves = jnp.concatenate([piece[:, 256:384] for _, _, piece in pieces], axis=0)
+    gate_own, _ = lax.optimization_barrier((gate_weight, halves))
     halves = lax.ppermute(halves, "c", [(0, 1), (1, 0)])
-    scalars = jnp.stack([z, core]).astype(jnp.int32)
-    gate_part, gathered, halves = lax.optimization_barrier((both[:, 392:], gathered, halves))
-    gate_all = lax.all_gather(gate_part, RING, axis=0, tiled=False)
+    gate_far = lax.ppermute(gate_own, "yh", ring(YH, 1))
+    scalars = jnp.stack([z, core, lax.axis_index("yh")]).astype(jnp.int32)
     gathered = in_hbm(gathered)
     proj, weights = run_first(gathered, pieces, halves, scalars)
+    gate_far, proj = lax.optimization_barrier((gate_far, proj))
+    gate_all = lax.all_gather(jnp.stack([gate_weight, gate_far]), RING, axis=0, tiled=False)
     rim = along_seq(proj[-8:, :512], 1)
     proj = run_rest(gathered, weights, proj)
 

time: 163 us -> 165 us (1.012)
  blocking collectives: 52.3 us -> 39.7 us
  starting transfers between devices: 40.8 us -> 52.2 us
  local copies, waits for them, and re-layouts: 8.64 us -> 13.2 us
  waiting for transfers between devices: 15.2 us -> 11.3 us
  other arithmetic: 1.26 us -> 3.48 us
    ppermute x0 -> x1, starting transfers between devices: none -> 13.6 us  [local(): gate_far = lax.ppermute(gate_own, 'yh', ring(YH, 1))]
    all_gather x1, blocking collectives: 20.7 us -> 13.3 us  [local(): both = lax.all_gather(pack, 'yh', axis=0, tiled=False)]
    unnamed x36 -> x42, local copies, waits for them, and re-layouts: 6.47 us -> 11.7 us
    all_gather x1, blocking collectives: 23.7 us -> 18.8 us  [local(): lax.all_gather(run_pair(own, eight, nine), 'zh', axis=0, tiled=False)]
    ppermute x1, waiting for transfers between devices: 2.26 us -> 0.01 us  [local(): halves = lax.ppermute(halves, 'c', [(0, 1), (1, 0)])]
    ppermute x1, starting transfers between devices: 3.25 us -> 1.29 us  [along_seq(): lax.ppermute(value, SEQ, [(i, i + step) for i in range(YH * Z - step)])]
    ppermute x3, waiting for transfers between devices: 11 us -> 9.32 us  [ring_gather(): right = lax.ppermute(right, RING, ring(Z, 1))]
  transfers between devices with their start and end apart: 14 -> 15, of which waited for: 5 -> 5; matrix products, arithmetic and copies ran while one was open for 5% -> 5% of each run, Pallas kernels for 14% -> 14%
where the time goes in v8:
time: 165 us; the launch traced here: 164 us
  starting transfers between devices  52.2 us (32%)
  blocking collectives  39.7 us (24%)
  Pallas kernels  30.5 us (18%)
  between operations  13.7 us (8%)
  local copies, waits for them, and re-layouts  13.2 us (8%)
  waiting for transfers between devices  11.3 us (7%)
  other arithmetic  3.48 us (2%)
    ppermute x3, starting transfers between devices, ring_gather(): left = lax.ppermute(left, RING, ring(Z, -1))  18.9 us
    all_gather x1, blocking collectives, local(): lax.all_gather(run_pair(own, eight, nine), 'zh', axis=0, tiled=False)  18.8 us
    ppermute x1, starting transfers between devices, local(): gate_far = lax.ppermute(gate_own, 'yh', ring(YH, 1))  13.6 us
    all_gather x1, blocking collectives, local(): both = lax.all_gather(pack, 'yh', axis=0, tiled=False)  13.3 us
    unnamed x42, local copies, waits for them, and re-layouts  11.7 us
    ppermute x3, waiting for transfers between devices, ring_gather(): right = lax.ppermute(right, RING, ring(Z, 1))  9.32 us
    ppermute x3, starting transfers between devices, ring_gather(): right = lax.ppermute(right, RING, ring(Z, 1))  8.09 us
    all_gather x1, blocking collectives, local(): own = lax.all_gather(packed, 'zc', axis=0, tiled=False)  7.62 us
  transfers between devices with their start and end apart: 15, of which 5 were waited for; matrix products, arithmetic and copies ran while one was open for 5% of the time, Pallas kernels for 14%

profile of v8, /device:TPU:6, one launch (start us, length us, event | category | flops | bytes accessed | tf_op | source)
XLA Modules:
  0.0 164.1 jit_solution(17771192928922237700)
XLA Ops:
  8.7 13.3 %all-gather = bf16[784,256]{1,0:T(8,128)(2,1)S(1)} all-gather(bf16[392,256]{1,0:T(8,128)(2,1)S(1)} %fusion.1), channel_id=2, replica_groups=mesh['yh'=2,'zh'=4,'zc'=2,'x'=4,'y'=4,'c'=2] {'yh'}, dimensions={0}, use_global_device_ids=true | all-gather | bytes 602112 | tf_op jit(solution)/shard_map/all_gather | solution.py:424
  22.0 4.3 %collective-permute-start = (bf16[2,392,256]{2,1,0:T(8,128)(2,1)S(1)}, bf16[2,392,256]{2,1,0:T(8,128)(2,1)S(1)}, u32[]{:S(2)}, u32[]{:S(2)}) collective-permute-start(bf16[2,392,256]{2,1,0:T(8,128)(2,1)S(1)} %bitcast.21), channel_id=1, source_target_pairs={{0,32},{32,64},{64,96},{96,128},{128,160},{160,192},{192,224},{224... | collective-permute-start | bytes 1204232 | tf_op jit(solution)/shard_map/ppermute | solution.py:40
  26.3 8.6 %collective-permute-start.1 = (bf16[2,392,256]{2,1,0:T(8,128)(2,1)S(1)}, bf16[2,392,256]{2,1,0:T(8,128)(2,1)S(1)}, u32[]{:S(2)}, u32[]{:S(2)}) collective-permute-start(bf16[2,392,256]{2,1,0:T(8,128)(2,1)S(1)} %bitcast.22), channel_id=1, source_target_pairs={{0,224},{32,0},{64,32},{96,64},{128,96},{160,128},{192,160},{224,1... | collective-permute-start | bytes 1204232 | tf_op jit(solution)/shard_map/ppermute | solution.py:41
  35.5 4.2 %collective-permute-done.refs_1_ = bf16[2,392,256]{2,1,0:T(8,128)(2,1)S(1)} collective-permute-done((bf16[2,392,256]{2,1,0:T(8,128)(2,1)S(1)}, bf16[2,392,256]{2,1,0:T(8,128)(2,1)S(1)}, u32[]{:S(2)}, u32[]{:S(2)}) %collective-permute-start) | collective-permute-done | bytes 401440 | tf_op jit(solution)/shard_map/ppermute | solution.py:40
  39.7 1.9 %collective-permute-start.2 = (bf16[2,392,256]{2,1,0:T(8,128)(2,1)S(1)}, bf16[2,392,256]{2,1,0:T(8,128)(2,1)S(1)}, u32[]{:S(2)}, u32[]{:S(2)}) collective-permute-start(bf16[2,392,256]{2,1,0:T(8,128)(2,1)S(1)} %collective-permute-done.refs_1_), channel_id=1, source_target_pairs={{0,32},{32,64},{64,96},{96,128},{128,160},{160,192},{192,224},{224... | collective-permute-start | bytes 1204232 | tf_op jit(solution)/shard_map/ppermute | solution.py:40
  41.6 5.1 %collective-permute-start.3 = (bf16[2,392,256]{2,1,0:T(8,128)(2,1)S(1)}, bf16[2,392,256]{2,1,0:T(8,128)(2,1)S(1)}, u32[]{:S(2)}, u32[]{:S(2)}) collective-permute-start(bf16[2,392,256]{2,1,0:T(8,128)(2,1)S(1)} %collective-permute-done.1.refs_2_), channel_id=1, source_target_pairs={{0,224},{32,0},{64,32},{96,64},{128,96},{160,128},{192,160},{224,1... | collective-permute-start | bytes 1204232 | tf_op jit(solution)/shard_map/ppermute | solution.py:41
  48.1 2.6 %collective-permute-done.2.refs_3_ = bf16[2,392,256]{2,1,0:T(8,128)(2,1)S(1)} collective-permute-done((bf16[2,392,256]{2,1,0:T(8,128)(2,1)S(1)}, bf16[2,392,256]{2,1,0:T(8,128)(2,1)S(1)}, u32[]{:S(2)}, u32[]{:S(2)}) %collective-permute-start.2) | collective-permute-done | bytes 401440 | tf_op jit(solution)/shard_map/ppermute | solution.py:40
  50.7 1.9 %collective-permute-start.4 = (bf16[2,392,256]{2,1,0:T(8,128)(2,1)S(1)}, bf16[2,392,256]{2,1,0:T(8,128)(2,1)S(1)}, u32[]{:S(2)}, u32[]{:S(2)}) collective-permute-start(bf16[2,392,256]{2,1,0:T(8,128)(2,1)S(1)} %collective-permute-done.2.refs_3_), channel_id=1, source_target_pairs={{0,32},{32,64},{64,96},{96,128},{128,160},{160,192},{192,224},{224... | collective-permute-start | bytes 1204232 | tf_op jit(solution)/shard_map/ppermute | solution.py:40
  52.6 5.1 %collective-permute-start.5 = (bf16[2,392,256]{2,1,0:T(8,128)(2,1)S(1)}, bf16[2,392,256]{2,1,0:T(8,128)(2,1)S(1)}, u32[]{:S(2)}, u32[]{:S(2)}) collective-permute-start(bf16[2,392,256]{2,1,0:T(8,128)(2,1)S(1)} %collective-permute-done.3.refs_4_), channel_id=1, source_target_pairs={{0,224},{32,0},{64,32},{96,64},{128,96},{160,128},{192,160},{224,1... | collective-permute-start | bytes 1204232 | tf_op jit(solution)/shard_map/ppermute | solution.py:41
  59.1 2.6 %collective-permute-done.4.refs_5_ = bf16[2,392,256]{2,1,0:T(8,128)(2,1)S(1)} collective-permute-done((bf16[2,392,256]{2,1,0:T(8,128)(2,1)S(1)}, bf16[2,392,256]{2,1,0:T(8,128)(2,1)S(1)}, u32[]{:S(2)}, u32[]{:S(2)}) %collective-permute-start.4) | collective-permute-done | bytes 401440 | tf_op jit(solution)/shard_map/ppermute | solution.py:40
  61.7 1.9 %collective-permute-start.6 = (bf16[1,392,256]{2,1,0:T(8,128)(2,1)S(1)}, bf16[1,392,256]{2,1,0:T(8,128)(2,1)S(1)}, u32[]{:S(2)}, u32[]{:S(2)}) collective-permute-start(bf16[1,392,256]{2,1,0:T(8,128)(2,1)S(1)} %slice.48), channel_id=1, source_target_pairs={{0,32},{32,64},{64,96},{96,128},{128,160},{160,192},{192,224},{224... | collective-permute-start | bytes 602120 | tf_op jit(solution)/shard_map/ppermute | solution.py:43
  63.6 5.2 %collective-permute-start.7 = (bf16[1,392,256]{2,1,0:T(8,128)(2,1)S(1)}, bf16[1,392,256]{2,1,0:T(8,128)(2,1)S(1)}, u32[]{:S(2)}, u32[]{:S(2)}) collective-permute-start(bf16[1,392,256]{2,1,0:T(8,128)(2,1)S(1)} %slice.49), channel_id=1, source_target_pairs={{0,224},{32,0},{64,32},{96,64},{128,96},{160,128},{192,160},{224,1... | collective-permute-start | bytes 602120 | tf_op jit(solution)/shard_map/ppermute | solution.py:44
  72.8 1.9 %collective-permute-start.8 = (bf16[16,128,256]{2,1,0:T(8,128)(2,1)}, bf16[16,128,256]{2,1,0:T(8,128)(2,1)S(1)}, u32[]{:S(2)}, u32[]{:S(2)}) collective-permute-start(bf16[16,128,256]{2,1,0:T(8,128)(2,1)} %slice_dynamic-update-slice_fusion.7), channel_id=1, source_target_pairs={{0,1},{1,0},{2,3},{3,2},{4,5},{5,4},{6,7},{7,6},{8,9},{9,8},{10,11... | collective-permute-start | bytes 3145736 | tf_op jit(solution)/shard_map/ppermute | solution.py:428
  74.7 13.6 %collective-permute-start.9 = (bf16[256,256]{1,0:T(8,128)(2,1)S(1)}, bf16[256,256]{1,0:T(8,128)(2,1)}, u32[]{:S(2)}, u32[]{:S(2)}) collective-permute-start(bf16[256,256]{1,0:T(8,128)(2,1)S(1)} %copy-done.13), channel_id=1, source_target_pairs={{0,256},{256,0},{1,257},{257,1},{2,258},{258,2},{3,259},{259,3},{4... | collective-permute-start | bytes 393224 | tf_op jit(solution)/shard_map/ppermute | solution.py:429
  89.4 5.9 %shard_map.100 = (bf16[1024,640]{1,0:T(8,128)(2,1)S(1)}, bf16[4096,640]{1,0:T(8,128)(2,1)S(1)}) custom-call(s32[3]{0:T(128)S(1)} %pad_add_fusion.scalars, bf16[1024,4096]{1,0:T(8,128)(2,1)} %all-gather.7.cloned.1.call-done.tok_ref, bf16[2,392,256]{2,1,0:T(8,128)(2,1)} %bitcast.24, bf16[2,392,256]{2,1,0:T(8,128)(2,1)} %copy-done.7, ...), custom_call_target="tpu_custom_call" | custom-call | flops 1342177280 | bytes 12582912 | tf_op jit(solution)/shard_map/pallas_call | solution.py:284
  95.3 2.4 %copy-done.1 = bf16[4096,640]{1,0:T(8,128)(2,1)} copy-done((bf16[4096,640]{1,0:T(8,128)(2,1)}, bf16[4096,640]{1,0:T(8,128)(2,1)S(1)}, u32[]{:S(2)}) %copy-start.1) | copy-done | bytes 5242904
  97.7 1.6 pad_maximum_fusion
  102.3 2.5 %copy-done.2 = bf16[4096,640]{1,0:T(8,128)(2,1)S(1)} copy-done((bf16[4096,640]{1,0:T(8,128)(2,1)S(1)}, bf16[4096,640]{1,0:T(8,128)(2,1)}, u32[]{:S(2)}) %copy-start.2) | copy-done | bytes 5242904
  104.8 7.0 %shard_map.101.proj_ref = bf16[1024,640]{1,0:T(8,128)(2,1)S(1)} custom-call(bf16[1024,4096]{1,0:T(8,128)(2,1)} %all-gather.7.cloned.1.call-done.tok_ref, bf16[4096,640]{1,0:T(8,128)(2,1)S(1)} %copy-done.2, bf16[1024,640]{1,0:T(8,128)(2,1)S(1)} %get-tuple-element.27._), custom_call_target="tpu_custom_call", output_to_operand_aliasing={{}: (2, {})} | custom-call | flops 4026531840 | bytes 8388608 | tf_op jit(solution)/shard_map/pallas_call | solution.py:299
  111.9 5.6 %shard_map.102 = (bf16[1024,512]{1,0:T(8,128)(2,1)S(1)}, f32[1024,128]{1,0:T(8,128)S(1)}, f32[1024,128]{1,0:T(8,128)S(1)}, f32[4,128,256]{2,1,0:T(8,128)S(1)}, f...) custom-call(s32[16]{0:T(128)S(1)} %sub.7.starts, s32[1]{0:T(128)} %bitcast.4.base, ...), custom_call_target="tpu_custom_call" | custom-call | flops 67108864 | bytes 4194304 | tf_op jit(solution)/shard_map/pallas_call | solution.py:314
  118.8 4.6 %shard_map.103 = (f32[1024,256]{1,0:T(8,128)}, f32[1024,256]{1,0:T(8,128)}) custom-call(s32[16]{0:T(128)S(1)} %sub.7.starts, s32[1]{0:T(128)} %bitcast.4.base, bf16[1024,512]{1,0:T(8,128)(2,1)S(1)} %get-tuple-element.29.act_ref, f32[1024,128]{1,0:T(8,128)S(1)} %get-tuple-element.30.cum_ref, f32[1024,128]{1,0:T(8,128)S(1)} %get-tuple-element.31.step_ref, ...), custom_call_target="tpu_custom_call" | custom-call | flops 536870912 | bytes 5242880 | tf_op jit(solution)/shard_map/pallas_call | solution.py:347
  123.4 7.6 %all-gather.1 = bf16[288,256]{1,0:T(8,128)(2,1)S(1)} all-gather(bf16[144,256]{1,0:T(8,128)(2,1)S(1)} %get-tuple-element.36), channel_id=3, replica_groups=mesh['yh'=2,'zh'=4,'zc'=2,'x'=4,'y'=4,'c'=2] {'zc'}, dimensions={0}, use_global_device_ids=true | all-gather | bytes 221184 | tf_op jit(solution)/shard_map/all_gather | solution.py:447
  131.1 18.8 %all-gather.2 = bf16[576,256]{1,0:T(8,128)(2,1)S(1)} all-gather(bf16[144,256]{1,0:T(8,128)(2,1)S(1)} %shard_map.104), channel_id=4, replica_groups=mesh['yh'=2,'zh'=4,'zc'=2,'x'=4,'y'=4,'c'=2] {'zh'}, dimensions={0}, use_global_device_ids=true | all-gather | bytes 368640 | tf_op jit(solution)/shard_map/all_gather | solution.py:449
  149.9 7.4 %shard_map.105 = bf16[1024,256]{1,0:T(8,128)(2,1)} custom-call(s32[3]{0:T(128)S(1)} %pad_add_fusion.scalars, bf16[144,256]{1,0:T(8,128)(2,1)S(1)} %collective-permute-done.11.eight_ref, bf16[144,256]{1,0:T(8,128)(2,1)S(1)} %collective-permute-done.12.nine_ref, bf16[2,144,256]{2,1,0:T(8,128)(2,1)S(1)} %bitcast.19, bf16[4,144,256]{2,1,0:T(8,128)(2,1)S(1)} %bitcast.20, ...), custom_call_target="tpu_custom_call" | custom-call | flops 2214592512 | bytes 13631488 | tf_op jit(solution)/shard_map/pallas_call | solution.py:378
  (74 shorter events, 14.8 us)
Async XLA Ops:
  6.5 82.9 %all-gather.7.cloned.1.call-start = ((), (), s32[]{:S(2)}) async-start(), calls=%async_computation | async-start | bytes 8650752 | tf_op jit(solution)/shard_map/all_gather | solution.py:418
  7.3 67.5 %copy-start.13 = (bf16[256,256]{1,0:T(8,128)(2,1)S(1)}, bf16[256,256]{1,0:T(8,128)(2,1)}, u32[]{:S(2)}) copy-start(bf16[256,256]{1,0:T(8,128)(2,1)} %param.13) | copy-start | bytes 393220
  7.3 142.6 %all-gather.9.cloned.1.call-start = ((), (), s32[]{:S(2)}) async-start(), calls=%async_computation.1 | async-start | bytes 2359296 | tf_op jit(solution)/shard_map/all_gather | solution.py:434
  22.0 67.4 %copy-start.3 = (bf16[784,256]{1,0:T(8,128)(2,1)}, bf16[784,256]{1,0:T(8,128)(2,1)S(1)}, u32[]{:S(2)}) copy-start(bf16[784,256]{1,0:T(8,128)(2,1)S(1)} %all-gather) | copy-start | bytes 1204228
  22.0 17.7 %collective-permute-start = (bf16[2,392,256]{2,1,0:T(8,128)(2,1)S(1)}, bf16[2,392,256]{2,1,0:T(8,128)(2,1)S(1)}, u32[]{:S(2)}, u32[]{:S(2)}) collective-permute-start(bf16[2,392,256]{2,1,0:T(8,128)(2,1)S(1)} %bitcast.21), channel_id=1, source_target_pairs={{0,32},{32,64},{64,96},{96,128},{128,160},{160,192},{192,224},{224... | collective-permute-start | bytes 1204232 | tf_op jit(solution)/shard_map/ppermute | solution.py:40
  26.3 15.4 %collective-permute-start.1 = (bf16[2,392,256]{2,1,0:T(8,128)(2,1)S(1)}, bf16[2,392,256]{2,1,0:T(8,128)(2,1)S(1)}, u32[]{:S(2)}, u32[]{:S(2)}) collective-permute-start(bf16[2,392,256]{2,1,0:T(8,128)(2,1)S(1)} %bitcast.22), channel_id=1, source_target_pairs={{0,224},{32,0},{64,32},{96,64},{128,96},{160,128},{192,160},{224,1... | collective-permute-start | bytes 1204232 | tf_op jit(solution)/shard_map/ppermute | solution.py:41
  39.7 12.9 %copy-start.7 = (bf16[2,392,256]{2,1,0:T(8,128)(2,1)}, bf16[2,392,256]{2,1,0:T(8,128)(2,1)S(1)}, u32[]{:S(2)}) copy-start(bf16[2,392,256]{2,1,0:T(8,128)(2,1)S(1)} %collective-permute-done.refs_1_) | copy-start | bytes 1204228
  39.7 11.0 %collective-permute-start.2 = (bf16[2,392,256]{2,1,0:T(8,128)(2,1)S(1)}, bf16[2,392,256]{2,1,0:T(8,128)(2,1)S(1)}, u32[]{:S(2)}, u32[]{:S(2)}) collective-permute-start(bf16[2,392,256]{2,1,0:T(8,128)(2,1)S(1)} %collective-permute-done.refs_1_), channel_id=1, source_target_pairs={{0,32},{32,64},{64,96},{96,128},{128,160},{160,192},{192,224},{224... | collective-permute-start | bytes 1204232 | tf_op jit(solution)/shard_map/ppermute | solution.py:40
  41.6 30.4 %copy-start.8 = (bf16[2,392,256]{2,1,0:T(8,128)(2,1)}, bf16[2,392,256]{2,1,0:T(8,128)(2,1)S(1)}, u32[]{:S(2)}) copy-start(bf16[2,392,256]{2,1,0:T(8,128)(2,1)S(1)} %collective-permute-done.1.refs_2_) | copy-start | bytes 1204228
  41.6 11.0 %collective-permute-start.3 = (bf16[2,392,256]{2,1,0:T(8,128)(2,1)S(1)}, bf16[2,392,256]{2,1,0:T(8,128)(2,1)S(1)}, u32[]{:S(2)}, u32[]{:S(2)}) collective-permute-start(bf16[2,392,256]{2,1,0:T(8,128)(2,1)S(1)} %collective-permute-done.1.refs_2_), channel_id=1, source_target_pairs={{0,224},{32,0},{64,32},{96,64},{128,96},{160,128},{192,160},{224,1... | collective-permute-start | bytes 1204232 | tf_op jit(solution)/shard_map/ppermute | solution.py:41
  50.7 22.1 %copy-start.9 = (bf16[2,392,256]{2,1,0:T(8,128)(2,1)}, bf16[2,392,256]{2,1,0:T(8,128)(2,1)S(1)}, u32[]{:S(2)}) copy-start(bf16[2,392,256]{2,1,0:T(8,128)(2,1)S(1)} %collective-permute-done.2.refs_3_) | copy-start | bytes 1204228
  50.7 11.0 %collective-permute-start.4 = (bf16[2,392,256]{2,1,0:T(8,128)(2,1)S(1)}, bf16[2,392,256]{2,1,0:T(8,128)(2,1)S(1)}, u32[]{:S(2)}, u32[]{:S(2)}) collective-permute-start(bf16[2,392,256]{2,1,0:T(8,128)(2,1)S(1)} %collective-permute-done.2.refs_3_), channel_id=1, source_target_pairs={{0,32},{32,64},{64,96},{96,128},{128,160},{160,192},{192,224},{224... | collective-permute-start | bytes 1204232 | tf_op jit(solution)/shard_map/ppermute | solution.py:40
  52.6 20.1 %copy-start.10 = (bf16[2,392,256]{2,1,0:T(8,128)(2,1)}, bf16[2,392,256]{2,1,0:T(8,128)(2,1)S(1)}, u32[]{:S(2)}) copy-start(bf16[2,392,256]{2,1,0:T(8,128)(2,1)S(1)} %collective-permute-done.3.refs_4_) | copy-start | bytes 1204228
  52.6 11.0 %collective-permute-start.5 = (bf16[2,392,256]{2,1,0:T(8,128)(2,1)S(1)}, bf16[2,392,256]{2,1,0:T(8,128)(2,1)S(1)}, u32[]{:S(2)}, u32[]{:S(2)}) collective-permute-start(bf16[2,392,256]{2,1,0:T(8,128)(2,1)S(1)} %collective-permute-done.3.refs_4_), channel_id=1, source_target_pairs={{0,224},{32,0},{64,32},{96,64},{128,96},{160,128},{192,160},{224,1... | collective-permute-start | bytes 1204232 | tf_op jit(solution)/shard_map/ppermute | solution.py:41
  61.6 27.8 %copy-start.4 = (bf16[2,392,256]{2,1,0:T(8,128)(2,1)}, bf16[2,392,256]{2,1,0:T(8,128)(2,1)S(1)}, u32[]{:S(2)}) copy-start(bf16[2,392,256]{2,1,0:T(8,128)(2,1)S(1)} %collective-permute-done.4.refs_5_) | copy-start | bytes 1204228
  61.7 8.8 %collective-permute-start.6 = (bf16[1,392,256]{2,1,0:T(8,128)(2,1)S(1)}, bf16[1,392,256]{2,1,0:T(8,128)(2,1)S(1)}, u32[]{:S(2)}, u32[]{:S(2)}) collective-permute-start(bf16[1,392,256]{2,1,0:T(8,128)(2,1)S(1)} %slice.48), channel_id=1, source_target_pairs={{0,32},{32,64},{64,96},{96,128},{128,160},{160,192},{192,224},{224... | collective-permute-start | bytes 602120 | tf_op jit(solution)/shard_map/ppermute | solution.py:43
  63.6 8.4 %collective-permute-start.7 = (bf16[1,392,256]{2,1,0:T(8,128)(2,1)S(1)}, bf16[1,392,256]{2,1,0:T(8,128)(2,1)S(1)}, u32[]{:S(2)}, u32[]{:S(2)}) collective-permute-start(bf16[1,392,256]{2,1,0:T(8,128)(2,1)S(1)} %slice.49), channel_id=1, source_target_pairs={{0,224},{32,0},{64,32},{96,64},{128,96},{160,128},{192,160},{224,1... | collective-permute-start | bytes 602120 | tf_op jit(solution)/shard_map/ppermute | solution.py:44
  72.8 15.6 %collective-permute-start.8 = (bf16[16,128,256]{2,1,0:T(8,128)(2,1)}, bf16[16,128,256]{2,1,0:T(8,128)(2,1)S(1)}, u32[]{:S(2)}, u32[]{:S(2)}) collective-permute-start(bf16[16,128,256]{2,1,0:T(8,128)(2,1)} %slice_dynamic-update-slice_fusion.7), channel_id=1, source_target_pairs={{0,1},{1,0},{2,3},{3,2},{4,5},{5,4},{6,7},{7,6},{8,9},{9,8},{10,11... | collective-permute-start | bytes 3145736 | tf_op jit(solution)/shard_map/ppermute | solution.py:428
  74.7 23.0 %collective-permute-start.9 = (bf16[256,256]{1,0:T(8,128)(2,1)S(1)}, bf16[256,256]{1,0:T(8,128)(2,1)}, u32[]{:S(2)}, u32[]{:S(2)}) collective-permute-start(bf16[256,256]{1,0:T(8,128)(2,1)S(1)} %copy-done.13), channel_id=1, source_target_pairs={{0,256},{256,0},{1,257},{257,1},{2,258},{258,2},{3,259},{259,3},{4... | collective-permute-start | bytes 393224 | tf_op jit(solution)/shard_map/ppermute | solution.py:429
  88.4 12.0 %copy-start.16 = (f32[4]{0:T(128)S(1)}, f32[4]{0:T(128)}, u32[]{:S(2)}) copy-start(f32[4]{0:T(128)} %param.19) | copy-start | bytes 52
  88.4 12.6 %copy-start.14 = (f32[4,256]{1,0:T(4,128)S(1)}, f32[4,256]{1,0:T(4,128)}, u32[]{:S(2)}) copy-start(f32[4,256]{1,0:T(4,128)} %param.16) | copy-start | bytes 12292
  101.0 10.8 %collective-permute-start.10 = (bf16[8,512]{1,0:T(8,128)(2,1)S(1)}, bf16[8,512]{1,0:T(8,128)(2,1)S(1)}, u32[]{:S(2)}, u32[]{:S(2)}) collective-permute-start(bf16[8,512]{1,0:T(8,128)(2,1)S(1)} %slice.47), channel_id=1, source_target_pairs={{0,32},{32,64},{64,96},{96,128},{128,160},{160,192},{192,224},{224... | collective-permute-start | bytes 24584 | tf_op jit(solution)/shard_map/ppermute | solution.py:33
  117.5 13.6 %collective-permute-start.11 = (bf16[144,256]{1,0:T(8,128)(2,1)S(1)}, bf16[144,256]{1,0:T(8,128)(2,1)S(1)}, u32[]{:S(2)}, u32[]{:S(2)}) collective-permute-start(bf16[144,256]{1,0:T(8,128)(2,1)S(1)} %get-tuple-element.36), channel_id=1, source_target_pairs={{224,256},{225,257},{226,258},{227,259},{228,260},{229,261},{230,2... | collective-permute-start | bytes 221192 | tf_op jit(solution)/shard_map/ppermute | solution.py:443
  118.1 12.9 %collective-permute-start.12 = (bf16[144,256]{1,0:T(8,128)(2,1)S(1)}, bf16[144,256]{1,0:T(8,128)(2,1)S(1)}, u32[]{:S(2)}, u32[]{:S(2)}) collective-permute-start(bf16[144,256]{1,0:T(8,128)(2,1)S(1)} %get-tuple-element.36), channel_id=1, source_target_pairs={{224,288},{225,289},{226,290},{227,291},{228,292},{229,293},{230,2... | collective-permute-start | bytes 221192 | tf_op jit(solution)/shard_map/ppermute | solution.py:444
  (8 other events, 27.1 us)
Sparse Core Ops, SparseCore 0:
  9.5 75.8 all-gather.6
  99.5 45.7 all-gather.8

commit v9 on v8

--- a/solution.py
+++ b/solution.py
@@ -84,7 +84,7 @@
 
 
 def first_kernel(layout, scalars, tok_ref, *refs):
-    pieces, other, proj_ref, out = refs[:-3], refs[-3], refs[-2], refs[-1]
+    pieces, (other, proj_ref, far_ref, out, sem) = refs[:-5], refs[-5:]
     z, core = scalars[0], scalars[1]
     count = 0
     for (offset, first, yh_count), piece in zip(layout, pieces):
@@ -100,7 +100,10 @@
             steps = piece[local_yh, 384:392, :].astype(F32).T
             steps = jnp.concatenate([steps, jnp.zeros((256, 120), F32)], axis=1)
             out[pl.ds(start, 256), 512:640] = steps.astype(BF16)
+    copy = pltpu.make_async_copy(out, far_ref, sem)
+    copy.start()
     project(tok_ref, out, proj_ref)
+    copy.wait()
 
 
 def project(tok_ref, w_ref, out_ref):
@@ -285,11 +288,12 @@
         functools.partial(first_kernel, layout),
         (1,),
         [pl.BlockSpec((BLOCK, depth), lambda *_: (last, 0))] + [whole(a.shape) for a in arrays],
-        [pl.BlockSpec((BLOCK, 640), lambda *_: (last, 0)), held(None)],
-        [shape((rows, 640), BF16), shape((depth, 640), BF16)],
+        [pl.BlockSpec((BLOCK, 640), lambda *_: (last, 0)), pl.BlockSpec(memory_space=pltpu.HBM)],
+        [shape((rows, 640), BF16), pltpu.HBM((depth, 640), BF16)],
+        scratch=[pltpu.VMEM((depth, 640), BF16), pltpu.SemaphoreType.DMA],
         prefetch=1,
         cost=work(2 * BLOCK * depth * 640, 12 << 20),
-        room=24,
+        room=32,
     )(scalars, gathered, *arrays)
 
 
@@ -299,13 +303,13 @@
     return call(
         rest_kernel,
         (count,),
-        [rows_of((BLOCK, depth)), held(weights), pl.BlockSpec(memory_space=pl.ANY)],
+        [rows_of((BLOCK, depth)), pl.BlockSpec((depth, 640), lambda *_: (0, 0), pipeline_mode=pl.Buffered(1)), pl.BlockSpec(memory_space=pl.ANY)],
         rows_of((BLOCK, 640)),
         shape((rows, 640), BF16),
         cost=work(2 * count * BLOCK * depth * 640, 8 << 20),
-        room=16,
+        room=24,
         aliases={2: 0},
-    )(gathered, weights, proj)
+    )(gathered, in_hbm(weights), proj)
 
 
 def run_state(starts, base, proj, rim, taps, small):

time: 165 us -> 164 us (level)
  local copies, waits for them, and re-layouts: 13.2 us -> 8.24 us
  Pallas kernels: 30.5 us -> 32.6 us
  blocking collectives: 39.7 us -> 41.6 us
    unnamed x42 -> x38, local copies, waits for them, and re-layouts: 11.7 us -> 6.76 us
    all_gather x1, blocking collectives: 18.8 us -> 20.9 us  [local(): lax.all_gather(run_pair(own, eight, nine), 'zh', axis=0, tiled=False)]
  transfers between devices with their start and end apart: 15 -> 15, of which waited for: 5 -> 5; matrix products, arithmetic and copies ran while one was open for 5% -> 5% of each run, Pallas kernels for 14% -> 15%
where the time goes in v9:
time: 164 us; the launch traced here: 163 us
  starting transfers between devices  52.2 us (32%)
  blocking collectives  41.6 us (25%)
  Pallas kernels  32.6 us (20%)
  between operations  13.7 us (8%)
  waiting for transfers between devices  11.3 us (7%)
  local copies, waits for them, and re-layouts  8.24 us (5%)
  other arithmetic  3.48 us (2%)
    all_gather x1, blocking collectives, local(): lax.all_gather(run_pair(own, eight, nine), 'zh', axis=0, tiled=False)  20.9 us
    ppermute x3, starting transfers between devices, ring_gather(): left = lax.ppermute(left, RING, ring(Z, -1))  18.9 us
    ppermute x1, starting transfers between devices, local(): gate_far = lax.ppermute(gate_own, 'yh', ring(YH, 1))  13.6 us
    all_gather x1, blocking collectives, local(): both = lax.all_gather(pack, 'yh', axis=0, tiled=False)  13.3 us
    ppermute x3, waiting for transfers between devices, ring_gather(): right = lax.ppermute(right, RING, ring(Z, 1))  9.29 us
    pallas_call x1, Pallas kernels, run_rest(): call(rest_kernel, (count,), [rows_of((BLOCK, depth)), pl.BlockSpec((depth...  8.56 us
    ppermute x3, starting transfers between devices, ring_gather(): right = lax.ppermute(right, RING, ring(Z, 1))  8.09 us
    pallas_call x1, Pallas kernels, run_finish(): call(finish_kernel, (rows // TALL,), [held(eight), held(nine), held(own),...  7.39 us
  transfers between devices with their start and end apart: 15, of which 5 were waited for; matrix products, arithmetic and copies ran while one was open for 5% of the time, Pallas kernels for 15%

profile of v9, /device:TPU:6, one launch (start us, length us, event | category | flops | bytes accessed | tf_op | source)
XLA Modules:
  0.0 163.2 jit_solution(16018997638694781608)
XLA Ops:
  8.7 13.3 %all-gather = bf16[784,256]{1,0:T(8,128)(2,1)S(1)} all-gather(bf16[392,256]{1,0:T(8,128)(2,1)S(1)} %fusion.1), channel_id=2, replica_groups=mesh['yh'=2,'zh'=4,'zc'=2,'x'=4,'y'=4,'c'=2] {'yh'}, dimensions={0}, use_global_device_ids=true | all-gather | bytes 602112 | tf_op jit(solution)/shard_map/all_gather | solution.py:428
  22.0 4.3 %collective-permute-start = (bf16[2,392,256]{2,1,0:T(8,128)(2,1)S(1)}, bf16[2,392,256]{2,1,0:T(8,128)(2,1)S(1)}, u32[]{:S(2)}, u32[]{:S(2)}) collective-permute-start(bf16[2,392,256]{2,1,0:T(8,128)(2,1)S(1)} %bitcast.21), channel_id=1, source_target_pairs={{0,32},{32,64},{64,96},{96,128},{128,160},{160,192},{192,224},{224... | collective-permute-start | bytes 1204232 | tf_op jit(solution)/shard_map/ppermute | solution.py:40
  26.3 8.6 %collective-permute-start.1 = (bf16[2,392,256]{2,1,0:T(8,128)(2,1)S(1)}, bf16[2,392,256]{2,1,0:T(8,128)(2,1)S(1)}, u32[]{:S(2)}, u32[]{:S(2)}) collective-permute-start(bf16[2,392,256]{2,1,0:T(8,128)(2,1)S(1)} %bitcast.22), channel_id=1, source_target_pairs={{0,224},{32,0},{64,32},{96,64},{128,96},{160,128},{192,160},{224,1... | collective-permute-start | bytes 1204232 | tf_op jit(solution)/shard_map/ppermute | solution.py:41
  35.5 4.2 %collective-permute-done.refs_1_ = bf16[2,392,256]{2,1,0:T(8,128)(2,1)S(1)} collective-permute-done((bf16[2,392,256]{2,1,0:T(8,128)(2,1)S(1)}, bf16[2,392,256]{2,1,0:T(8,128)(2,1)S(1)}, u32[]{:S(2)}, u32[]{:S(2)}) %collective-permute-start) | collective-permute-done | bytes 401440 | tf_op jit(solution)/shard_map/ppermute | solution.py:40
  39.7 1.9 %collective-permute-start.2 = (bf16[2,392,256]{2,1,0:T(8,128)(2,1)S(1)}, bf16[2,392,256]{2,1,0:T(8,128)(2,1)S(1)}, u32[]{:S(2)}, u32[]{:S(2)}) collective-permute-start(bf16[2,392,256]{2,1,0:T(8,128)(2,1)S(1)} %collective-permute-done.refs_1_), channel_id=1, source_target_pairs={{0,32},{32,64},{64,96},{96,128},{128,160},{160,192},{192,224},{224... | collective-permute-start | bytes 1204232 | tf_op jit(solution)/shard_map/ppermute | solution.py:40
  41.6 5.1 %collective-permute-start.3 = (bf16[2,392,256]{2,1,0:T(8,128)(2,1)S(1)}, bf16[2,392,256]{2,1,0:T(8,128)(2,1)S(1)}, u32[]{:S(2)}, u32[]{:S(2)}) collective-permute-start(bf16[2,392,256]{2,1,0:T(8,128)(2,1)S(1)} %collective-permute-done.1.refs_2_), channel_id=1, source_target_pairs={{0,224},{32,0},{64,32},{96,64},{128,96},{160,128},{192,160},{224,1... | collective-permute-start | bytes 1204232 | tf_op jit(solution)/shard_map/ppermute | solution.py:41
  48.1 2.6 %collective-permute-done.2.refs_3_ = bf16[2,392,256]{2,1,0:T(8,128)(2,1)S(1)} collective-permute-done((bf16[2,392,256]{2,1,0:T(8,128)(2,1)S(1)}, bf16[2,392,256]{2,1,0:T(8,128)(2,1)S(1)}, u32[]{:S(2)}, u32[]{:S(2)}) %collective-permute-start.2) | collective-permute-done | bytes 401440 | tf_op jit(solution)/shard_map/ppermute | solution.py:40
  50.7 1.9 %collective-permute-start.4 = (bf16[2,392,256]{2,1,0:T(8,128)(2,1)S(1)}, bf16[2,392,256]{2,1,0:T(8,128)(2,1)S(1)}, u32[]{:S(2)}, u32[]{:S(2)}) collective-permute-start(bf16[2,392,256]{2,1,0:T(8,128)(2,1)S(1)} %collective-permute-done.2.refs_3_), channel_id=1, source_target_pairs={{0,32},{32,64},{64,96},{96,128},{128,160},{160,192},{192,224},{224... | collective-permute-start | bytes 1204232 | tf_op jit(solution)/shard_map/ppermute | solution.py:40
  52.6 5.1 %collective-permute-start.5 = (bf16[2,392,256]{2,1,0:T(8,128)(2,1)S(1)}, bf16[2,392,256]{2,1,0:T(8,128)(2,1)S(1)}, u32[]{:S(2)}, u32[]{:S(2)}) collective-permute-start(bf16[2,392,256]{2,1,0:T(8,128)(2,1)S(1)} %collective-permute-done.3.refs_4_), channel_id=1, source_target_pairs={{0,224},{32,0},{64,32},{96,64},{128,96},{160,128},{192,160},{224,1... | collective-permute-start | bytes 1204232 | tf_op jit(solution)/shard_map/ppermute | solution.py:41
  59.1 2.5 %collective-permute-done.4.refs_5_ = bf16[2,392,256]{2,1,0:T(8,128)(2,1)S(1)} collective-permute-done((bf16[2,392,256]{2,1,0:T(8,128)(2,1)S(1)}, bf16[2,392,256]{2,1,0:T(8,128)(2,1)S(1)}, u32[]{:S(2)}, u32[]{:S(2)}) %collective-permute-start.4) | collective-permute-done | bytes 401440 | tf_op jit(solution)/shard_map/ppermute | solution.py:40
  61.7 1.9 %collective-permute-start.6 = (bf16[1,392,256]{2,1,0:T(8,128)(2,1)S(1)}, bf16[1,392,256]{2,1,0:T(8,128)(2,1)S(1)}, u32[]{:S(2)}, u32[]{:S(2)}) collective-permute-start(bf16[1,392,256]{2,1,0:T(8,128)(2,1)S(1)} %slice.48), channel_id=1, source_target_pairs={{0,32},{32,64},{64,96},{96,128},{128,160},{160,192},{192,224},{224... | collective-permute-start | bytes 602120 | tf_op jit(solution)/shard_map/ppermute | solution.py:43
  63.6 5.2 %collective-permute-start.7 = (bf16[1,392,256]{2,1,0:T(8,128)(2,1)S(1)}, bf16[1,392,256]{2,1,0:T(8,128)(2,1)S(1)}, u32[]{:S(2)}, u32[]{:S(2)}) collective-permute-start(bf16[1,392,256]{2,1,0:T(8,128)(2,1)S(1)} %slice.49), channel_id=1, source_target_pairs={{0,224},{32,0},{64,32},{96,64},{128,96},{160,128},{192,160},{224,1... | collective-permute-start | bytes 602120 | tf_op jit(solution)/shard_map/ppermute | solution.py:44
  72.8 1.9 %collective-permute-start.8 = (bf16[16,128,256]{2,1,0:T(8,128)(2,1)}, bf16[16,128,256]{2,1,0:T(8,128)(2,1)S(1)}, u32[]{:S(2)}, u32[]{:S(2)}) collective-permute-start(bf16[16,128,256]{2,1,0:T(8,128)(2,1)} %slice_dynamic-update-slice_fusion.7), channel_id=1, source_target_pairs={{0,1},{1,0},{2,3},{3,2},{4,5},{5,4},{6,7},{7,6},{8,9},{9,8},{10,11... | collective-permute-start | bytes 3145736 | tf_op jit(solution)/shard_map/ppermute | solution.py:432
  74.7 13.6 %collective-permute-start.9 = (bf16[256,256]{1,0:T(8,128)(2,1)S(1)}, bf16[256,256]{1,0:T(8,128)(2,1)}, u32[]{:S(2)}, u32[]{:S(2)}) collective-permute-start(bf16[256,256]{1,0:T(8,128)(2,1)S(1)} %copy-done.11), channel_id=1, source_target_pairs={{0,256},{256,0},{1,257},{257,1},{2,258},{258,2},{3,259},{259,3},{4... | collective-permute-start | bytes 393224 | tf_op jit(solution)/shard_map/ppermute | solution.py:433
  88.4 1.0 copy-done.4
  89.4 6.4 %shard_map.100 = (bf16[1024,640]{1,0:T(8,128)(2,1)S(1)}, bf16[4096,640]{1,0:T(8,128)(2,1)}) custom-call(s32[3]{0:T(128)S(1)} %pad_add_fusion.scalars, bf16[1024,4096]{1,0:T(8,128)(2,1)} %all-gather.7.cloned.1.call-done.tok_ref, bf16[2,392,256]{2,1,0:T(8,128)(2,1)} %bitcast.24, bf16[2,392,256]{2,1,0:T(8,128)(2,1)} %copy-done.5, ...), custom_call_target="tpu_custom_call" | custom-call | flops 1342177280 | bytes 12582912 | tf_op jit(solution)/shard_map/pallas_call | solution.py:287
  95.8 1.6 %pad_maximum_fusion = bf16[2,256,256]{2,1,0:T(8,128)(2,1)} fusion(bf16[1,256,256]{2,1,0:T(8,128)(2,1)} %bitcast.14, bf16[1,256,256]{2,1,0:T(8,128)(2,1)S(1)} %bitcast.26), kind=kLoop, calls=%fused_computation.2 | loop fusion | flops 131072 | bytes 524288 | tf_op jit(solution)/shard_map/stack | solution.py:438
  99.1 1.3 collective-permute-start.10
  100.4 8.6 %shard_map.101.proj_ref = bf16[1024,640]{1,0:T(8,128)(2,1)S(1)} custom-call(bf16[1024,4096]{1,0:T(8,128)(2,1)} %all-gather.7.cloned.1.call-done.tok_ref, bf16[4096,640]{1,0:T(8,128)(2,1)} %get-tuple-element.24.w_ref, bf16[1024,640]{1,0:T(8,128)(2,1)S(1)} %get-tuple-element.27._), custom_call_target="tpu_custom_call", output_to_operand_aliasing={{}: (2, {})} | custom-call | flops 4026531840 | bytes 8388608 | tf_op jit(solution)/shard_map/pallas_call | solution.py:303
  109.0 5.6 %shard_map.102 = (bf16[1024,512]{1,0:T(8,128)(2,1)S(1)}, f32[1024,128]{1,0:T(8,128)S(1)}, f32[1024,128]{1,0:T(8,128)S(1)}, f32[4,128,256]{2,1,0:T(8,128)S(1)}, f...) custom-call(s32[16]{0:T(128)S(1)} %sub.7.starts, s32[1]{0:T(128)} %bitcast.4.base, ...), custom_call_target="tpu_custom_call" | custom-call | flops 67108864 | bytes 4194304 | tf_op jit(solution)/shard_map/pallas_call | solution.py:318
  116.0 4.6 %shard_map.103 = (f32[1024,256]{1,0:T(8,128)}, f32[1024,256]{1,0:T(8,128)}) custom-call(s32[16]{0:T(128)S(1)} %sub.7.starts, s32[1]{0:T(128)} %bitcast.4.base, bf16[1024,512]{1,0:T(8,128)(2,1)S(1)} %get-tuple-element.29.act_ref, f32[1024,128]{1,0:T(8,128)S(1)} %get-tuple-element.30.cum_ref, f32[1024,128]{1,0:T(8,128)S(1)} %get-tuple-element.31.step_ref, ...), custom_call_target="tpu_custom_call" | custom-call | flops 536870912 | bytes 5242880 | tf_op jit(solution)/shard_map/pallas_call | solution.py:351
  120.6 7.4 %all-gather.1 = bf16[288,256]{1,0:T(8,128)(2,1)S(1)} all-gather(bf16[144,256]{1,0:T(8,128)(2,1)S(1)} %get-tuple-element.36), channel_id=3, replica_groups=mesh['yh'=2,'zh'=4,'zc'=2,'x'=4,'y'=4,'c'=2] {'zc'}, dimensions={0}, use_global_device_ids=true | all-gather | bytes 221184 | tf_op jit(solution)/shard_map/all_gather | solution.py:451
  128.0 20.9 %all-gather.2 = bf16[576,256]{1,0:T(8,128)(2,1)S(1)} all-gather(bf16[144,256]{1,0:T(8,128)(2,1)S(1)} %shard_map.104), channel_id=4, replica_groups=mesh['yh'=2,'zh'=4,'zc'=2,'x'=4,'y'=4,'c'=2] {'zh'}, dimensions={0}, use_global_device_ids=true | all-gather | bytes 368640 | tf_op jit(solution)/shard_map/all_gather | solution.py:453
  149.0 7.4 %shard_map.105 = bf16[1024,256]{1,0:T(8,128)(2,1)} custom-call(s32[3]{0:T(128)S(1)} %pad_add_fusion.scalars, bf16[144,256]{1,0:T(8,128)(2,1)S(1)} %collective-permute-done.11.eight_ref, bf16[144,256]{1,0:T(8,128)(2,1)S(1)} %collective-permute-done.12.nine_ref, bf16[2,144,256]{2,1,0:T(8,128)(2,1)S(1)} %bitcast.19, bf16[4,144,256]{2,1,0:T(8,128)(2,1)S(1)} %bitcast.20, ...), custom_call_target="tpu_custom_call" | custom-call | flops 2214592512 | bytes 13631488 | tf_op jit(solution)/shard_map/pallas_call | solution.py:382
  (70 shorter events, 12.5 us)
Async XLA Ops:
  6.5 82.9 %all-gather.7.cloned.1.call-start = ((), (), s32[]{:S(2)}) async-start(), calls=%async_computation | async-start | bytes 8650752 | tf_op jit(solution)/shard_map/all_gather | solution.py:422
  7.3 67.5 %copy-start.11 = (bf16[256,256]{1,0:T(8,128)(2,1)S(1)}, bf16[256,256]{1,0:T(8,128)(2,1)}, u32[]{:S(2)}) copy-start(bf16[256,256]{1,0:T(8,128)(2,1)} %param.13) | copy-start | bytes 393220
  7.3 141.7 %all-gather.9.cloned.1.call-start = ((), (), s32[]{:S(2)}) async-start(), calls=%async_computation.1 | async-start | bytes 2359296 | tf_op jit(solution)/shard_map/all_gather | solution.py:438
  22.0 67.4 %copy-start.1 = (bf16[784,256]{1,0:T(8,128)(2,1)}, bf16[784,256]{1,0:T(8,128)(2,1)S(1)}, u32[]{:S(2)}) copy-start(bf16[784,256]{1,0:T(8,128)(2,1)S(1)} %all-gather) | copy-start | bytes 1204228
  22.0 17.7 %collective-permute-start = (bf16[2,392,256]{2,1,0:T(8,128)(2,1)S(1)}, bf16[2,392,256]{2,1,0:T(8,128)(2,1)S(1)}, u32[]{:S(2)}, u32[]{:S(2)}) collective-permute-start(bf16[2,392,256]{2,1,0:T(8,128)(2,1)S(1)} %bitcast.21), channel_id=1, source_target_pairs={{0,32},{32,64},{64,96},{96,128},{128,160},{160,192},{192,224},{224... | collective-permute-start | bytes 1204232 | tf_op jit(solution)/shard_map/ppermute | solution.py:40
  26.3 15.4 %collective-permute-start.1 = (bf16[2,392,256]{2,1,0:T(8,128)(2,1)S(1)}, bf16[2,392,256]{2,1,0:T(8,128)(2,1)S(1)}, u32[]{:S(2)}, u32[]{:S(2)}) collective-permute-start(bf16[2,392,256]{2,1,0:T(8,128)(2,1)S(1)} %bitcast.22), channel_id=1, source_target_pairs={{0,224},{32,0},{64,32},{96,64},{128,96},{160,128},{192,160},{224,1... | collective-permute-start | bytes 1204232 | tf_op jit(solution)/shard_map/ppermute | solution.py:41
  39.7 12.9 %copy-start.5 = (bf16[2,392,256]{2,1,0:T(8,128)(2,1)}, bf16[2,392,256]{2,1,0:T(8,128)(2,1)S(1)}, u32[]{:S(2)}) copy-start(bf16[2,392,256]{2,1,0:T(8,128)(2,1)S(1)} %collective-permute-done.refs_1_) | copy-start | bytes 1204228
  39.7 11.0 %collective-permute-start.2 = (bf16[2,392,256]{2,1,0:T(8,128)(2,1)S(1)}, bf16[2,392,256]{2,1,0:T(8,128)(2,1)S(1)}, u32[]{:S(2)}, u32[]{:S(2)}) collective-permute-start(bf16[2,392,256]{2,1,0:T(8,128)(2,1)S(1)} %collective-permute-done.refs_1_), channel_id=1, source_target_pairs={{0,32},{32,64},{64,96},{96,128},{128,160},{160,192},{192,224},{224... | collective-permute-start | bytes 1204232 | tf_op jit(solution)/shard_map/ppermute | solution.py:40
  41.6 30.4 %copy-start.6 = (bf16[2,392,256]{2,1,0:T(8,128)(2,1)}, bf16[2,392,256]{2,1,0:T(8,128)(2,1)S(1)}, u32[]{:S(2)}) copy-start(bf16[2,392,256]{2,1,0:T(8,128)(2,1)S(1)} %collective-permute-done.1.refs_2_) | copy-start | bytes 1204228
  41.6 11.0 %collective-permute-start.3 = (bf16[2,392,256]{2,1,0:T(8,128)(2,1)S(1)}, bf16[2,392,256]{2,1,0:T(8,128)(2,1)S(1)}, u32[]{:S(2)}, u32[]{:S(2)}) collective-permute-start(bf16[2,392,256]{2,1,0:T(8,128)(2,1)S(1)} %collective-permute-done.1.refs_2_), channel_id=1, source_target_pairs={{0,224},{32,0},{64,32},{96,64},{128,96},{160,128},{192,160},{224,1... | collective-permute-start | bytes 1204232 | tf_op jit(solution)/shard_map/ppermute | solution.py:41
  50.7 22.1 %copy-start.7 = (bf16[2,392,256]{2,1,0:T(8,128)(2,1)}, bf16[2,392,256]{2,1,0:T(8,128)(2,1)S(1)}, u32[]{:S(2)}) copy-start(bf16[2,392,256]{2,1,0:T(8,128)(2,1)S(1)} %collective-permute-done.2.refs_3_) | copy-start | bytes 1204228
  50.7 11.0 %collective-permute-start.4 = (bf16[2,392,256]{2,1,0:T(8,128)(2,1)S(1)}, bf16[2,392,256]{2,1,0:T(8,128)(2,1)S(1)}, u32[]{:S(2)}, u32[]{:S(2)}) collective-permute-start(bf16[2,392,256]{2,1,0:T(8,128)(2,1)S(1)} %collective-permute-done.2.refs_3_), channel_id=1, source_target_pairs={{0,32},{32,64},{64,96},{96,128},{128,160},{160,192},{192,224},{224... | collective-permute-start | bytes 1204232 | tf_op jit(solution)/shard_map/ppermute | solution.py:40
  52.6 20.1 %copy-start.8 = (bf16[2,392,256]{2,1,0:T(8,128)(2,1)}, bf16[2,392,256]{2,1,0:T(8,128)(2,1)S(1)}, u32[]{:S(2)}) copy-start(bf16[2,392,256]{2,1,0:T(8,128)(2,1)S(1)} %collective-permute-done.3.refs_4_) | copy-start | bytes 1204228
  52.6 11.0 %collective-permute-start.5 = (bf16[2,392,256]{2,1,0:T(8,128)(2,1)S(1)}, bf16[2,392,256]{2,1,0:T(8,128)(2,1)S(1)}, u32[]{:S(2)}, u32[]{:S(2)}) collective-permute-start(bf16[2,392,256]{2,1,0:T(8,128)(2,1)S(1)} %collective-permute-done.3.refs_4_), channel_id=1, source_target_pairs={{0,224},{32,0},{64,32},{96,64},{128,96},{160,128},{192,160},{224,1... | collective-permute-start | bytes 1204232 | tf_op jit(solution)/shard_map/ppermute | solution.py:41
  61.6 27.8 %copy-start.2 = (bf16[2,392,256]{2,1,0:T(8,128)(2,1)}, bf16[2,392,256]{2,1,0:T(8,128)(2,1)S(1)}, u32[]{:S(2)}) copy-start(bf16[2,392,256]{2,1,0:T(8,128)(2,1)S(1)} %collective-permute-done.4.refs_5_) | copy-start | bytes 1204228
  61.7 8.8 %collective-permute-start.6 = (bf16[1,392,256]{2,1,0:T(8,128)(2,1)S(1)}, bf16[1,392,256]{2,1,0:T(8,128)(2,1)S(1)}, u32[]{:S(2)}, u32[]{:S(2)}) collective-permute-start(bf16[1,392,256]{2,1,0:T(8,128)(2,1)S(1)} %slice.48), channel_id=1, source_target_pairs={{0,32},{32,64},{64,96},{96,128},{128,160},{160,192},{192,224},{224... | collective-permute-start | bytes 602120 | tf_op jit(solution)/shard_map/ppermute | solution.py:43
  63.6 8.4 %collective-permute-start.7 = (bf16[1,392,256]{2,1,0:T(8,128)(2,1)S(1)}, bf16[1,392,256]{2,1,0:T(8,128)(2,1)S(1)}, u32[]{:S(2)}, u32[]{:S(2)}) collective-permute-start(bf16[1,392,256]{2,1,0:T(8,128)(2,1)S(1)} %slice.49), channel_id=1, source_target_pairs={{0,224},{32,0},{64,32},{96,64},{128,96},{160,128},{192,160},{224,1... | collective-permute-start | bytes 602120 | tf_op jit(solution)/shard_map/ppermute | solution.py:44
  72.8 15.6 %collective-permute-start.8 = (bf16[16,128,256]{2,1,0:T(8,128)(2,1)}, bf16[16,128,256]{2,1,0:T(8,128)(2,1)S(1)}, u32[]{:S(2)}, u32[]{:S(2)}) collective-permute-start(bf16[16,128,256]{2,1,0:T(8,128)(2,1)} %slice_dynamic-update-slice_fusion.7), channel_id=1, source_target_pairs={{0,1},{1,0},{2,3},{3,2},{4,5},{5,4},{6,7},{7,6},{8,9},{9,8},{10,11... | collective-permute-start | bytes 3145736 | tf_op jit(solution)/shard_map/ppermute | solution.py:432
  74.7 21.1 %collective-permute-start.9 = (bf16[256,256]{1,0:T(8,128)(2,1)S(1)}, bf16[256,256]{1,0:T(8,128)(2,1)}, u32[]{:S(2)}, u32[]{:S(2)}) collective-permute-start(bf16[256,256]{1,0:T(8,128)(2,1)S(1)} %copy-done.11), channel_id=1, source_target_pairs={{0,256},{256,0},{1,257},{257,1},{2,258},{258,2},{3,259},{259,3},{4... | collective-permute-start | bytes 393224 | tf_op jit(solution)/shard_map/ppermute | solution.py:433
  88.4 10.0 %copy-start.14 = (f32[4]{0:T(128)S(1)}, f32[4]{0:T(128)}, u32[]{:S(2)}) copy-start(f32[4]{0:T(128)} %param.19) | copy-start | bytes 52
  88.4 10.7 %copy-start.12 = (f32[4,256]{1,0:T(4,128)S(1)}, f32[4,256]{1,0:T(4,128)}, u32[]{:S(2)}) copy-start(f32[4,256]{1,0:T(4,128)} %param.16) | copy-start | bytes 12292
  99.1 9.9 %collective-permute-start.10 = (bf16[8,512]{1,0:T(8,128)(2,1)S(1)}, bf16[8,512]{1,0:T(8,128)(2,1)S(1)}, u32[]{:S(2)}, u32[]{:S(2)}) collective-permute-start(bf16[8,512]{1,0:T(8,128)(2,1)S(1)} %slice.47), channel_id=1, source_target_pairs={{0,32},{32,64},{64,96},{96,128},{128,160},{160,192},{192,224},{224... | collective-permute-start | bytes 24584 | tf_op jit(solution)/shard_map/ppermute | solution.py:33
  114.6 13.3 %collective-permute-start.11 = (bf16[144,256]{1,0:T(8,128)(2,1)S(1)}, bf16[144,256]{1,0:T(8,128)(2,1)S(1)}, u32[]{:S(2)}, u32[]{:S(2)}) collective-permute-start(bf16[144,256]{1,0:T(8,128)(2,1)S(1)} %get-tuple-element.36), channel_id=1, source_target_pairs={{224,256},{225,257},{226,258},{227,259},{228,260},{229,261},{230,2... | collective-permute-start | bytes 221192 | tf_op jit(solution)/shard_map/ppermute | solution.py:447
  115.3 12.7 %collective-permute-start.12 = (bf16[144,256]{1,0:T(8,128)(2,1)S(1)}, bf16[144,256]{1,0:T(8,128)(2,1)S(1)}, u32[]{:S(2)}, u32[]{:S(2)}) collective-permute-start(bf16[144,256]{1,0:T(8,128)(2,1)S(1)} %get-tuple-element.36), channel_id=1, source_target_pairs={{224,288},{225,289},{226,290},{227,291},{228,292},{229,293},{230,2... | collective-permute-start | bytes 221192 | tf_op jit(solution)/shard_map/ppermute | solution.py:448
  (6 other events, 20.2 us)
Sparse Core Ops, SparseCore 0:
  9.5 75.8 all-gather.6
  97.6 45.4 all-gather.8
